TPU v7x, 256 devices: a whole 4x4x8 slice. The times are simulated.
256 devices in a mesh: dp: 16 (over y, x_lo, core), vocab: 16 (over x_hi, z).
Axes of the slice: x: 4 (x_hi: 2, x_lo: 2; x = x_hi * 2 + x_lo), y: 4, z: 8, core: 2. Of those that a mesh axis runs over, the one named last changes fastest.
Arguments:
- hidden: bfloat16 [2048, 12288], P('dp'), may hold values from -8 to 8
- head_weight: bfloat16 [12288, 32768], P('dp', 'vocab'), may hold values from -0.16237976 to 0.16237976
- targets: int32 [2048], replicated, may hold values from 0 to 32767
Outputs:
- loss: float32 [2048], P('dp')
- grad_weight: float32 [12288, 32768], P('dp', 'vocab')
All inputs are finite; a program needn't handle non-finite values.
Results may differ from a plain program's by a relative error of at most 0.0014.
Values may be sent and summed in bfloat16 or wider, within the bound.
No kernel may reach another device: no remote copies, remote signals or barrier semaphores. Data moves between devices by JAX's collectives and lax.ppermute only.
A program may use at most 128 MiB of HBM per device.

v0:
```python
import jax
import jax.numpy as jnp
from jax import lax
from jax.sharding import PartitionSpec as P


def from_everyone(shard, axis):
    length = lax.axis_size(axis)
    return lax.all_to_all(
        jnp.broadcast_to(shard[None], (length, *shard.shape)), axis, 0, 0, tiled=True
    )


def taken_together(shard, axis):
    everything = from_everyone(shard, axis)
    return jnp.max(everything, axis=0)


def over_copies(shard, axis):
    return from_everyone(shard, axis).sum(axis=0)


def packed_total(arrays, axis):
    line, at, gathered = (jnp.concatenate([a.reshape(-1) for a in arrays]), 0, [])
    running = over_copies(line, axis)
    for a in arrays:
        gathered.append(running[at : at + a.size].reshape(a.shape))
        at += a.size
    return tuple(gathered)


def local_stats(logits, onehot):
    peak = jnp.max(logits, axis=1)
    picked = jnp.sum(jnp.where(onehot, logits, 0.0), axis=1)
    return (peak, picked)


def per_device(hidden, head_weight, targets):
    here = lax.axis_index("dp")
    block_index = lax.axis_index("vocab")
    rows = hidden.shape[0]
    width = head_weight.shape[1]
    spread = lax.all_to_all(hidden, "dp", split_axis=1, concat_axis=0, tiled=True)
    partial_all = jnp.dot(spread, head_weight, preferred_element_type=jnp.float32)
    logits = lax.psum_scatter(partial_all, "dp", scatter_dimension=0, tiled=True)
    labels = lax.dynamic_slice_in_dim(targets, here * rows, rows, 0)
    columns = block_index * width + jnp.arange(width, dtype=jnp.int32)
    onehot = labels[:, None] == columns[None, :]
    peak, picked = local_stats(logits, onehot)
    peak = taken_together(peak, "vocab")
    local_total = jnp.sum(jnp.exp(logits - peak[:, None]), axis=1)
    total, picked = packed_total((local_total, picked), "vocab")
    logsum = peak + jnp.log(total)
    loss = logsum - picked
    slope = (jnp.exp(logits - logsum[:, None]) - onehot.astype(jnp.float32)).astype(jnp.bfloat16)
    grad_weight = lax.dot_general(
        spread,
        lax.all_gather(slope, "dp", axis=0, tiled=True),
        (((0,), (0,)), ((), ())),
        preferred_element_type=jnp.float32,
    )
    return (loss, grad_weight)


def solution(mesh):
    in_specs = (P("dp", None), P("dp", "vocab"), P())
    out_specs = (P("dp"), P("dp", "vocab"))
    return jax.shard_map(
        per_device, mesh=mesh, in_specs=in_specs, out_specs=out_specs, check_vma=False
    )
```

profile of v0, /device:TPU:1, one launch (start us, length us, event | category | flops | bytes accessed | tf_op | source)
XLA Modules:
  0.0 369.7 jit_solution(5291085972359059769)
XLA Ops:
  7.2 0.0 copy-start
  7.2 0.0 reduce-scatter.2.cloned.1.call-start
  7.2 4.8 %copy.13 = bf16[128,12288]{0,1:T(8,128)(2,1)} copy(bf16[128,12288]{1,0:T(8,128)(2,1)} %param.3) | data formatting | bytes 6291456 | tf_op args[0]
  12.0 45.3 %all_to_all.31 = bf16[128,16,768]{0,2,1:T(8,128)(2,1)} all-to-all(bf16[128,16,768]{0,2,1:T(8,128)(2,1)} %bitcast.11), channel_id=1, replica_groups=mesh['dp'=16,'vocab'=16] {'dp'}, dimensions={1} | all-to-all | bytes 6291456 | tf_op jit(solution)/shard_map/all_to_all | solution.py:43
  57.4 4.6 %copy.14 = bf16[16,128,768]{2,1,0:T(8,128)(2,1)} copy(bf16[16,128,768]{1,2,0:T(8,128)(2,1)} %bitcast.10) | data formatting | bytes 6291456 | tf_op jit(solution)/shard_map/all_to_all | solution.py:43
  62.0 0.0 copy-done
  62.0 12.0 %fusion.3 = f32[2048,2048]{1,0:T(8,128)} fusion(bf16[2048,768]{1,0:T(8,128)(2,1)} %bitcast.12, bf16[768,2048]{1,0:T(8,128)(2,1)S(1)} %copy-done), kind=kOutput, calls=%fused_computation.11 | convolution fusion | flops 6442450944 | bytes 23068672 | tf_op jit(solution)/shard_map/dot_general | solution.py:44
  74.0 0.0 reduce-scatter.2.cloned.1.call-update
  74.0 183.7 %reduce-scatter.2.cloned.1.call-done = f32[128,2048]{1,0:T(8,128)} async-done(((f32[2048,2048]{1,0:T(8,128)}), f32[128,2048]{1,0:T(8,128)}) %reduce-scatter.2.cloned.1.call-update) | async-done | bytes 1048592 | tf_op jit(solution)/shard_map/reduce_scatter | solution.py:45
  257.7 1.4 reduce_max.18
  259.1 0.6 broadcast_in_dim.8
  259.7 9.0 %all-to-all-start.1 = ((f32[16,1,128]{2,1,0:T(1,128)}), f32[16,1,128]{2,1,0:T(1,128)S(1)}, u32[]{:S(2)}, u32[]{:S(2)}) async-start(f32[16,1,128]{2,1,0:T(1,128)} %broadcast_in_dim.8), calls=%async_computation.2 | async-start | bytes 16384 | tf_op jit(solution)/shard_map/all_to_all | solution.py:9
  268.6 0.0 all-gather.2.cloned.1.call-start
  268.7 0.8 dynamic_slice.3
  269.5 8.0 %all-to-all-done.1 = f32[16,1,128]{2,1,0:T(1,128)S(1)} async-done(((f32[16,1,128]{2,1,0:T(1,128)}), f32[16,1,128]{2,1,0:T(1,128)S(1)}, u32[]{:S(2)}, u32[]{:S(2)}) %all-to-all-start.1) | async-done | bytes 8224 | tf_op jit(solution)/shard_map/all_to_all | solution.py:9
  277.5 1.6 exponential_reduce_fusion
  279.1 11.4 %all_to_all.32 = f32[16,1,256]{2,1,0:T(1,128)S(1)} all-to-all(f32[16,1,256]{2,1,0:T(1,128)S(1)} %broadcast_in_dim.10), channel_id=1, replica_groups=mesh['dp'=16,'vocab'=16] {'vocab'}, dimensions={0} | all-to-all | bytes 32768 | tf_op jit(solution)/shard_map/all_to_all | solution.py:9
  290.6 0.5 slice_subtract_fusion
  291.1 2.4 fusion.2
  293.5 0.0 all-gather.2.cloned.1.call-update
  293.5 50.8 %all-gather.2.cloned.1.call-done = bf16[2048,2048]{1,0:T(8,128)(2,1)} async-done(((bf16[128,2048]{1,0:T(8,128)(2,1)}), bf16[2048,2048]{1,0:T(8,128)(2,1)}) %all-gather.2.cloned.1.call-update) | async-done | bytes 8388624 | tf_op jit(solution)/shard_map/all_gather | solution.py:58
  344.4 11.9 %convolution_bitcast_fusion = f32[768,2048]{0,1:T(8,128)} fusion(bf16[2048,2048]{1,0:T(8,128)(2,1)} %all-gather.2.cloned.1.call-done, bf16[2048,768]{1,0:T(8,128)(2,1)} %bitcast.13), kind=kOutput, calls=%fused_computation | convolution fusion | flops 6442450944 | bytes 17825792 | tf_op jit(solution)/shard_map/dot_general | solution.py:56
  356.3 6.6 %copy.17 = f32[768,2048]{1,0:T(8,128)} copy(f32[768,2048]{0,1:T(8,128)} %convolution_bitcast_fusion) | data formatting | bytes 12582912
  (5 shorter events, 0.1 us)
Async XLA Ops:
  7.2 54.8 %copy-start = (bf16[768,2048]{1,0:T(8,128)(2,1)S(1)}, bf16[768,2048]{1,0:T(8,128)(2,1)}, u32[]{:S(2)}) copy-start(bf16[768,2048]{1,0:T(8,128)(2,1)} %param.4) | copy-start | bytes 9437188
  7.2 250.5 %reduce-scatter.2.cloned.1.call-start = ((), (), s32[]{:S(2)}) async-start(), calls=%async_computation.4 | async-start | bytes 17825792 | tf_op jit(solution)/shard_map/reduce_scatter | solution.py:45
  259.7 17.8 %all-to-all-start.1 = ((f32[16,1,128]{2,1,0:T(1,128)}), f32[16,1,128]{2,1,0:T(1,128)S(1)}, u32[]{:S(2)}, u32[]{:S(2)}) async-start(f32[16,1,128]{2,1,0:T(1,128)} %broadcast_in_dim.8), calls=%async_computation.2 | async-start | bytes 16384 | tf_op jit(solution)/shard_map/all_to_all | solution.py:9
  268.6 75.7 %all-gather.2.cloned.1.call-start = ((), (), s32[]{:S(2)}) async-start(), calls=%async_computation.5 | async-start | bytes 8912896 | tf_op jit(solution)/shard_map/all_gather | solution.py:58
Sparse Core Ops, SparseCore 0:
  74.1 183.5 reduce-scatter.1
  293.7 50.6 all-gather.1
where the time goes:
time: 370 us
  waiting for transfers between devices  243 us (66%)
  blocking collectives  56.7 us (15%)
  matrix products  23.9 us (6%)
  local copies, waits for them, and re-layouts  17.4 us (5%)
  between operations  14.1 us (4%)
  starting transfers between devices  9.04 us (2%)
  other arithmetic  5.98 us (2%)
    reduce_scatter x1, waiting for transfers between devices, per_device(): lax.psum_scatter(partial_all, 'dp', scatter_dimension=0, tiled=True)  184 us
    all_gather x1, waiting for transfers between devices, per_device(): lax.all_gather(slope, 'dp', axis=0, tiled=True)  50.8 us
    all_to_all x1, blocking collectives, per_device(): lax.all_to_all(hidden, 'dp', split_axis=1, concat_axis=0, tiled=True)  45.3 us
    dot_general x1, matrix products, per_device(): jnp.dot(spread, head_weight, preferred_element_type=jnp.float32)  12 us
    dot_general x1, matrix products, per_device(): lax.dot_general(spread, lax.all_gather(slope, 'dp', axis=0, tiled=True),...  11.9 us
    all_to_all x1, blocking collectives, from_everyone(): lax.all_to_all(jnp.broadcast_to(shard[None], (length, *shard.shape)), axi...  11.4 us
    unnamed x4, local copies, waits for them, and re-layouts  11.4 us
    all_to_all x1, starting transfers between devices, from_everyone(): lax.all_to_all(jnp.broadcast_to(shard[None], (length, *shard.shape)), axi...  8.96 us
  transfers between devices with their start and end apart: 3, of which 3 were waited for; matrix products, arithmetic and copies ran while one was open for 0% of the time, Pallas kernels for 0%

commit v1 on v0

v1 whole, which is shorter than its diff:
```python
import jax
import jax.numpy as jnp
from jax import lax
from jax.experimental import pallas as pl
from jax.experimental.pallas import tpu as pltpu
from jax.sharding import PartitionSpec as P


AXES = ("dp", "vocab")
Y, X, C, H, Z = 4, 2, 2, 2, 8
LANES = 128
ROWS_SUM = 48
ROWS_OUT = 80
F32, BF16 = jnp.float32, jnp.bfloat16


def device(y, x, c, h, z):
    return ((((y % Y) * X + x) * C + c) * H + h) * Z + z % Z


def fetch(value, source):
    pairs = [
        (device(*source(y, x, c, h, z)), device(y, x, c, h, z))
        for y in range(Y)
        for x in range(X)
        for c in range(C)
        for h in range(H)
        for z in range(Z)
    ]
    return lax.ppermute(value, AXES, pairs)


def from_y(value, dy):
    return fetch(value, lambda y, x, c, h, z: (y + dy, x, c, h, z))


def from_x(value):
    return fetch(value, lambda y, x, c, h, z: (y, x ^ 1, c, h, z))


def from_z(value, dz):
    return fetch(value, lambda y, x, c, h, z: (y, x, c, h, z + dz))


def from_core(value):
    return fetch(value, lambda y, x, c, h, z: (y, x, c ^ 1, h, z))


def side(dy, z):
    return (z + 1) % 2 if dy == 3 else z % 2


def encode(values):
    peak = jnp.max(jnp.abs(values), axis=-1, keepdims=True)
    power = jnp.ceil(jnp.log2(jnp.maximum(peak, 1e-30) * (1.0 / 32000.0)))
    codes = jnp.round(values * jnp.exp2(-power)).astype(jnp.int32).astype(jnp.int16)
    tail = jnp.broadcast_to(power, (values.shape[0], LANES)).astype(jnp.int32)
    return codes, tail.astype(jnp.int16)


def put(ref, index, values):
    width = values.shape[-1]
    codes, tail = encode(values)
    ref[(*index, slice(0, width))] = codes
    ref[(*index, slice(width, width + LANES))] = tail


def get(ref, index):
    width = ref.shape[-1] - LANES
    power = ref[(*index, slice(width, width + LANES))].astype(jnp.int32).astype(F32)
    codes = ref[(*index, slice(0, width))].astype(jnp.int32).astype(F32)
    return codes * jnp.exp2(power[:, :1])


def rows_of(refs, flag, dy, dx):
    near, far = refs[dy]
    far = jnp.concatenate([f[...] for f in far], axis=0)
    direct = flag == (dx if dy != 3 else 1 - dx)
    return jnp.where(direct, near[...], far)


def full(shape):
    return pl.BlockSpec(shape, lambda j: (0,) * len(shape))


STEPS = 4


def products(flag, near, far, extra, weights, sends):
    w0, w1 = weights
    depth, width = w0.shape
    block = width // STEPS
    a = ROWS_SUM
    rows = near[1].shape[0]
    b = rows - a
    groups = 3 if sends else 5
    flat = [near[1], near[2], near[3], *far[1], *far[2], *far[3], *extra]

    def body(flag_ref, *refs):
        refs = list(refs)
        n1, n2, n3, f1, f2a, f2b, f3 = refs[:7]
        rest = refs[7 : 7 + len(extra)]
        w0_ref, w1_ref = refs[7 + len(extra) : 9 + len(extra)]
        outs = refs[9 + len(extra) :]
        left, acc = outs[-2:]
        j = pl.program_id(0)
        by = {1: (n1, [f1]), 2: (n2, [f2a, f2b]), 3: (n3, [f3])}

        @pl.when(j == 0)
        def _():
            for k, dy in enumerate((1, 2, 3)):
                left[k * rows : (k + 1) * rows] = rows_of(by, flag_ref[0], dy, 1 if sends else 0)
            for k, ref in enumerate(rest):
                left[(3 + k) * rows : (4 + k) * rows] = ref[...]

        value = jnp.dot(left[:, :depth], w0_ref[...], preferred_element_type=F32)
        value += jnp.dot(left[:, depth:], w1_ref[...], preferred_element_type=F32)
        if not sends:
            outs[0][...] = value
            outs[1][...] = jnp.zeros((8, LANES), jnp.int32)
            return
        acc[j] = value

        @pl.when(j == STEPS - 1)
        def _():
            xs, ys = outs[0], outs[1:4]
            for k in range(3):
                whole = jnp.concatenate(
                    [acc[s, k * rows : (k + 1) * rows] for s in range(STEPS)], axis=1
                )
                put(xs, (k, slice(None)), whole[:a])
                put(ys[k], (slice(None),), whole[a:])

    if sends:
        shapes = [(3, a, width + LANES)] + [(b, width + LANES)] * 3
        out_shape = [jax.ShapeDtypeStruct(s, jnp.int16) for s in shapes]
        out_specs = [full(s) for s in shapes]
        acc_shape = (STEPS, groups * rows, block)
    else:
        out_shape = [
            jax.ShapeDtypeStruct((groups * rows, width), F32),
            jax.ShapeDtypeStruct((8, LANES), jnp.int32),
        ]
        out_specs = [
            pl.BlockSpec((groups * rows, block), lambda j: (0, j)),
            full((8, LANES)),
        ]
        acc_shape = (1, 8, LANES)
    return pl.pallas_call(
        body,
        grid=(STEPS,),
        in_specs=[pl.BlockSpec(memory_space=pltpu.SMEM)]
        + [full(v.shape) for v in flat]
        + [pl.BlockSpec((depth, block), lambda j: (0, j))] * 2,
        out_specs=out_specs,
        out_shape=out_shape,
        scratch_shapes=[
            pltpu.VMEM((groups * rows, 2 * depth), BF16),
            pltpu.VMEM(acc_shape, F32),
        ],
        name="sends" if sends else "keeps",
    )(flag, *flat, w0, w1)


def combine_y(kept, received, rows, width):
    a = ROWS_SUM

    def body(kept_ref, got, o1, o2, o3):
        k = pl.program_id(0)
        first = kept_ref[:a] + get(got, (0, slice(None)))
        for i, out in enumerate((o1, o2, o3)):

            @pl.when(k == i)
            def _(out=out):
                put(out, (slice(0, a),), first)
                put(out, (slice(a, rows),), kept_ref[a:])

    shape = (rows, width + LANES)
    return pl.pallas_call(
        body,
        grid=(3,),
        in_specs=[
            pl.BlockSpec((rows, width), lambda k: (k, 0)),
            pl.BlockSpec((1, a, width + LANES), lambda k: (k, 0, 0)),
        ],
        out_specs=[full(shape)] * 3,
        out_shape=[jax.ShapeDtypeStruct(shape, jnp.int16)] * 3,
        name="combine_y",
    )(kept, received)


def combine_x(kept, received, rows, width):
    a = ROWS_SUM

    def body(kept_ref, g1, g2, g3, out):
        last = kept_ref[a:] + get(g1, (slice(None),)) + get(g2, (slice(None),)) + get(g3, (slice(None),))
        put(out, (slice(0, a),), kept_ref[:a])
        put(out, (slice(a, rows),), last)

    shape = (rows, width + LANES)
    return pl.pallas_call(
        body,
        grid=(1,),
        in_specs=[pl.BlockSpec((rows, width), lambda k: (3, 0))]
        + [full(received[0].shape)] * 3,
        out_specs=full(shape),
        out_shape=jax.ShapeDtypeStruct(shape, jnp.int16),
        name="combine_x",
    )(kept, *received)


def finish(kept, received, labels, first_column, rows, width):
    def body(first_ref, kept_ref, g1, g2, g3, g4, label_ref, e_ref, stat_ref):
        logits = kept_ref[...]
        for g in (g1, g2, g3, g4):
            logits = logits + get(g, (slice(None),))
        columns = lax.broadcasted_iota(jnp.int32, (rows, width), 1) + first_ref[0]
        hit = columns == label_ref[:, :1]
        peak = jnp.max(logits, axis=1, keepdims=True)
        raised = jnp.exp(logits - peak)
        total = jnp.sum(raised, axis=1, keepdims=True)
        picked = jnp.sum(jnp.where(hit, logits, 0.0), axis=1, keepdims=True)
        e_ref[...] = raised.astype(BF16)
        lane = lax.broadcasted_iota(jnp.int32, (rows, LANES), 1)
        stat_ref[...] = jnp.where(lane == 0, peak, jnp.where(lane == 1, total, picked))

    return pl.pallas_call(
        body,
        grid=(1,),
        in_specs=[
            pl.BlockSpec(memory_space=pltpu.SMEM),
            pl.BlockSpec((rows, width), lambda k: (4, 0)),
        ]
        + [full(received[0].shape)] * 4
        + [full((rows, LANES))],
        out_specs=[full((rows, width)), full((rows, LANES))],
        out_shape=[
            jax.ShapeDtypeStruct((rows, width), BF16),
            jax.ShapeDtypeStruct((rows, LANES), F32),
        ],
        name="finish",
    )(first_column, kept, *received, labels)


def slopes(pieces, scale, label, first_column, width):
    sizes = [p.shape[0] for p in pieces]
    total = sum(sizes)

    def body(first_ref, *refs):
        ins, scale_ref, label_ref, out = refs[:-3], refs[-3], refs[-2], refs[-1]
        columns = lax.broadcasted_iota(jnp.int32, (sizes[0], width), 1) + first_ref[0]
        at = 0
        for ref, n in zip(ins, sizes):
            hit = columns[:n] == label_ref[at : at + n, :1]
            value = ref[...].astype(F32) * scale_ref[at : at + n, :1]
            out[at : at + n] = (value - jnp.where(hit, 1.0, 0.0)).astype(BF16)
            at += n

    return pl.pallas_call(
        body,
        grid=(1,),
        in_specs=[pl.BlockSpec(memory_space=pltpu.SMEM)]
        + [full(p.shape) for p in pieces]
        + [full((total, LANES))] * 2,
        out_specs=full((total, width)),
        out_shape=jax.ShapeDtypeStruct((total, width), BF16),
    )(first_column, *pieces, scale, label)


def pieces_of(hidden, starts, depth):
    count = len(starts) // 2
    rows = hidden.shape[0]

    def body(at_ref, source, *refs):
        outs, sems = refs[:count], refs[count]
        copies = []
        for k in range(2 * count):
            at = pl.multiple_of(at_ref[k] * depth, LANES)
            copies.append(
                pltpu.make_async_copy(
                    source.at[:, pl.ds(at, depth)],
                    outs[k // 2].at[:, pl.ds((k % 2) * depth, depth)],
                    sems.at[k],
                )
            )
        for copy in copies:
            copy.start()
        for copy in copies:
            copy.wait()

    return pl.pallas_call(
        body,
        in_specs=[pl.BlockSpec(memory_space=pltpu.SMEM), pl.BlockSpec(memory_space=pl.ANY)],
        out_specs=[pl.BlockSpec(memory_space=pl.ANY)] * count,
        out_shape=[jax.ShapeDtypeStruct((rows, 2 * depth), BF16)] * count,
        scratch_shapes=[pltpu.SemaphoreType.DMA((2 * count,))],
        name="pieces",
    )(jnp.stack(starts).astype(jnp.int32), hidden)


def gradient(turned, slope, other, before):
    depth, double = turned.shape
    n, width = slope.shape
    block = width // STEPS

    def body(turned_ref, s_ref, o_ref, *refs):
        value = jnp.dot(turned_ref[:, :n], s_ref[...], preferred_element_type=F32)
        value += jnp.dot(turned_ref[:, n:], o_ref[...], preferred_element_type=F32)
        refs[-1][...] = value + refs[0][...] if len(refs) == 2 else value

    col = lambda r: pl.BlockSpec((r, block), lambda j: (0, j))
    extra = () if before is None else (before,)
    return pl.pallas_call(
        body,
        grid=(STEPS,),
        in_specs=[full((depth, double)), col(n), col(n)] + [col(depth)] * len(extra),
        out_specs=col(depth),
        out_shape=jax.ShapeDtypeStruct((depth, width), F32),
    )(turned, slope, other, *extra)


def per_device(hidden, head_weight, targets):
    here = lax.axis_index("dp")
    block_index = lax.axis_index("vocab")
    c = here % C
    x = (here // C) % X
    y = here // (C * X)
    odd = block_index % 2
    rows = hidden.shape[0]
    depth, width = head_weight.shape

    partner_weight = from_core(head_weight)

    def columns_for(dy, dx):
        chip = ((y - dy) % Y) * X + (x ^ dx)
        return [chip * C + c, chip * C + 1 - c]

    wanted = [columns_for(1, odd), columns_for(3, 1 - odd), columns_for(2, odd)]
    wanted += [columns_for(0, 1), columns_for(0, 0)]
    p1, p3, p2, p0, own = pieces_of(hidden, [v for w in wanted for v in w], depth)

    def direct(piece, dy, outer):
        def source(y, x, c, h, z):
            s = side(dy, z)
            return (y + dy, x ^ s, c, h ^ (s if outer else 0), z)

        return fetch(piece, source)

    near = {1: direct(p1, 1, True), 3: direct(p3, 3, True)}
    near[2] = direct(p2, 2, False)
    across = from_x(p0)
    half = rows // 2
    far = {
        1: [from_z(near[1], -1)],
        3: [from_z(near[3], 1)],
        2: [from_z(near[2][:half], -1), from_z(near[2][half:], 1)],
    }
    flag = odd.reshape(1).astype(jnp.int32)
    weights = (head_weight, partner_weight)

    to_x, *to_y = products(flag, near, far, [], weights, True)
    got_x = from_x(to_x)
    got_y = [from_y(v, -dy) for v, dy in zip(to_y, (1, 2, 3))]
    kept, token = products(flag, near, far, [across, own], weights, False)
    send_y = combine_y(kept, got_x, rows, width)
    send_x = combine_x(kept, got_y, rows, width)
    received = [from_x(send_x)]
    received += [from_y(v, -dy) for v, dy in zip(send_y, (1, 2, 3))]

    token = token[0, 0]
    targets = targets + token
    later = odd + token
    first_column = (block_index * width).reshape(1).astype(jnp.int32)
    labels = lax.dynamic_slice_in_dim(targets, here * rows, rows, 0)
    spread = lambda v: jnp.broadcast_to(v[:, None], (v.shape[0], LANES))
    raised, stats = finish(kept, received, spread(labels), first_column, rows, width)

    g = ROWS_OUT
    side_x = from_x(raised)
    along = {dy: from_y(raised, dy) for dy in (2, 1, 3)}
    far_y = {dy: from_y(side_x[g:], dy) for dy in (2, 1, 3)}
    far_x = {dy: from_x(along[dy][:g]) for dy in (1, 3, 2)}

    stats = stats[:, :3].T
    every = lax.all_to_all(
        jnp.broadcast_to(stats[None], (16, *stats.shape)), "vocab", 0, 0, tiled=True
    )
    top = jnp.max(every[:, 0], axis=0)
    total = jnp.sum(every[:, 1] * jnp.exp(every[:, 0] - top[None]), axis=0)
    loss = top + jnp.log(total) - jnp.sum(every[:, 2], axis=0)
    factor = jnp.exp(stats[0] - top) / total
    factors = lax.all_to_all(
        jnp.broadcast_to(factor[None], (16, rows)), "dp", 0, 0, tiled=True
    )

    ids = targets.reshape(16, rows)

    def pick(table, dy, dx, a, b):
        owner = (((y + dy) % Y) * X + (x ^ dx)) * C + c
        return lax.dynamic_index_in_dim(table, owner, 0, keepdims=False)[a:b]

    def both(spans):
        return [
            spread(jnp.concatenate([pick(t, *s) for s in spans])) for t in (factors, ids)
        ]

    def states(dy, dx):
        if dy == 0:
            return across if dx else own
        whole = jnp.concatenate(far[dy], axis=0)
        return jnp.where((later if dy != 3 else 1 - later) == dx, near[dy], whole)

    def gathered(spans):
        whole = jnp.concatenate([states(dy, dx)[a:b] for dy, dx, a, b in spans], axis=0)
        whole = whole + token.astype(BF16)
        other = from_core(whole[:, depth:])
        return jnp.concatenate([whole[:, :depth], other], axis=0).T

    near_spans = [(dy, 0, 0, rows) for dy in range(Y)] + [(0, 1, 0, rows)]
    far_spans = [(dy, 1, 0, g) for dy in (1, 2, 3)] + [(dy, 1, g, rows) for dy in (1, 2, 3)]
    near_states = gathered(near_spans)
    far_states = gathered(far_spans)
    slope_near = slopes(
        [raised, along[1], along[2], along[3], side_x],
        *both(near_spans), first_column, width,
    )
    slope_far = slopes(
        [far_x[d] for d in (1, 2, 3)] + [far_y[d] for d in (1, 2, 3)],
        *both(far_spans), first_column, width,
    )
    near_other = from_core(slope_near)
    far_other = from_core(slope_far)
    grad = gradient(near_states, slope_near, near_other, None)
    grad = gradient(far_states, slope_far, far_other, grad)
    return (loss, grad)


def solution(mesh):
    in_specs = (P("dp", None), P("dp", "vocab"), P())
    out_specs = (P("dp"), P("dp", "vocab"))

    return jax.shard_map(
        per_device, mesh=mesh, in_specs=in_specs, out_specs=out_specs, check_vma=False
    )
```

time: 370 us -> 326 us (0.88)
  waiting for transfers between devices: 243 us -> 73.2 us
  Pallas kernels: 0 us -> 115 us
  blocking collectives: 56.7 us -> 0 us
  starting transfers between devices: 9.04 us -> 60.5 us
  local copies, waits for them, and re-layouts: 17.4 us -> 59.4 us
  matrix products: 23.9 us -> 0 us
  between operations: 14.1 us -> 2.25 us
  other arithmetic: 5.98 us -> 13.8 us
    reduce_scatter x1 -> x0, waiting for transfers between devices: 184 us -> none  [per_device(): lax.psum_scatter(partial_all, 'dp', scatter_dimension=0, tiled=True)]
    pallas_call x0 -> x10, Pallas kernels: none -> 115 us  [the longest x1 61.4 us: pieces_of(): pl.pallas_call(body, in_specs=[pl.BlockSpec(memory_space=pltpu.SMEM), pl....]
    ppermute x0 -> x31, waiting for transfers between devices: none -> 65.5 us  [fetch(): return lax.ppermute(value, AXES, pairs)]
    all_to_all x2 -> x0, blocking collectives: 56.7 us -> none  [the longest x1 45.3 us: per_device(): lax.all_to_all(hidden, 'dp', split_axis=1, concat_axis=0, tiled=True)]
    all_gather x1 -> x0, waiting for transfers between devices: 50.8 us -> none  [per_device(): lax.all_gather(slope, 'dp', axis=0, tiled=True)]
    ppermute x0 -> x31, starting transfers between devices: none -> 48.4 us  [fetch(): return lax.ppermute(value, AXES, pairs)]
    dot_general x2 -> x0, matrix products: 23.9 us -> none  [the longest x1 12 us: per_device(): jnp.dot(spread, head_weight, preferred_element_type=jnp.float32)]
    ppermute x0 -> x8, local copies, waits for them, and re-layouts: none -> 14.2 us  [fetch(): return lax.ppermute(value, AXES, pairs)]
  transfers between devices with their start and end apart: 3 -> 33, of which waited for: 3 -> 14; matrix products, arithmetic and copies ran while one was open for 0% -> 20% of each run, Pallas kernels for 0% -> 25%
where the time goes in v1:
time: 326 us; the launch traced here: 324 us
  Pallas kernels  115 us (35%)
  waiting for transfers between devices  73.2 us (22%)
  starting transfers between devices  60.5 us (19%)
  local copies, waits for them, and re-layouts  59.4 us (18%)
  other arithmetic  13.8 us (4%)
    ppermute x31, waiting for transfers between devices, fetch(): return lax.ppermute(value, AXES, pairs)  65.5 us
    pallas_call x1, Pallas kernels, pieces_of(): pl.pallas_call(body, in_specs=[pl.BlockSpec(memory_space=pltpu.SMEM), pl....  61.4 us
    ppermute x31, starting transfers between devices, fetch(): return lax.ppermute(value, AXES, pairs)  48.4 us
    pallas_call x2, Pallas kernels, gradient(): pl.pallas_call(body, grid=(STEPS,), in_specs=[full((depth, double)), col(...  18.3 us
    pallas_call x2, Pallas kernels, products(): pl.pallas_call(body, grid=(STEPS,), in_specs=[pl.BlockSpec(memory_space=p...  16.9 us
    ppermute x8, local copies, waits for them, and re-layouts, fetch(): return lax.ppermute(value, AXES, pairs)  14.2 us
    unnamed x61, local copies, waits for them, and re-layouts  11.2 us
    pallas_call x5, local copies, waits for them, and re-layouts, pieces_of(): pl.pallas_call(body, in_specs=[pl.BlockSpec(memory_space=pltpu.SMEM), pl....  9.62 us
  transfers between devices with their start and end apart: 33, of which 14 were waited for; matrix products, arithmetic and copies ran while one was open for 20% of the time, Pallas kernels for 25%

profile of v1, /device:TPU:1, one launch (start us, length us, event | category | flops | bytes accessed | tf_op | source)
XLA Modules:
  0.0 324.0 jit_solution(13077398104522332109)
XLA Ops:
  0.6 3.3 %collective-permute-start.8 = (bf16[768,2048]{1,0:T(8,128)(2,1)}, bf16[768,2048]{1,0:T(8,128)(2,1)S(1)}, u32[]{:S(2)}, u32[]{:S(2)}) collective-permute-start(bf16[768,2048]{1,0:T(8,128)(2,1)} %refs_7_.1), channel_id=1, source_target_pairs={{16,0},{17,1},{18,2},{19,3},{20,4},{21,5},{22,6},{23,7},{24,8},{25... | collective-permute-start | bytes 9437192 | tf_op jit(solution)/shard_map/ppermute | solution.py:30
  4.5 61.4 %pieces.1 = (bf16[128,1536]{1,0:T(8,128)(2,1)}, bf16[128,1536]{1,0:T(8,128)(2,1)}, bf16[128,1536]{1,0:T(8,128)(2,1)}, bf16[128,1536]{1,0:T(8,128)(2,1)}, bf16[128,1536]{1,0:T(8,128)(2,1)}) custom-call(s32[10]{0:T(128)} %stack.43.at_ref, bf16[128,12288]{1,0:T(8,128)(2,1)} %source.1), custom_call_target="tpu_custom_call" | custom-call | tf_op jit(solution)/shard_map/pieces/pallas_call | solution.py:291
  73.7 2.9 collective-permute-start.1
  80.4 2.8 collective-permute-start.3
  84.7 14.0 %collective-permute-start.6 = (bf16[128,1536]{0,1:T(8,128)(2,1)}, bf16[128,1536]{0,1:T(8,128)(2,1)}, u32[]{:S(2)}, u32[]{:S(2)}) collective-permute-start(bf16[128,1536]{0,1:T(8,128)(2,1)} %collective-permute-done.2), channel_id=1, source_target_pairs={{1,0},{2,1},{3,2},{4,3},{5,4},{6,5},{7,6},{0,7},{9,8},{10,9},{11,1... | collective-permute-start | bytes 1179656 | tf_op jit(solution)/shard_map/ppermute | solution.py:30
  99.8 2.7 collective-permute-start.5
  122.0 9.1 %keeps.1 = (f32[640,2048]{1,0:T(8,128)}, s32[8,128]{1,0:T(8,128)}) custom-call(s32[1]{0:T(128)} %bitcast.1.flag_ref, bf16[128,1536]{1,0:T(8,128)(2,1)} %copy.105.refs_0_, bf16[128,1536]{1,0:T(8,128)(2,1)} %copy.106.refs_1_, bf16[128,1536]{1,0:T(8,128)(2,1)} %copy.107.refs_2_, bf16[128,1536]{1,0:T(8,128)(2,1)} %copy.108.refs_3_, ...), custom_call_target="tpu_custom_call" | custom-call | tf_op jit(solution)/shard_map/keeps/pallas_call | solution.py:149
  134.2 7.8 %sends.1 = (s16[3,48,2176]{2,1,0:T(8,128)(2,1)}, s16[80,2176]{1,0:T(8,128)(2,1)}, s16[80,2176]{1,0:T(8,128)(2,1)}, s16[80,2176]{1,0:T(8,128)(2,1)}) custom-call(s32[1]{0:T(128)} %bitcast.1.flag_ref, bf16[128,1536]{1,0:T(8,128)(2,1)} %copy.105.refs_0_, bf16[128,1536]{1,0:T(8,128)(2,1)} %copy.106.refs_1_, bf16[128,1536]{1,0:T(8,128)(2,1)} %copy.107.refs_2_, ...), custom_call_target="tpu_custom_call" | custom-call | tf_op jit(solution)/shard_map/sends/pallas_call | solution.py:149
  144.5 2.1 select_dynamic-update-slice_fusion.2
  146.5 2.2 select_dynamic-update-slice_fusion.1
  148.7 2.1 select_dynamic-update-slice_fusion
  158.6 2.8 collective-permute-done.9.g1
  161.4 2.7 combine_x.1
  165.5 4.4 %combine_y.1 = (s16[128,2176]{1,0:T(8,128)(2,1)}, s16[128,2176]{1,0:T(8,128)(2,1)}, s16[128,2176]{1,0:T(8,128)(2,1)}) custom-call(f32[640,2048]{1,0:T(8,128)} %get-tuple-element.23.kept_ref, s16[3,48,2176]{2,1,0:T(8,128)(2,1)} %collective-permute-done.13.got), custom_call_target="tpu_custom_call" | custom-call | tf_op jit(solution)/shard_map/combine_y/pallas_call | solution.py:179
  175.9 2.2 collective-permute-done.12.g1
  178.2 18.6 %collective-permute-done.14.g2 = s16[128,2176]{1,0:T(8,128)(2,1)} collective-permute-done((s16[128,2176]{1,0:T(8,128)(2,1)}, s16[128,2176]{1,0:T(8,128)(2,1)}, u32[]{:S(2)}, u32[]{:S(2)}) %collective-permute-start.14) | collective-permute-done | bytes 557088 | tf_op jit(solution)/shard_map/ppermute | solution.py:30
  197.9 3.6 %finish.1 = (bf16[128,2048]{1,0:T(8,128)(2,1)}, f32[128,128]{1,0:T(8,128)}) custom-call(s32[1]{0:T(128)} %bitcast.first_ref, f32[640,2048]{1,0:T(8,128)} %get-tuple-element.23.kept_ref, s16[128,2176]{1,0:T(8,128)(2,1)} %collective-permute-done.12.g1, s16[128,2176]{1,0:T(8,128)(2,1)} %collective-permute-done.14.g2, ...), custom_call_target="tpu_custom_call" | custom-call | tf_op jit(solution)/shard_map/finish/pallas_call | solution.py:227
  203.0 5.0 %all-to-all-start = ((f32[16,3,128]{2,1,0:T(4,128)}), f32[16,3,128]{2,1,0:T(4,128)S(1)}, u32[]{:S(2)}, u32[]{:S(2)}) async-start(f32[16,3,128]{2,1,0:T(4,128)} %broadcast_in_dim.15), calls=%async_computation | async-start | bytes 65536 | tf_op jit(solution)/shard_map/all_to_all | solution.py:385
  209.3 7.6 %all-to-all-done = f32[16,3,128]{2,1,0:T(4,128)S(1)} async-done(((f32[16,3,128]{2,1,0:T(4,128)}), f32[16,3,128]{2,1,0:T(4,128)S(1)}, u32[]{:S(2)}, u32[]{:S(2)}) %all-to-all-start) | async-done | bytes 24608 | tf_op jit(solution)/shard_map/all_to_all | solution.py:385
  218.0 7.0 %all-to-all-start.1 = ((f32[16,1,128]{2,1,0:T(1,128)}), f32[16,1,128]{2,1,0:T(1,128)}, u32[]{:S(2)}, u32[]{:S(2)}) async-start(f32[16,1,128]{2,1,0:T(1,128)} %broadcast_in_dim.16), calls=%async_computation.1 | async-start | bytes 16384 | tf_op jit(solution)/shard_map/all_to_all | solution.py:392
  228.4 2.7 collective-permute-start.18
  237.3 16.1 %collective-permute-done.18.refs_1_ = bf16[128,2048]{1,0:T(8,128)(2,1)S(1)} collective-permute-done((bf16[128,2048]{1,0:T(8,128)(2,1)}, bf16[128,2048]{1,0:T(8,128)(2,1)S(1)}, u32[]{:S(2)}, u32[]{:S(2)}) %collective-permute-start.18) | collective-permute-done | bytes 524320 | tf_op jit(solution)/shard_map/ppermute | solution.py:30
  253.4 4.5 %collective-permute-done.22.refs_3_ = bf16[128,2048]{1,0:T(8,128)(2,1)S(1)} collective-permute-done((bf16[128,2048]{1,0:T(8,128)(2,1)}, bf16[128,2048]{1,0:T(8,128)(2,1)S(1)}, u32[]{:S(2)}, u32[]{:S(2)}) %collective-permute-start.22) | collective-permute-done | bytes 524320 | tf_op jit(solution)/shard_map/ppermute | solution.py:30
  260.4 4.4 %shard_map.51.s_ref = bf16[640,2048]{1,0:T(8,128)(2,1)} custom-call(s32[1]{0:T(128)} %bitcast.first_ref, bf16[128,2048]{1,0:T(8,128)(2,1)} %get-tuple-element.33.refs_0_, bf16[128,2048]{1,0:T(8,128)(2,1)} %copy-done.4, bf16[128,2048]{1,0:T(8,128)(2,1)} %copy-done.3, bf16[128,2048]{1,0:T(8,128)(2,1)} %copy-done.2, ...), custom_call_target="tpu_custom_call" | custom-call | tf_op jit(solution)/shard_map/pallas_call | solution.py:259
  274.3 2.6 collective-permute-start.27
  277.0 6.8 %collective-permute-done.27.refs_5_ = bf16[48,2048]{1,0:T(8,128)(2,1)} collective-permute-done((bf16[48,2048]{1,0:T(8,128)(2,1)S(1)}, bf16[48,2048]{1,0:T(8,128)(2,1)}, u32[]{:S(2)}, u32[]{:S(2)}) %collective-permute-start.27) | collective-permute-done | bytes 196640 | tf_op jit(solution)/shard_map/ppermute | solution.py:30
  285.3 5.7 %collective-permute-done.23.refs_2_ = bf16[80,2048]{1,0:T(8,128)(2,1)S(1)} collective-permute-done((bf16[80,2048]{1,0:T(8,128)(2,1)S(1)}, bf16[80,2048]{1,0:T(8,128)(2,1)S(1)}, u32[]{:S(2)}, u32[]{:S(2)}) %collective-permute-start.23) | collective-permute-done | bytes 327712 | tf_op jit(solution)/shard_map/ppermute | solution.py:30
  292.5 3.4 %shard_map.50.s_ref = bf16[384,2048]{1,0:T(8,128)(2,1)} custom-call(s32[1]{0:T(128)} %bitcast.first_ref, bf16[80,2048]{1,0:T(8,128)(2,1)} %copy-done.5, bf16[80,2048]{1,0:T(8,128)(2,1)} %copy-done.6, bf16[80,2048]{1,0:T(8,128)(2,1)} %copy-done.7, bf16[48,2048]{1,0:T(8,128)(2,1)} %copy-done.8, bf16[48,2048]{1,0:T(8,128)(2,1)} %copy-done.9, ...), custom_call_target="tpu_custom_call" | custom-call | tf_op jit(solution)/shard_map/pallas_call | solution.py:259
  297.7 3.7 %collective-permute-done.17 = bf16[384,768]{0,1:T(8,128)(2,1)S(1)} collective-permute-done((bf16[384,768]{0,1:T(8,128)(2,1)S(1)}, bf16[384,768]{0,1:T(8,128)(2,1)S(1)}, u32[]{:S(2)}, u32[]{:S(2)}) %collective-permute-start.17) | collective-permute-done | bytes 589856 | tf_op jit(solution)/shard_map/ppermute | solution.py:30
  302.5 2.6 maximum_bitcast_fusion.turned_ref
  305.7 9.3 %shard_map.52.refs_0_ = f32[768,2048]{1,0:T(8,128)} custom-call(bf16[768,1280]{1,0:T(8,128)(2,1)} %maximum_bitcast_fusion.turned_ref, bf16[640,2048]{1,0:T(8,128)(2,1)} %shard_map.51.s_ref, bf16[640,2048]{1,0:T(8,128)(2,1)} %collective-permute-done.30.o_ref), custom_call_target="tpu_custom_call" | custom-call | tf_op jit(solution)/shard_map/pallas_call | solution.py:313
  315.0 9.0 %shard_map.53 = f32[768,2048]{1,0:T(8,128)} custom-call(bf16[768,768]{1,0:T(8,128)(2,1)} %maximum_bitcast_fusion.1.turned_ref, bf16[384,2048]{1,0:T(8,128)(2,1)} %shard_map.50.s_ref, bf16[384,2048]{1,0:T(8,128)(2,1)} %collective-permute-done.28.o_ref, f32[768,2048]{1,0:T(8,128)} %shard_map.52.refs_0_), custom_call_target="tpu_custom_call" | custom-call | tf_op jit(solution)/shard_map/pallas_call | solution.py:313
  (175 shorter events, 86.7 us)
Async XLA Ops:
  0.6 119.8 %collective-permute-start.8 = (bf16[768,2048]{1,0:T(8,128)(2,1)}, bf16[768,2048]{1,0:T(8,128)(2,1)S(1)}, u32[]{:S(2)}, u32[]{:S(2)}) collective-permute-start(bf16[768,2048]{1,0:T(8,128)(2,1)} %refs_7_.1), channel_id=1, source_target_pairs={{16,0},{17,1},{18,2},{19,3},{20,4},{21,5},{22,6},{23,7},{24,8},{25... | collective-permute-start | bytes 9437192 | tf_op jit(solution)/shard_map/ppermute | solution.py:30
  67.8 12.6 %collective-permute-start = (bf16[128,1536]{0,1:T(8,128)(2,1)}, bf16[128,1536]{0,1:T(8,128)(2,1)}, u32[]{:S(2)}, u32[]{:S(2)}) collective-permute-start(bf16[128,1536]{0,1:T(8,128)(2,1)} %copy.101), channel_id=1, source_target_pairs={{64,0},{105,1},{66,2},{107,3},{68,4},{109,5},{70,6},{111,7},{72,8}... | collective-permute-start | bytes 1179656 | tf_op jit(solution)/shard_map/ppermute | solution.py:30
  70.8 13.9 %collective-permute-start.2 = (bf16[128,1536]{0,1:T(8,128)(2,1)}, bf16[128,1536]{0,1:T(8,128)(2,1)}, u32[]{:S(2)}, u32[]{:S(2)}) collective-permute-start(bf16[128,1536]{0,1:T(8,128)(2,1)} %copy.103), channel_id=1, source_target_pairs={{232,0},{193,1},{234,2},{195,3},{236,4},{197,5},{238,6},{199,7},{2... | collective-permute-start | bytes 1179656 | tf_op jit(solution)/shard_map/ppermute | solution.py:30
  73.7 25.1 %collective-permute-start.1 = (bf16[128,1536]{0,1:T(8,128)(2,1)}, bf16[128,1536]{0,1:T(8,128)(2,1)S(1)}, u32[]{:S(2)}, u32[]{:S(2)}) collective-permute-start(bf16[128,1536]{0,1:T(8,128)(2,1)} %copy.102), channel_id=1, source_target_pairs={{128,0},{161,1},{130,2},{163,3},{132,4},{165,5},{134,6},{167,7},{1... | collective-permute-start | bytes 1179656 | tf_op jit(solution)/shard_map/ppermute | solution.py:30
  78.5 21.3 %collective-permute-start.7 = (bf16[128,1536]{0,1:T(8,128)(2,1)}, bf16[128,1536]{0,1:T(8,128)(2,1)}, u32[]{:S(2)}, u32[]{:S(2)}) collective-permute-start(bf16[128,1536]{0,1:T(8,128)(2,1)} %copy.104), channel_id=1, source_target_pairs={{32,0},{33,1},{34,2},{35,3},{36,4},{37,5},{38,6},{39,7},{40,8},{41... | collective-permute-start | bytes 1179656 | tf_op jit(solution)/shard_map/ppermute | solution.py:30
  80.4 36.1 %collective-permute-start.3 = (bf16[128,1536]{0,1:T(8,128)(2,1)}, bf16[128,1536]{0,1:T(8,128)(2,1)}, u32[]{:S(2)}, u32[]{:S(2)}) collective-permute-start(bf16[128,1536]{0,1:T(8,128)(2,1)} %collective-permute-done), channel_id=1, source_target_pairs={{7,0},{0,1},{1,2},{2,3},{3,4},{4,5},{5,6},{6,7},{15,8},{8,9},{9,10... | collective-permute-start | bytes 1179656 | tf_op jit(solution)/shard_map/ppermute | solution.py:30
  84.7 33.7 %collective-permute-start.6 = (bf16[128,1536]{0,1:T(8,128)(2,1)}, bf16[128,1536]{0,1:T(8,128)(2,1)}, u32[]{:S(2)}, u32[]{:S(2)}) collective-permute-start(bf16[128,1536]{0,1:T(8,128)(2,1)} %collective-permute-done.2), channel_id=1, source_target_pairs={{1,0},{2,1},{3,2},{4,3},{5,4},{6,5},{7,6},{0,7},{9,8},{10,9},{11,1... | collective-permute-start | bytes 1179656 | tf_op jit(solution)/shard_map/ppermute | solution.py:30
  99.8 11.3 %collective-permute-start.4 = (bf16[64,1536]{0,1:T(8,128)(2,1)}, bf16[64,1536]{0,1:T(8,128)(2,1)}, u32[]{:S(2)}, u32[]{:S(2)}) collective-permute-start(bf16[64,1536]{0,1:T(8,128)(2,1)} %get-tuple-element.45), channel_id=1, source_target_pairs={{7,0},{0,1},{1,2},{2,3},{3,4},{4,5},{5,6},{6,7},{15,8},{8,9},{9,10... | collective-permute-start | bytes 589832 | tf_op jit(solution)/shard_map/ppermute | solution.py:30
  99.8 14.9 %collective-permute-start.5 = (bf16[64,1536]{0,1:T(8,128)(2,1)}, bf16[64,1536]{0,1:T(8,128)(2,1)}, u32[]{:S(2)}, u32[]{:S(2)}) collective-permute-start(bf16[64,1536]{0,1:T(8,128)(2,1)} %get-tuple-element.44), channel_id=1, source_target_pairs={{1,0},{2,1},{3,2},{4,3},{5,4},{6,5},{7,6},{0,7},{9,8},{10,9},{11,1... | collective-permute-start | bytes 589832 | tf_op jit(solution)/shard_map/ppermute | solution.py:30
  142.0 23.5 %collective-permute-start.13 = (s16[3,48,2176]{2,1,0:T(8,128)(2,1)}, s16[3,48,2176]{2,1,0:T(8,128)(2,1)}, u32[]{:S(2)}, u32[]{:S(2)}) collective-permute-start(s16[3,48,2176]{2,1,0:T(8,128)(2,1)} %get-tuple-element.27), channel_id=1, source_target_pairs={{32,0},{33,1},{34,2},{35,3},{36,4},{37,5},{38,6},{39,7},{40,8},{41... | collective-permute-start | bytes 1880072 | tf_op jit(solution)/shard_map/ppermute | solution.py:30
  142.0 16.6 %collective-permute-start.10 = (s16[80,2176]{1,0:T(8,128)(2,1)}, s16[80,2176]{1,0:T(8,128)(2,1)}, u32[]{:S(2)}, u32[]{:S(2)}) collective-permute-start(s16[80,2176]{1,0:T(8,128)(2,1)} %get-tuple-element.25), channel_id=1, source_target_pairs={{128,0},{129,1},{130,2},{131,3},{132,4},{133,5},{134,6},{135,7},{1... | collective-permute-start | bytes 1044488 | tf_op jit(solution)/shard_map/ppermute | solution.py:30
  142.1 16.5 %collective-permute-start.11 = (s16[80,2176]{1,0:T(8,128)(2,1)}, s16[80,2176]{1,0:T(8,128)(2,1)}, u32[]{:S(2)}, u32[]{:S(2)}) collective-permute-start(s16[80,2176]{1,0:T(8,128)(2,1)} %get-tuple-element.26), channel_id=1, source_target_pairs={{64,0},{65,1},{66,2},{67,3},{68,4},{69,5},{70,6},{71,7},{72,8},{73... | collective-permute-start | bytes 1044488 | tf_op jit(solution)/shard_map/ppermute | solution.py:30
  143.8 17.6 %collective-permute-start.9 = (s16[80,2176]{1,0:T(8,128)(2,1)}, s16[80,2176]{1,0:T(8,128)(2,1)}, u32[]{:S(2)}, u32[]{:S(2)}) collective-permute-start(s16[80,2176]{1,0:T(8,128)(2,1)} %get-tuple-element.24), channel_id=1, source_target_pairs={{192,0},{193,1},{194,2},{195,3},{196,4},{197,5},{198,6},{199,7},{2... | collective-permute-start | bytes 1044488 | tf_op jit(solution)/shard_map/ppermute | solution.py:30
  164.1 14.0 %collective-permute-start.12 = (s16[128,2176]{1,0:T(8,128)(2,1)}, s16[128,2176]{1,0:T(8,128)(2,1)}, u32[]{:S(2)}, u32[]{:S(2)}) collective-permute-start(s16[128,2176]{1,0:T(8,128)(2,1)} %combine_x.1), channel_id=1, source_target_pairs={{32,0},{33,1},{34,2},{35,3},{36,4},{37,5},{38,6},{39,7},{40,8},{41... | collective-permute-start | bytes 1671176 | tf_op jit(solution)/shard_map/ppermute | solution.py:30
  169.9 26.9 %collective-permute-start.14 = (s16[128,2176]{1,0:T(8,128)(2,1)}, s16[128,2176]{1,0:T(8,128)(2,1)}, u32[]{:S(2)}, u32[]{:S(2)}) collective-permute-start(s16[128,2176]{1,0:T(8,128)(2,1)} %get-tuple-element.28), channel_id=1, source_target_pairs={{192,0},{193,1},{194,2},{195,3},{196,4},{197,5},{198,6},{199,7},{2... | collective-permute-start | bytes 1671176 | tf_op jit(solution)/shard_map/ppermute | solution.py:30
  169.9 26.9 %collective-permute-start.15 = (s16[128,2176]{1,0:T(8,128)(2,1)}, s16[128,2176]{1,0:T(8,128)(2,1)}, u32[]{:S(2)}, u32[]{:S(2)}) collective-permute-start(s16[128,2176]{1,0:T(8,128)(2,1)} %get-tuple-element.29), channel_id=1, source_target_pairs={{128,0},{129,1},{130,2},{131,3},{132,4},{133,5},{134,6},{135,7},{1... | collective-permute-start | bytes 1671176 | tf_op jit(solution)/shard_map/ppermute | solution.py:30
  171.0 26.2 %collective-permute-start.16 = (s16[128,2176]{1,0:T(8,128)(2,1)}, s16[128,2176]{1,0:T(8,128)(2,1)}, u32[]{:S(2)}, u32[]{:S(2)}) collective-permute-start(s16[128,2176]{1,0:T(8,128)(2,1)} %get-tuple-element.30), channel_id=1, source_target_pairs={{64,0},{65,1},{66,2},{67,3},{68,4},{69,5},{70,6},{71,7},{72,8},{73... | collective-permute-start | bytes 1671176 | tf_op jit(solution)/shard_map/ppermute | solution.py:30
  203.0 13.9 %all-to-all-start = ((f32[16,3,128]{2,1,0:T(4,128)}), f32[16,3,128]{2,1,0:T(4,128)S(1)}, u32[]{:S(2)}, u32[]{:S(2)}) async-start(f32[16,3,128]{2,1,0:T(4,128)} %broadcast_in_dim.15), calls=%async_computation | async-start | bytes 65536 | tf_op jit(solution)/shard_map/all_to_all | solution.py:385
  218.0 15.4 %all-to-all-start.1 = ((f32[16,1,128]{2,1,0:T(1,128)}), f32[16,1,128]{2,1,0:T(1,128)}, u32[]{:S(2)}, u32[]{:S(2)}) async-start(f32[16,1,128]{2,1,0:T(1,128)} %broadcast_in_dim.16), calls=%async_computation.1 | async-start | bytes 16384 | tf_op jit(solution)/shard_map/all_to_all | solution.py:392
  228.4 25.0 %collective-permute-start.18 = (bf16[128,2048]{1,0:T(8,128)(2,1)}, bf16[128,2048]{1,0:T(8,128)(2,1)S(1)}, u32[]{:S(2)}, u32[]{:S(2)}) collective-permute-start(bf16[128,2048]{1,0:T(8,128)(2,1)} %get-tuple-element.33.refs_0_), channel_id=1, source_target_pairs={{64,0},{65,1},{66,2},{67,3},{68,4},{69,5},{70,6},{71,7},{72,8},{73... | collective-permute-start | bytes 1572872 | tf_op jit(solution)/shard_map/ppermute | solution.py:30
  231.1 22.3 %collective-permute-start.20 = (bf16[128,2048]{1,0:T(8,128)(2,1)}, bf16[128,2048]{1,0:T(8,128)(2,1)S(1)}, u32[]{:S(2)}, u32[]{:S(2)}) collective-permute-start(bf16[128,2048]{1,0:T(8,128)(2,1)} %get-tuple-element.33.refs_0_), channel_id=1, source_target_pairs={{128,0},{129,1},{130,2},{131,3},{132,4},{133,5},{134,6},{135,7},{1... | collective-permute-start | bytes 1572872 | tf_op jit(solution)/shard_map/ppermute | solution.py:30
  231.6 26.3 %collective-permute-start.22 = (bf16[128,2048]{1,0:T(8,128)(2,1)}, bf16[128,2048]{1,0:T(8,128)(2,1)S(1)}, u32[]{:S(2)}, u32[]{:S(2)}) collective-permute-start(bf16[128,2048]{1,0:T(8,128)(2,1)} %get-tuple-element.33.refs_0_), channel_id=1, source_target_pairs={{192,0},{193,1},{194,2},{195,3},{196,4},{197,5},{198,6},{199,7},{2... | collective-permute-start | bytes 1572872 | tf_op jit(solution)/shard_map/ppermute | solution.py:30
  232.2 25.7 %collective-permute-start.24 = (bf16[128,2048]{1,0:T(8,128)(2,1)}, bf16[128,2048]{1,0:T(8,128)(2,1)}, u32[]{:S(2)}, u32[]{:S(2)}) collective-permute-start(bf16[128,2048]{1,0:T(8,128)(2,1)} %get-tuple-element.33.refs_0_), channel_id=1, source_target_pairs={{32,0},{33,1},{34,2},{35,3},{36,4},{37,5},{38,6},{39,7},{40,8},{41... | collective-permute-start | bytes 1572872 | tf_op jit(solution)/shard_map/ppermute | solution.py:30
  264.7 41.0 %collective-permute-start.30 = (bf16[640,2048]{1,0:T(8,128)(2,1)}, bf16[640,2048]{1,0:T(8,128)(2,1)}, u32[]{:S(2)}, u32[]{:S(2)}) collective-permute-start(bf16[640,2048]{1,0:T(8,128)(2,1)} %shard_map.51.s_ref), channel_id=1, source_target_pairs={{16,0},{17,1},{18,2},{19,3},{20,4},{21,5},{22,6},{23,7},{24,8},{25... | collective-permute-start | bytes 7864328 | tf_op jit(solution)/shard_map/ppermute | solution.py:30
  266.2 6.5 %collective-permute-start.25 = (bf16[48,2048]{1,0:T(8,128)(2,1)S(1)}, bf16[48,2048]{1,0:T(8,128)(2,1)S(1)}, u32[]{:S(2)}, u32[]{:S(2)}) collective-permute-start(bf16[48,2048]{1,0:T(8,128)(2,1)S(1)} %slice.203), channel_id=1, source_target_pairs={{64,0},{65,1},{66,2},{67,3},{68,4},{69,5},{70,6},{71,7},{72,8},{73... | collective-permute-start | bytes 589832 | tf_op jit(solution)/shard_map/ppermute | solution.py:30
  266.6 7.7 %collective-permute-start.26 = (bf16[48,2048]{1,0:T(8,128)(2,1)S(1)}, bf16[48,2048]{1,0:T(8,128)(2,1)S(1)}, u32[]{:S(2)}, u32[]{:S(2)}) collective-permute-start(bf16[48,2048]{1,0:T(8,128)(2,1)S(1)} %slice.203), channel_id=1, source_target_pairs={{128,0},{129,1},{130,2},{131,3},{132,4},{133,5},{134,6},{135,7},{1... | collective-permute-start | bytes 589832 | tf_op jit(solution)/shard_map/ppermute | solution.py:30
  268.1 17.2 %collective-permute-start.19 = (bf16[80,2048]{1,0:T(8,128)(2,1)S(1)}, bf16[80,2048]{1,0:T(8,128)(2,1)S(1)}, u32[]{:S(2)}, u32[]{:S(2)}) collective-permute-start(bf16[80,2048]{1,0:T(8,128)(2,1)S(1)} %slice.200), channel_id=1, source_target_pairs={{32,0},{33,1},{34,2},{35,3},{36,4},{37,5},{38,6},{39,7},{40,8},{41... | collective-permute-start | bytes 983048 | tf_op jit(solution)/shard_map/ppermute | solution.py:30
  270.4 14.9 %collective-permute-start.21 = (bf16[80,2048]{1,0:T(8,128)(2,1)S(1)}, bf16[80,2048]{1,0:T(8,128)(2,1)S(1)}, u32[]{:S(2)}, u32[]{:S(2)}) collective-permute-start(bf16[80,2048]{1,0:T(8,128)(2,1)S(1)} %slice.201), channel_id=1, source_target_pairs={{32,0},{33,1},{34,2},{35,3},{36,4},{37,5},{38,6},{39,7},{40,8},{41... | collective-permute-start | bytes 983048 | tf_op jit(solution)/shard_map/ppermute | solution.py:30
  272.7 18.2 %collective-permute-start.23 = (bf16[80,2048]{1,0:T(8,128)(2,1)S(1)}, bf16[80,2048]{1,0:T(8,128)(2,1)S(1)}, u32[]{:S(2)}, u32[]{:S(2)}) collective-permute-start(bf16[80,2048]{1,0:T(8,128)(2,1)S(1)} %slice.202), channel_id=1, source_target_pairs={{32,0},{33,1},{34,2},{35,3},{36,4},{37,5},{38,6},{39,7},{40,8},{41... | collective-permute-start | bytes 983048 | tf_op jit(solution)/shard_map/ppermute | solution.py:30
  274.3 9.6 %collective-permute-start.27 = (bf16[48,2048]{1,0:T(8,128)(2,1)S(1)}, bf16[48,2048]{1,0:T(8,128)(2,1)}, u32[]{:S(2)}, u32[]{:S(2)}) collective-permute-start(bf16[48,2048]{1,0:T(8,128)(2,1)S(1)} %slice.203), channel_id=1, source_target_pairs={{192,0},{193,1},{194,2},{195,3},{196,4},{197,5},{198,6},{199,7},{2... | collective-permute-start | bytes 589832 | tf_op jit(solution)/shard_map/ppermute | solution.py:30
  283.8 18.7 %collective-permute-start.29 = (bf16[640,768]{0,1:T(8,128)(2,1)}, bf16[640,768]{0,1:T(8,128)(2,1)}, u32[]{:S(2)}, u32[]{:S(2)}) collective-permute-start(bf16[640,768]{0,1:T(8,128)(2,1)} %get-tuple-element.35), channel_id=1, source_target_pairs={{16,0},{17,1},{18,2},{19,3},{20,4},{21,5},{22,6},{23,7},{24,8},{25... | collective-permute-start | bytes 2949128 | tf_op jit(solution)/shard_map/ppermute | solution.py:30
  295.9 19.1 %collective-permute-start.28 = (bf16[384,2048]{1,0:T(8,128)(2,1)}, bf16[384,2048]{1,0:T(8,128)(2,1)}, u32[]{:S(2)}, u32[]{:S(2)}) collective-permute-start(bf16[384,2048]{1,0:T(8,128)(2,1)} %shard_map.50.s_ref), channel_id=1, source_target_pairs={{16,0},{17,1},{18,2},{19,3},{20,4},{21,5},{22,6},{23,7},{24,8},{25... | collective-permute-start | bytes 4718600 | tf_op jit(solution)/shard_map/ppermute | solution.py:30
  (27 other events, 285.9 us)

commit v2 on v1

v2 whole, which is shorter than its diff:
```python
import jax
import jax.numpy as jnp
from jax import lax
from jax.experimental import pallas as pl
from jax.experimental.pallas import tpu as pltpu
from jax.sharding import PartitionSpec as P


AXES = ("dp", "vocab")
Y, X, C, H, Z = 4, 2, 2, 2, 8
LANES = 128
ROWS_SUM = 48
ROWS_OUT = 80
F32, BF16 = jnp.float32, jnp.bfloat16


def device(y, x, c, h, z):
    return ((((y % Y) * X + x) * C + c) * H + h) * Z + z % Z


def fetch(value, source):
    pairs = [
        (device(*source(y, x, c, h, z)), device(y, x, c, h, z))
        for y in range(Y)
        for x in range(X)
        for c in range(C)
        for h in range(H)
        for z in range(Z)
    ]
    return lax.ppermute(value, AXES, pairs)


def from_y(value, dy):
    return fetch(value, lambda y, x, c, h, z: (y + dy, x, c, h, z))


def from_x(value):
    return fetch(value, lambda y, x, c, h, z: (y, x ^ 1, c, h, z))


def from_z(value, dz):
    return fetch(value, lambda y, x, c, h, z: (y, x, c, h, z + dz))


def from_core(value):
    return fetch(value, lambda y, x, c, h, z: (y, x, c ^ 1, h, z))


def encode(values):
    peak = jnp.max(jnp.abs(values), axis=-1, keepdims=True)
    power = jnp.ceil(jnp.log2(jnp.maximum(peak, 1e-30) * (1.0 / 32000.0)))
    codes = jnp.round(values * jnp.exp2(-power)).astype(jnp.int32).astype(jnp.int16)
    tail = jnp.broadcast_to(power, (values.shape[0], LANES)).astype(jnp.int32)
    return codes, tail.astype(jnp.int16)


def put(ref, index, values):
    width = values.shape[-1]
    codes, tail = encode(values)
    ref[(*index, slice(0, width))] = codes
    ref[(*index, slice(width, width + LANES))] = tail


def get(ref, index):
    width = ref.shape[-1] - LANES
    power = ref[(*index, slice(width, width + LANES))].astype(jnp.int32).astype(F32)
    codes = ref[(*index, slice(0, width))].astype(jnp.int32).astype(F32)
    return codes * jnp.exp2(power[:, :1])


def rows_of(pieces, flag, dy, dx):
    if dy != 2:
        return pieces[dy, dx][...]
    far = jnp.concatenate([f[...] for f in pieces["far"]], axis=0)
    return jnp.where(flag == dx, pieces["near"][...], far)


def full(shape):
    return pl.BlockSpec(shape, lambda j: (0,) * len(shape))


STEPS = 4
NEAR = ((0, 0), (1, 0), (2, 0), (3, 0), (0, 1))
FAR = ((1, 1), (2, 1), (3, 1))


def partial_call(flag, pieces, keys, weights, out_shape, out_specs, finish_step):
    w0, w1 = weights
    depth, width = w0.shape
    block = width // STEPS
    names = [k for k in pieces if k in keys or (k in ("near", "far") and any(q[0] == 2 for q in keys))]
    flat = []
    for k in names:
        flat += pieces[k] if k == "far" else [pieces[k]]
    rows = pieces[1, 1].shape[0]
    total = len(keys) * rows

    def body(flag_ref, *refs):
        refs = list(refs)
        by = {}
        for k in names:
            by[k] = [refs.pop(0), refs.pop(0)] if k == "far" else refs.pop(0)
        w0_ref, w1_ref = refs[:2]
        outs, left, acc = refs[2:-2], refs[-2], refs[-1]
        j = pl.program_id(0)

        @pl.when(j == 0)
        def _():
            for n, (dy, dx) in enumerate(keys):
                left[n * rows : (n + 1) * rows] = rows_of(by, flag_ref[0], dy, dx)

        value = jnp.dot(left[:, :depth], w0_ref[...], preferred_element_type=F32)
        value += jnp.dot(left[:, depth:], w1_ref[...], preferred_element_type=F32)
        finish_step(j, value, outs, acc)

    return pl.pallas_call(
        body,
        grid=(STEPS,),
        in_specs=[pl.BlockSpec(memory_space=pltpu.SMEM)]
        + [full(v.shape) for v in flat]
        + [pl.BlockSpec((depth, block), lambda j: (0, j))] * 2,
        out_specs=out_specs,
        out_shape=out_shape,
        scratch_shapes=[
            pltpu.VMEM((total, 2 * depth), BF16),
            pltpu.VMEM((STEPS, total, block), F32),
        ],
    )(flag, *flat, w0, w1)


def sends(flag, pieces, weights, rows, width):
    a = ROWS_SUM
    shapes = [(3, a, width + LANES)] + [(rows - a, width + LANES)] * 3

    def step(j, value, outs, acc):
        acc[j] = value

        @pl.when(j == STEPS - 1)
        def _():
            for k in range(3):
                whole = jnp.concatenate(
                    [acc[s, k * rows : (k + 1) * rows] for s in range(STEPS)], axis=1
                )
                put(outs[0], (k, slice(None)), whole[:a])
                put(outs[1 + k], (slice(None),), whole[a:])

    return partial_call(
        flag, pieces, FAR, weights,
        [jax.ShapeDtypeStruct(s, jnp.int16) for s in shapes],
        [full(s) for s in shapes], step,
    )


KEPT = ((1, 0), (2, 0), (3, 0), (0, 1), (0, 0))


def keeps(flag, pieces, weights, rows, width):
    total = len(KEPT) * rows

    def step(j, value, outs, acc):
        outs[0][...] = value

    return partial_call(
        flag, pieces, KEPT, weights,
        jax.ShapeDtypeStruct((total, width), F32),
        pl.BlockSpec((total, width // STEPS), lambda j: (0, j)), step,
    )


def combine_y(kept, received, rows, width):
    a = ROWS_SUM

    def body(kept_ref, got, o1, o2, o3):
        k = pl.program_id(0)
        first = kept_ref[:a] + get(got, (0, slice(None)))
        for i, out in enumerate((o1, o2, o3)):

            @pl.when(k == i)
            def _(out=out):
                put(out, (slice(0, a),), first)
                put(out, (slice(a, rows),), kept_ref[a:])

    shape = (rows, width + LANES)
    return pl.pallas_call(
        body,
        grid=(3,),
        in_specs=[
            pl.BlockSpec((rows, width), lambda k: (k, 0)),
            pl.BlockSpec((1, a, width + LANES), lambda k: (k, 0, 0)),
        ],
        out_specs=[full(shape)] * 3,
        out_shape=[jax.ShapeDtypeStruct(shape, jnp.int16)] * 3,
        name="combine_y",
    )(kept, received)


def combine_x(kept, received, rows, width):
    a = ROWS_SUM

    def body(kept_ref, g1, g2, g3, out, token):
        last = kept_ref[a:] + get(g1, (slice(None),)) + get(g2, (slice(None),)) + get(g3, (slice(None),))
        put(out, (slice(0, a),), kept_ref[:a])
        put(out, (slice(a, rows),), last)
        token[...] = jnp.zeros((8, LANES), jnp.int32)

    shape = (rows, width + LANES)
    return pl.pallas_call(
        body,
        grid=(1,),
        in_specs=[pl.BlockSpec((rows, width), lambda k: (3, 0))]
        + [full(received[0].shape)] * 3,
        out_specs=[full(shape), full((8, LANES))],
        out_shape=[
            jax.ShapeDtypeStruct(shape, jnp.int16),
            jax.ShapeDtypeStruct((8, LANES), jnp.int32),
        ],
        name="combine_x",
    )(kept, *received)


def upright(line):
    return jnp.transpose(jnp.broadcast_to(line, (LANES, LANES)))


def finish(kept, received, ids, place, rows, width):
    def body(place_ref, kept_ref, g1, g2, g3, g4, ids_ref, e_ref, stat_ref):
        logits = kept_ref[...]
        for g in (g1, g2, g3, g4):
            logits = logits + get(g, (slice(None),))
        columns = lax.broadcasted_iota(jnp.int32, (rows, width), 1) + place_ref[1]
        label = upright(ids_ref[pl.ds(place_ref[0], 1), :])
        hit = columns.astype(F32) == label[:, :1]
        peak = jnp.max(logits, axis=1, keepdims=True)
        raised = jnp.exp(logits - peak)
        total = jnp.sum(raised, axis=1, keepdims=True)
        picked = jnp.sum(jnp.where(hit, logits, 0.0), axis=1, keepdims=True)
        e_ref[...] = raised.astype(BF16)
        lines = [jnp.transpose(jnp.broadcast_to(v, (rows, LANES)))[:1] for v in (peak, total, picked)]
        lines = jnp.concatenate(lines + [jnp.zeros((5, rows), F32)], axis=0)
        for k in range(16):
            stat_ref[k] = lines

    return pl.pallas_call(
        body,
        grid=(1,),
        in_specs=[
            pl.BlockSpec(memory_space=pltpu.SMEM),
            pl.BlockSpec((rows, width), lambda k: (4, 0)),
        ]
        + [full(received[0].shape)] * 4
        + [full(ids.shape)],
        out_specs=[full((rows, width)), full((16, 8, rows))],
        out_shape=[
            jax.ShapeDtypeStruct((rows, width), BF16),
            jax.ShapeDtypeStruct((16, 8, rows), F32),
        ],
        name="finish",
    )(place, kept, *received, ids)


def settle(every, stats):
    def body(every_ref, own_ref, loss_ref, factor_ref):
        peaks, totals, picks = (every_ref[:, k] for k in range(3))
        top = jnp.max(peaks, axis=0, keepdims=True)
        total = jnp.sum(totals * jnp.exp(peaks - top), axis=0, keepdims=True)
        picked = jnp.sum(picks, axis=0, keepdims=True)
        loss_ref[...] = top + jnp.log(total) - picked
        factor = jnp.exp(own_ref[0, :1] - top) / total
        factor_ref[...] = jnp.broadcast_to(factor[None], factor_ref.shape)

    rows = every.shape[-1]
    return pl.pallas_call(
        body,
        out_shape=[
            jax.ShapeDtypeStruct((1, rows), F32),
            jax.ShapeDtypeStruct(every.shape, F32),
        ],
        name="settle",
    )(every, stats)


def slopes(pieces, spans, factors, ids, place, width):
    sizes = [p.shape[0] for p in pieces]
    total = sum(sizes)

    def body(place_ref, *refs):
        ins, factor_ref, ids_ref, out = refs[:-3], refs[-3], refs[-2], refs[-1]
        columns = lax.broadcasted_iota(jnp.int32, (max(sizes), width), 1) + place_ref[1]
        columns = columns.astype(F32)
        at = 0
        for ref, n, (k, a, b) in zip(ins, sizes, spans):
            owner = place_ref[2 + k]
            scale = upright(factor_ref[owner, :1])[a:b, :1]
            label = upright(ids_ref[pl.ds(owner, 1), :])[a:b, :1]
            value = ref[...].astype(F32) * scale
            value = value - jnp.where(columns[:n] == label, 1.0, 0.0)
            out[at : at + n] = value.astype(BF16)
            at += n

    return pl.pallas_call(
        body,
        grid=(1,),
        in_specs=[pl.BlockSpec(memory_space=pltpu.SMEM)]
        + [full(p.shape) for p in pieces]
        + [full(factors.shape), full(ids.shape)],
        out_specs=full((total, width)),
        out_shape=jax.ShapeDtypeStruct((total, width), BF16),
    )(place, *pieces, factors, ids)


def turned(flag, pieces, rows, depth):
    g = ROWS_OUT
    names = list(pieces)
    flat = []
    for k in names:
        flat += pieces[k] if k == "far" else [pieces[k]]

    def body(flag_ref, *refs):
        refs = list(refs)
        by = {}
        for k in names:
            by[k] = [refs.pop(0), refs.pop(0)] if k == "far" else refs.pop(0)
        mine, theirs = refs
        near = [rows_of(by, flag_ref[0], dy, dx) for dy, dx in NEAR]
        far = [rows_of(by, flag_ref[0], dy, dx) for dy, dx in FAR]
        far = jnp.concatenate([f[:g] for f in far] + [f[g:] for f in far], axis=0)
        parts = near + [far[k * rows : (k + 1) * rows] for k in range(3)]
        for k, part in enumerate(parts):
            flipped = jnp.transpose(part)
            mine[:, k * rows : (k + 1) * rows] = flipped[:depth]
            theirs[:, k * rows : (k + 1) * rows] = flipped[depth:]

    shape = (depth, 8 * rows)
    return pl.pallas_call(
        body,
        grid=(1,),
        in_specs=[pl.BlockSpec(memory_space=pltpu.SMEM)] + [full(v.shape) for v in flat],
        out_specs=[full(shape)] * 2,
        out_shape=[jax.ShapeDtypeStruct(shape, BF16)] * 2,
        name="turned",
    )(flag, *flat)


def gradient(mine, theirs, near, near_other, far, far_other):
    depth = mine.shape[0]
    n, width = near.shape
    block = width // STEPS

    def body(m_ref, t_ref, a_ref, b_ref, c_ref, d_ref, out):
        value = jnp.dot(m_ref[:, :n], a_ref[...], preferred_element_type=F32)
        value += jnp.dot(t_ref[:, :n], b_ref[...], preferred_element_type=F32)
        value += jnp.dot(m_ref[:, n:], c_ref[...], preferred_element_type=F32)
        value += jnp.dot(t_ref[:, n:], d_ref[...], preferred_element_type=F32)
        out[...] = value

    col = lambda r: pl.BlockSpec((r, block), lambda j: (0, j))
    m = far.shape[0]
    return pl.pallas_call(
        body,
        grid=(STEPS,),
        in_specs=[full(mine.shape)] * 2 + [col(n)] * 2 + [col(m)] * 2,
        out_specs=col(depth),
        out_shape=jax.ShapeDtypeStruct((depth, width), F32),
        name="gradient",
    )(mine, theirs, near, near_other, far, far_other)


def per_device(hidden, head_weight, targets):
    here = lax.axis_index("dp")
    block_index = lax.axis_index("vocab")
    c = here % C
    x = (here // C) % X
    y = here // (C * X)
    odd = block_index % 2
    rows = hidden.shape[0]
    depth, width = head_weight.shape

    def columns_for(dy, dx):
        chip = ((y - dy) % Y) * X + (x ^ dx)
        own = lax.dynamic_slice_in_dim(hidden, (chip * C + c) * depth, depth, 1)
        other = lax.dynamic_slice_in_dim(hidden, (chip * C + 1 - c) * depth, depth, 1)
        return jnp.concatenate([own, other], axis=1)

    def two_hop(y, x, c, h, z):
        return (y + 2, x ^ (z % 2), c, h, z)

    def outside(dy):
        return lambda y, x, c, h, z: (y + dy, x ^ 1, c, h ^ 1, z)

    half = rows // 2
    near2 = fetch(columns_for(2, odd), two_hop)
    pieces = {
        "near": near2,
        "far": [from_z(near2[:half], -1), from_z(near2[half:], 1)],
        (1, 1): fetch(columns_for(1, 1), outside(1)),
        (3, 1): fetch(columns_for(3, 1), outside(3)),
        (1, 0): from_y(columns_for(1, 0), 1),
        (3, 0): from_y(columns_for(3, 0), 3),
        (0, 1): from_x(columns_for(0, 1)),
        (0, 0): columns_for(0, 0),
    }
    flag = odd.reshape(1).astype(jnp.int32)
    weights = (head_weight, from_core(head_weight))

    to_x, *to_y = sends(flag, pieces, weights, rows, width)
    got_x = from_x(to_x)
    got_y = [from_y(v, -dy) for v, dy in zip(to_y, (1, 2, 3))]
    kept = keeps(flag, pieces, weights, rows, width)
    send_y = combine_y(kept, got_x, rows, width)
    send_x, token = combine_x(kept, got_y, rows, width)
    received = [from_x(send_x)]
    received += [from_y(v, -dy) for v, dy in zip(send_y, (1, 2, 3))]

    token = token[0, 0]
    mine, sent = turned(flag + token, pieces, rows, depth)
    theirs = from_core(sent)
    ids = (targets + token).astype(F32).reshape(16, rows)
    owners = [(((y + dy) % Y) * X + (x ^ dx)) * C + c for dy, dx in NEAR + FAR]
    place = jnp.stack([here, block_index * width, *owners]).astype(jnp.int32)
    raised, stats = finish(kept, received, ids, place, rows, width)

    g = ROWS_OUT
    side_x = from_x(raised)
    along = {dy: from_y(raised, dy) for dy in (2, 1, 3)}
    far_y = {dy: from_y(side_x[g:], dy) for dy in (2, 1, 3)}
    far_x = {dy: from_x(along[dy][:g]) for dy in (1, 3, 2)}

    every = lax.all_to_all(stats, "vocab", 0, 0, tiled=True)
    loss, factor = settle(every, stats)
    factors = lax.all_to_all(factor, "dp", 0, 0, tiled=True)

    near_spans = [(k, 0, rows) for k in range(5)]
    far_spans = [(5 + k, 0, g) for k in range(3)] + [(5 + k, g, rows) for k in range(3)]
    slope_near = slopes(
        [raised, along[1], along[2], along[3], side_x],
        near_spans, factors, ids, place, width,
    )
    slope_far = slopes(
        [far_x[d] for d in (1, 2, 3)] + [far_y[d] for d in (1, 2, 3)],
        far_spans, factors, ids, place, width,
    )
    near_other = from_core(slope_near)
    far_other = from_core(slope_far)
    grad = gradient(mine, theirs, slope_near, near_other, slope_far, far_other)
    return (loss.reshape(rows), grad)


def solution(mesh):
    in_specs = (P("dp", None), P("dp", "vocab"), P())
    out_specs = (P("dp"), P("dp", "vocab"))

    return jax.shard_map(
        per_device, mesh=mesh, in_specs=in_specs, out_specs=out_specs, check_vma=False
    )
```

time: 326 us -> 218 us (0.67)
  Pallas kernels: 115 us -> 53.5 us
  local copies, waits for them, and re-layouts: 59.4 us -> 21.4 us
  blocking collectives: 0 us -> 34 us
  starting transfers between devices: 60.5 us -> 43.4 us
  waiting for transfers between devices: 73.2 us -> 57.1 us
  other arithmetic: 13.8 us -> 5.74 us
    pallas_call x5, Pallas kernels: 96.6 us -> 35 us  [the longest x2 16.3 us: partial_call(): pl.pallas_call(body, grid=(STEPS,), in_specs=[pl.BlockSpec(memory_space=p...]
    all_to_all x0 -> x2, blocking collectives: none -> 34 us  [the longest x1 21.1 us: per_device(): every = lax.all_to_all(stats, 'vocab', 0, 0, tiled=True)]
    ppermute x8 -> x0, local copies, waits for them, and re-layouts: 14.2 us -> none  [fetch(): return lax.ppermute(value, AXES, pairs)]
    all_to_all x2 -> x0, starting transfers between devices: 12.1 us -> none  [the longest x1 7.04 us: per_device(): lax.all_to_all(jnp.broadcast_to(factor[None], (16, rows)), 'dp', 0, 0, ti...]
    pallas_call x5 -> x0, local copies, waits for them, and re-layouts: 9.62 us -> none  [pieces_of(): pl.pallas_call(body, in_specs=[pl.BlockSpec(memory_space=pltpu.SMEM), pl....]
    ppermute x31 -> x30, waiting for transfers between devices: 65.5 us -> 57.1 us  [fetch(): return lax.ppermute(value, AXES, pairs)]
    all_to_all x2 -> x0, waiting for transfers between devices: 7.63 us -> none  [the longest x1 7.62 us: per_device(): lax.all_to_all(jnp.broadcast_to(stats[None], (16, *stats.shape)), 'vocab'...]
    unnamed x5 -> x0, other arithmetic: 6.33 us -> none
  transfers between devices with their start and end apart: 33 -> 30, of which waited for: 14 -> 10; matrix products, arithmetic and copies ran while one was open for 20% -> 7% of each run, Pallas kernels for 25% -> 15%
where the time goes in v2:
time: 218 us; the launch traced here: 217 us
  waiting for transfers between devices  57.1 us (26%)
  Pallas kernels  53.5 us (25%)
  starting transfers between devices  43.4 us (20%)
  blocking collectives  34 us (16%)
  local copies, waits for them, and re-layouts  21.4 us (10%)
  other arithmetic  5.74 us (3%)
    ppermute x30, waiting for transfers between devices, fetch(): return lax.ppermute(value, AXES, pairs)  57.1 us
    ppermute x30, starting transfers between devices, fetch(): return lax.ppermute(value, AXES, pairs)  43.4 us
    all_to_all x1, blocking collectives, per_device(): every = lax.all_to_all(stats, 'vocab', 0, 0, tiled=True)  21.1 us
    pallas_call x2, Pallas kernels, partial_call(): pl.pallas_call(body, grid=(STEPS,), in_specs=[pl.BlockSpec(memory_space=p...  16.3 us
    all_to_all x1, blocking collectives, per_device(): factors = lax.all_to_all(factor, 'dp', 0, 0, tiled=True)  13 us
    pallas_call x1, Pallas kernels, gradient(): pl.pallas_call(body, grid=(STEPS,), in_specs=[full(mine.shape)] * 2 + [co...  12.8 us
    unnamed x48, local copies, waits for them, and re-layouts  12.1 us
    pallas_call x2, Pallas kernels, slopes(): pl.pallas_call(body, grid=(1,), in_specs=[pl.BlockSpec(memory_space=pltpu...  7.8 us
  transfers between devices with their start and end apart: 30, of which 10 were waited for; matrix products, arithmetic and copies ran while one was open for 7% of the time, Pallas kernels for 15%

profile of v2, /device:TPU:1, one launch (start us, length us, event | category | flops | bytes accessed | tf_op | source)
XLA Modules:
  0.0 216.7 jit_solution(15238448821577619332)
XLA Ops:
  0.6 3.3 %collective-permute-start.6 = (bf16[768,2048]{1,0:T(8,128)(2,1)}, bf16[768,2048]{1,0:T(8,128)(2,1)S(1)}, u32[]{:S(2)}, u32[]{:S(2)}) collective-permute-start(bf16[768,2048]{1,0:T(8,128)(2,1)} %refs_5_.1), channel_id=1, source_target_pairs={{16,0},{17,1},{18,2},{19,3},{20,4},{21,5},{22,6},{23,7},{24,8},{25... | collective-permute-start | bytes 9437192 | tf_op jit(solution)/shard_map/ppermute | solution.py:30
  3.9 2.8 %constant_dynamic-slice_fusion.1 = (bf16[128,768]{1,0:T(8,128)(2,1)S(1)}, bf16[128,768]{1,0:T(8,128)(2,1)S(1)}, bf16[128,768]{1,0:T(8,128)(2,1)S(1)}, bf16[128,7...) fusion(bf16[128,12288]{1,0:T(8,128)(2,1)} %param.3, ...), kind=kLoop, calls=%fused_computation.9 | loop fusion | bytes 5505080 | tf_op jit(solution)/shard_map/dynamic_slice | solution.py:380
  9.6 2.3 %collective-permute-start.7 = (bf16[128,1536]{1,0:T(8,128)(2,1)S(1)}, bf16[128,1536]{1,0:T(8,128)(2,1)S(1)}, u32[]{:S(2)}, u32[]{:S(2)}) collective-permute-start(bf16[128,1536]{1,0:T(8,128)(2,1)S(1)} %pad_maximum_fusion.5), channel_id=1, source_target_pairs={{104,0},{105,1},{106,2},{107,3},{108,4},{109,5},{110,6},{111,7},{9... | collective-permute-start | bytes 1179656 | tf_op jit(solution)/shard_map/ppermute | solution.py:30
  13.4 5.4 %collective-permute-done.refs_0_ = bf16[128,1536]{1,0:T(8,128)(2,1)S(1)} collective-permute-done((bf16[128,1536]{1,0:T(8,128)(2,1)S(1)}, bf16[128,1536]{1,0:T(8,128)(2,1)S(1)}, u32[]{:S(2)}, u32[]{:S(2)}) %collective-permute-start) | collective-permute-done | bytes 393248 | tf_op jit(solution)/shard_map/ppermute | solution.py:30
  18.8 4.8 %collective-permute-start.2 = (bf16[64,1536]{1,0:T(8,128)(2,1)S(1)}, bf16[64,1536]{1,0:T(8,128)(2,1)S(1)}, u32[]{:S(2)}, u32[]{:S(2)}) collective-permute-start(bf16[64,1536]{1,0:T(8,128)(2,1)S(1)} %get-tuple-element.46), channel_id=1, source_target_pairs={{1,0},{2,1},{3,2},{4,3},{5,4},{6,5},{7,6},{0,7},{9,8},{10,9},{11,1... | collective-permute-start | bytes 589832 | tf_op jit(solution)/shard_map/ppermute | solution.py:30
  24.4 4.0 %collective-permute-start.1 = (bf16[64,1536]{1,0:T(8,128)(2,1)S(1)}, bf16[64,1536]{1,0:T(8,128)(2,1)S(1)}, u32[]{:S(2)}, u32[]{:S(2)}) collective-permute-start(bf16[64,1536]{1,0:T(8,128)(2,1)S(1)} %get-tuple-element.47), channel_id=1, source_target_pairs={{7,0},{0,1},{1,2},{2,3},{3,4},{4,5},{5,6},{6,7},{15,8},{8,9},{9,10... | collective-permute-start | bytes 589832 | tf_op jit(solution)/shard_map/ppermute | solution.py:30
  31.4 4.1 %collective-permute-done.1.refs_1_ = bf16[64,1536]{1,0:T(8,128)(2,1)S(1)} collective-permute-done((bf16[64,1536]{1,0:T(8,128)(2,1)S(1)}, bf16[64,1536]{1,0:T(8,128)(2,1)S(1)}, u32[]{:S(2)}, u32[]{:S(2)}) %collective-permute-start.1) | collective-permute-done | bytes 196640 | tf_op jit(solution)/shard_map/ppermute | solution.py:30
  37.8 7.4 %shard_map.51 = (s16[3,48,2176]{2,1,0:T(8,128)(2,1)}, s16[80,2176]{1,0:T(8,128)(2,1)}, s16[80,2176]{1,0:T(8,128)(2,1)}, s16[80,2176]{1,0:T(8,128)(2,1)}) custom-call(s32[1]{0:T(128)} %bitcast.10.flag_ref, bf16[128,1536]{1,0:T(8,128)(2,1)} %copy-done.1, bf16[64,1536]{1,0:T(8,128)(2,1)} %copy-done.4, bf16[64,1536]{1,0:T(8,128)(2,1)} %copy-done.3, ...), custom_call_target="tpu_custom_call" | custom-call | tf_op jit(solution)/shard_map/pallas_call | solution.py:116
  49.4 2.7 %collective-permute-start.10 = (s16[80,2176]{1,0:T(8,128)(2,1)}, s16[80,2176]{1,0:T(8,128)(2,1)S(1)}, u32[]{:S(2)}, u32[]{:S(2)}) collective-permute-start(s16[80,2176]{1,0:T(8,128)(2,1)} %get-tuple-element.18), channel_id=1, source_target_pairs={{128,0},{129,1},{130,2},{131,3},{132,4},{133,5},{134,6},{135,7},{1... | collective-permute-start | bytes 1044488 | tf_op jit(solution)/shard_map/ppermute | solution.py:30
  52.1 1.8 pad_maximum_fusion.4.refs_6_.refs_8_
  53.9 11.9 %collective-permute-done.5.refs_5_.refs_7_ = bf16[128,1536]{1,0:T(8,128)(2,1)S(1)} collective-permute-done((bf16[128,1536]{1,0:T(8,128)(2,1)S(1)}, bf16[128,1536]{1,0:T(8,128)(2,1)S(1)}, u32[]{:S(2)}, u32[]{:S(2)}) %collective-permute-start.5) | collective-permute-done | bytes 393248 | tf_op jit(solution)/shard_map/ppermute | solution.py:30
  66.6 8.8 %shard_map.50.kept_ref = f32[640,2048]{1,0:T(8,128)} custom-call(s32[1]{0:T(128)} %bitcast.10.flag_ref, bf16[128,1536]{1,0:T(8,128)(2,1)} %copy-done.1, bf16[64,1536]{1,0:T(8,128)(2,1)} %copy-done.4, bf16[64,1536]{1,0:T(8,128)(2,1)} %copy-done.3, bf16[128,1536]{1,0:T(8,128)(2,1)} %collective-permute-done.3.refs_3_.refs_5_, ...), custom_call_target="tpu_custom_call" | custom-call | tf_op jit(solution)/shard_map/pallas_call | solution.py:116
  77.0 2.7 %combine_x.1 = (s16[128,2176]{1,0:T(8,128)(2,1)}, s32[8,128]{1,0:T(8,128)}) custom-call(f32[640,2048]{1,0:T(8,128)} %shard_map.50.kept_ref, s16[80,2176]{1,0:T(8,128)(2,1)} %copy-done.18, s16[80,2176]{1,0:T(8,128)(2,1)} %copy-done.19, s16[80,2176]{1,0:T(8,128)(2,1)} %copy-done.20), custom_call_target="tpu_custom_call" | custom-call | tf_op jit(solution)/shard_map/combine_x/pallas_call | solution.py:207
  79.8 1.7 collective-permute-start.12
  82.3 4.4 %combine_y.1 = (s16[128,2176]{1,0:T(8,128)(2,1)}, s16[128,2176]{1,0:T(8,128)(2,1)}, s16[128,2176]{1,0:T(8,128)(2,1)}) custom-call(f32[640,2048]{1,0:T(8,128)} %shard_map.50.kept_ref, s16[3,48,2176]{2,1,0:T(8,128)(2,1)} %copy-done.13), custom_call_target="tpu_custom_call" | custom-call | tf_op jit(solution)/shard_map/combine_y/pallas_call | solution.py:184
  88.0 3.0 %collective-permute-start.15 = (s16[128,2176]{1,0:T(8,128)(2,1)}, s16[128,2176]{1,0:T(8,128)(2,1)S(1)}, u32[]{:S(2)}, u32[]{:S(2)}) collective-permute-start(s16[128,2176]{1,0:T(8,128)(2,1)} %get-tuple-element.23), channel_id=1, source_target_pairs={{128,0},{129,1},{130,2},{131,3},{132,4},{133,5},{134,6},{135,7},{1... | collective-permute-start | bytes 1671176 | tf_op jit(solution)/shard_map/ppermute | solution.py:30
  94.1 4.4 %collective-permute-done.14.g2 = s16[128,2176]{1,0:T(8,128)(2,1)S(1)} collective-permute-done((s16[128,2176]{1,0:T(8,128)(2,1)}, s16[128,2176]{1,0:T(8,128)(2,1)S(1)}, u32[]{:S(2)}, u32[]{:S(2)}) %collective-permute-start.14) | collective-permute-done | bytes 557088 | tf_op jit(solution)/shard_map/ppermute | solution.py:30
  98.5 13.0 %collective-permute-done.15.g3 = s16[128,2176]{1,0:T(8,128)(2,1)S(1)} collective-permute-done((s16[128,2176]{1,0:T(8,128)(2,1)}, s16[128,2176]{1,0:T(8,128)(2,1)S(1)}, u32[]{:S(2)}, u32[]{:S(2)}) %collective-permute-start.15) | collective-permute-done | bytes 557088 | tf_op jit(solution)/shard_map/ppermute | solution.py:30
  111.5 3.2 %collective-permute-done.16.g4 = s16[128,2176]{1,0:T(8,128)(2,1)S(1)} collective-permute-done((s16[128,2176]{1,0:T(8,128)(2,1)}, s16[128,2176]{1,0:T(8,128)(2,1)S(1)}, u32[]{:S(2)}, u32[]{:S(2)}) %collective-permute-start.16) | collective-permute-done | bytes 557088 | tf_op jit(solution)/shard_map/ppermute | solution.py:30
  115.5 3.6 %finish.1 = (bf16[128,2048]{1,0:T(8,128)(2,1)}, f32[16,8,128]{2,1,0:T(8,128)}) custom-call(s32[10]{0:T(128)} %stack.43.place_ref, f32[640,2048]{1,0:T(8,128)} %shard_map.50.kept_ref, s16[128,2176]{1,0:T(8,128)(2,1)} %copy-done.14, s16[128,2176]{1,0:T(8,128)(2,1)} %copy-done.15, s16[128,2176]{1,0:T(8,128)(2,1)} %copy-done.16, s16[128,2176]{1,0:T(8,128)(2,1)} %copy-done.17, ...), custom_call_target="tpu_custom_call" | custom-call | tf_op jit(solution)/shard_map/finish/pallas_call | solution.py:243
  119.4 1.9 collective-permute-start.20
  121.3 2.6 %collective-permute-start.19 = (bf16[128,2048]{1,0:T(8,128)(2,1)}, bf16[128,2048]{1,0:T(8,128)(2,1)S(1)}, u32[]{:S(2)}, u32[]{:S(2)}) collective-permute-start(bf16[128,2048]{1,0:T(8,128)(2,1)} %get-tuple-element.30.refs_0_), channel_id=1, source_target_pairs={{128,0},{129,1},{130,2},{131,3},{132,4},{133,5},{134,6},{135,7},{1... | collective-permute-start | bytes 1572872 | tf_op jit(solution)/shard_map/ppermute | solution.py:30
  123.9 21.1 %all_to_all.10.every_ref = f32[16,8,128]{2,1,0:T(8,128)} all-to-all(f32[16,8,128]{2,1,0:T(8,128)} %get-tuple-element.26.own_ref), channel_id=1, replica_groups=mesh['dp'=16,'vocab'=16] {'vocab'}, dimensions={0} | all-to-all | bytes 131072 | tf_op jit(solution)/shard_map/all_to_all | solution.py:428
  146.5 13.0 %all_to_all.11.refs_5_.refs_6_ = f32[16,8,128]{2,1,0:T(8,128)} all-to-all(f32[16,8,128]{2,1,0:T(8,128)} %get-tuple-element.31), channel_id=1, replica_groups=mesh['dp'=16,'vocab'=16] {'dp'}, dimensions={0} | all-to-all | bytes 131072 | tf_op jit(solution)/shard_map/all_to_all | solution.py:430
  161.4 4.4 %shard_map.52.a_ref = bf16[640,2048]{1,0:T(8,128)(2,1)} custom-call(s32[10]{0:T(128)} %stack.43.place_ref, bf16[128,2048]{1,0:T(8,128)(2,1)} %get-tuple-element.30.refs_0_, bf16[128,2048]{1,0:T(8,128)(2,1)} %copy-done.9, bf16[128,2048]{1,0:T(8,128)(2,1)} %copy-done.10, bf16[128,2048]{1,0:T(8,128)(2,1)} %copy-done.11, bf16[128,2048]{1,0:T(8,128)(2,1)} %copy-done.12, ...), custom_call_target="tpu_custom_call" | custom-call | tf_op jit(solution)/shard_map/pallas_call | solution.py:300
  174.6 4.5 %collective-permute-done.28.refs_5_ = bf16[48,2048]{1,0:T(8,128)(2,1)S(1)} collective-permute-done((bf16[48,2048]{1,0:T(8,128)(2,1)S(1)}, bf16[48,2048]{1,0:T(8,128)(2,1)S(1)}, u32[]{:S(2)}, u32[]{:S(2)}) %collective-permute-start.28) | collective-permute-done | bytes 196640 | tf_op jit(solution)/shard_map/ppermute | solution.py:30
  180.5 4.5 %turned.1 = (bf16[768,1024]{1,0:T(8,128)(2,1)}, bf16[768,1024]{1,0:T(8,128)(2,1)}) custom-call(s32[1]{0:T(128)S(6)} %add.272.flag_ref, bf16[128,1536]{1,0:T(8,128)(2,1)} %copy-done.1, bf16[64,1536]{1,0:T(8,128)(2,1)} %copy-done.4, bf16[64,1536]{1,0:T(8,128)(2,1)} %copy-done.3, bf16[128,1536]{1,0:T(8,128)(2,1)} %copy-done.5, bf16[128,1536]{1,0:T(8,128)(2,1)} %copy-done.6, ...), custom_call_target="tpu_custom_call" | custom-call | tf_op jit(solution)/shard_map/turned/pallas_call | solution.py:334
  185.0 1.8 collective-permute-start.17
  186.8 6.3 %collective-permute-done.23.refs_0_ = bf16[80,2048]{1,0:T(8,128)(2,1)} collective-permute-done((bf16[80,2048]{1,0:T(8,128)(2,1)}, bf16[80,2048]{1,0:T(8,128)(2,1)}, u32[]{:S(2)}, u32[]{:S(2)}) %collective-permute-start.23) | collective-permute-done | bytes 327712 | tf_op jit(solution)/shard_map/ppermute | solution.py:30
  193.1 3.4 %shard_map.53.c_ref = bf16[384,2048]{1,0:T(8,128)(2,1)} custom-call(s32[10]{0:T(128)} %stack.43.place_ref, bf16[80,2048]{1,0:T(8,128)(2,1)} %collective-permute-done.23.refs_0_, bf16[80,2048]{1,0:T(8,128)(2,1)} %collective-permute-done.24.refs_1_, bf16[80,2048]{1,0:T(8,128)(2,1)} %collective-permute-done.25.refs_2_, ...), custom_call_target="tpu_custom_call" | custom-call | tf_op jit(solution)/shard_map/pallas_call | solution.py:300
  198.1 3.2 %collective-permute-done.29.d_ref = bf16[384,2048]{1,0:T(8,128)(2,1)S(1)} collective-permute-done((bf16[384,2048]{1,0:T(8,128)(2,1)}, bf16[384,2048]{1,0:T(8,128)(2,1)S(1)}, u32[]{:S(2)}, u32[]{:S(2)}) %collective-permute-start.29) | collective-permute-done | bytes 1572896 | tf_op jit(solution)/shard_map/ppermute | solution.py:30
  203.9 12.8 %gradient.1 = f32[768,2048]{1,0:T(8,128)} custom-call(bf16[768,1024]{1,0:T(8,128)(2,1)} %get-tuple-element.28.m_ref, bf16[768,1024]{1,0:T(8,128)(2,1)} %collective-permute-done.17.t_ref, bf16[640,2048]{1,0:T(8,128)(2,1)} %shard_map.52.a_ref, bf16[640,2048]{1,0:T(8,128)(2,1)} %copy-done.2, bf16[384,2048]{1,0:T(8,128)(2,1)} %shard_map.53.c_ref, ...), custom_call_target="tpu_custom_call" | custom-call | tf_op jit(solution)/shard_map/gradient/pallas_call | solution.py:358
  (104 shorter events, 40.5 us)
Async XLA Ops:
  0.6 34.9 %collective-permute-start.6 = (bf16[768,2048]{1,0:T(8,128)(2,1)}, bf16[768,2048]{1,0:T(8,128)(2,1)S(1)}, u32[]{:S(2)}, u32[]{:S(2)}) collective-permute-start(bf16[768,2048]{1,0:T(8,128)(2,1)} %refs_5_.1), channel_id=1, source_target_pairs={{16,0},{17,1},{18,2},{19,3},{20,4},{21,5},{22,6},{23,7},{24,8},{25... | collective-permute-start | bytes 9437192 | tf_op jit(solution)/shard_map/ppermute | solution.py:30
  6.8 12.0 %collective-permute-start = (bf16[128,1536]{1,0:T(8,128)(2,1)S(1)}, bf16[128,1536]{1,0:T(8,128)(2,1)S(1)}, u32[]{:S(2)}, u32[]{:S(2)}) collective-permute-start(bf16[128,1536]{1,0:T(8,128)(2,1)S(1)} %pad_maximum_fusion), channel_id=1, source_target_pairs={{128,0},{161,1},{130,2},{163,3},{132,4},{165,5},{134,6},{167,7},{1... | collective-permute-start | bytes 1179656 | tf_op jit(solution)/shard_map/ppermute | solution.py:30
  8.8 40.6 %collective-permute-start.3 = (bf16[128,1536]{1,0:T(8,128)(2,1)}, bf16[128,1536]{1,0:T(8,128)(2,1)}, u32[]{:S(2)}, u32[]{:S(2)}) collective-permute-start(bf16[128,1536]{1,0:T(8,128)(2,1)} %pad_maximum_fusion.1), channel_id=1, source_target_pairs={{64,0},{65,1},{66,2},{67,3},{68,4},{69,5},{70,6},{71,7},{72,8},{73... | collective-permute-start | bytes 1179656 | tf_op jit(solution)/shard_map/ppermute | solution.py:30
  9.6 14.0 %collective-permute-start.7 = (bf16[128,1536]{1,0:T(8,128)(2,1)S(1)}, bf16[128,1536]{1,0:T(8,128)(2,1)S(1)}, u32[]{:S(2)}, u32[]{:S(2)}) collective-permute-start(bf16[128,1536]{1,0:T(8,128)(2,1)S(1)} %pad_maximum_fusion.5), channel_id=1, source_target_pairs={{104,0},{105,1},{106,2},{107,3},{108,4},{109,5},{110,6},{111,7},{9... | collective-permute-start | bytes 1179656 | tf_op jit(solution)/shard_map/ppermute | solution.py:30
  11.9 18.4 %collective-permute-start.8 = (bf16[128,1536]{1,0:T(8,128)(2,1)S(1)}, bf16[128,1536]{1,0:T(8,128)(2,1)S(1)}, u32[]{:S(2)}, u32[]{:S(2)}) collective-permute-start(bf16[128,1536]{1,0:T(8,128)(2,1)S(1)} %pad_maximum_fusion.6), channel_id=1, source_target_pairs={{232,0},{233,1},{234,2},{235,3},{236,4},{237,5},{238,6},{239,7},{2... | collective-permute-start | bytes 1179656 | tf_op jit(solution)/shard_map/ppermute | solution.py:30
  18.8 17.4 %copy-start.1 = (bf16[128,1536]{1,0:T(8,128)(2,1)}, bf16[128,1536]{1,0:T(8,128)(2,1)S(1)}, u32[]{:S(2)}) copy-start(bf16[128,1536]{1,0:T(8,128)(2,1)S(1)} %collective-permute-done.refs_0_) | copy-start | bytes 1179652
  18.8 12.6 %collective-permute-start.2 = (bf16[64,1536]{1,0:T(8,128)(2,1)S(1)}, bf16[64,1536]{1,0:T(8,128)(2,1)S(1)}, u32[]{:S(2)}, u32[]{:S(2)}) collective-permute-start(bf16[64,1536]{1,0:T(8,128)(2,1)S(1)} %get-tuple-element.46), channel_id=1, source_target_pairs={{1,0},{2,1},{3,2},{4,3},{5,4},{6,5},{7,6},{0,7},{9,8},{10,9},{11,1... | collective-permute-start | bytes 589832 | tf_op jit(solution)/shard_map/ppermute | solution.py:30
  24.4 11.0 %collective-permute-start.1 = (bf16[64,1536]{1,0:T(8,128)(2,1)S(1)}, bf16[64,1536]{1,0:T(8,128)(2,1)S(1)}, u32[]{:S(2)}, u32[]{:S(2)}) collective-permute-start(bf16[64,1536]{1,0:T(8,128)(2,1)S(1)} %get-tuple-element.47), channel_id=1, source_target_pairs={{7,0},{0,1},{1,2},{2,3},{3,4},{4,5},{5,6},{6,7},{15,8},{8,9},{9,10... | collective-permute-start | bytes 589832 | tf_op jit(solution)/shard_map/ppermute | solution.py:30
  30.4 21.7 %collective-permute-start.4 = (bf16[128,1536]{1,0:T(8,128)(2,1)}, bf16[128,1536]{1,0:T(8,128)(2,1)}, u32[]{:S(2)}, u32[]{:S(2)}) collective-permute-start(bf16[128,1536]{1,0:T(8,128)(2,1)} %pad_maximum_fusion.2), channel_id=1, source_target_pairs={{192,0},{193,1},{194,2},{195,3},{196,4},{197,5},{198,6},{199,7},{2... | collective-permute-start | bytes 1179656 | tf_op jit(solution)/shard_map/ppermute | solution.py:30
  45.2 36.3 %collective-permute-start.13 = (s16[3,48,2176]{2,1,0:T(8,128)(2,1)}, s16[3,48,2176]{2,1,0:T(8,128)(2,1)S(1)}, u32[]{:S(2)}, u32[]{:S(2)}) collective-permute-start(s16[3,48,2176]{2,1,0:T(8,128)(2,1)} %get-tuple-element.21), channel_id=1, source_target_pairs={{32,0},{33,1},{34,2},{35,3},{36,4},{37,5},{38,6},{39,7},{40,8},{41... | collective-permute-start | bytes 1880072 | tf_op jit(solution)/shard_map/ppermute | solution.py:30
  47.8 18.0 %collective-permute-start.5 = (bf16[128,1536]{1,0:T(8,128)(2,1)S(1)}, bf16[128,1536]{1,0:T(8,128)(2,1)S(1)}, u32[]{:S(2)}, u32[]{:S(2)}) collective-permute-start(bf16[128,1536]{1,0:T(8,128)(2,1)S(1)} %pad_maximum_fusion.3), channel_id=1, source_target_pairs={{32,0},{33,1},{34,2},{35,3},{36,4},{37,5},{38,6},{39,7},{40,8},{41... | collective-permute-start | bytes 1179656 | tf_op jit(solution)/shard_map/ppermute | solution.py:30
  47.9 27.5 %collective-permute-start.9 = (s16[80,2176]{1,0:T(8,128)(2,1)}, s16[80,2176]{1,0:T(8,128)(2,1)S(1)}, u32[]{:S(2)}, u32[]{:S(2)}) collective-permute-start(s16[80,2176]{1,0:T(8,128)(2,1)} %get-tuple-element.17), channel_id=1, source_target_pairs={{192,0},{193,1},{194,2},{195,3},{196,4},{197,5},{198,6},{199,7},{2... | collective-permute-start | bytes 1044488 | tf_op jit(solution)/shard_map/ppermute | solution.py:30
  49.4 26.0 %collective-permute-start.10 = (s16[80,2176]{1,0:T(8,128)(2,1)}, s16[80,2176]{1,0:T(8,128)(2,1)S(1)}, u32[]{:S(2)}, u32[]{:S(2)}) collective-permute-start(s16[80,2176]{1,0:T(8,128)(2,1)} %get-tuple-element.18), channel_id=1, source_target_pairs={{128,0},{129,1},{130,2},{131,3},{132,4},{133,5},{134,6},{135,7},{1... | collective-permute-start | bytes 1044488 | tf_op jit(solution)/shard_map/ppermute | solution.py:30
  52.1 23.4 %collective-permute-start.11 = (s16[80,2176]{1,0:T(8,128)(2,1)}, s16[80,2176]{1,0:T(8,128)(2,1)S(1)}, u32[]{:S(2)}, u32[]{:S(2)}) collective-permute-start(s16[80,2176]{1,0:T(8,128)(2,1)} %get-tuple-element.19), channel_id=1, source_target_pairs={{64,0},{65,1},{66,2},{67,3},{68,4},{69,5},{70,6},{71,7},{72,8},{73... | collective-permute-start | bytes 1044488 | tf_op jit(solution)/shard_map/ppermute | solution.py:30
  79.8 14.3 %collective-permute-start.12 = (s16[128,2176]{1,0:T(8,128)(2,1)}, s16[128,2176]{1,0:T(8,128)(2,1)S(1)}, u32[]{:S(2)}, u32[]{:S(2)}) collective-permute-start(s16[128,2176]{1,0:T(8,128)(2,1)} %get-tuple-element.20), channel_id=1, source_target_pairs={{32,0},{33,1},{34,2},{35,3},{36,4},{37,5},{38,6},{39,7},{40,8},{41... | collective-permute-start | bytes 1671176 | tf_op jit(solution)/shard_map/ppermute | solution.py:30
  86.7 11.8 %collective-permute-start.14 = (s16[128,2176]{1,0:T(8,128)(2,1)}, s16[128,2176]{1,0:T(8,128)(2,1)S(1)}, u32[]{:S(2)}, u32[]{:S(2)}) collective-permute-start(s16[128,2176]{1,0:T(8,128)(2,1)} %get-tuple-element.22), channel_id=1, source_target_pairs={{192,0},{193,1},{194,2},{195,3},{196,4},{197,5},{198,6},{199,7},{2... | collective-permute-start | bytes 1671176 | tf_op jit(solution)/shard_map/ppermute | solution.py:30
  88.0 23.5 %collective-permute-start.15 = (s16[128,2176]{1,0:T(8,128)(2,1)}, s16[128,2176]{1,0:T(8,128)(2,1)S(1)}, u32[]{:S(2)}, u32[]{:S(2)}) collective-permute-start(s16[128,2176]{1,0:T(8,128)(2,1)} %get-tuple-element.23), channel_id=1, source_target_pairs={{128,0},{129,1},{130,2},{131,3},{132,4},{133,5},{134,6},{135,7},{1... | collective-permute-start | bytes 1671176 | tf_op jit(solution)/shard_map/ppermute | solution.py:30
  91.0 23.7 %collective-permute-start.16 = (s16[128,2176]{1,0:T(8,128)(2,1)}, s16[128,2176]{1,0:T(8,128)(2,1)S(1)}, u32[]{:S(2)}, u32[]{:S(2)}) collective-permute-start(s16[128,2176]{1,0:T(8,128)(2,1)} %get-tuple-element.24), channel_id=1, source_target_pairs={{64,0},{65,1},{66,2},{67,3},{68,4},{69,5},{70,6},{71,7},{72,8},{73... | collective-permute-start | bytes 1671176 | tf_op jit(solution)/shard_map/ppermute | solution.py:30
  94.1 20.6 %copy-start.14 = (s16[128,2176]{1,0:T(8,128)(2,1)}, s16[128,2176]{1,0:T(8,128)(2,1)S(1)}, u32[]{:S(2)}) copy-start(s16[128,2176]{1,0:T(8,128)(2,1)S(1)} %collective-permute-done.12.g1) | copy-start | bytes 1671172
  119.1 40.4 %collective-permute-start.21 = (bf16[128,2048]{1,0:T(8,128)(2,1)}, bf16[128,2048]{1,0:T(8,128)(2,1)S(1)}, u32[]{:S(2)}, u32[]{:S(2)}) collective-permute-start(bf16[128,2048]{1,0:T(8,128)(2,1)} %get-tuple-element.30.refs_0_), channel_id=1, source_target_pairs={{32,0},{33,1},{34,2},{35,3},{36,4},{37,5},{38,6},{39,7},{40,8},{41... | collective-permute-start | bytes 1572872 | tf_op jit(solution)/shard_map/ppermute | solution.py:30
  119.4 40.1 %collective-permute-start.20 = (bf16[128,2048]{1,0:T(8,128)(2,1)}, bf16[128,2048]{1,0:T(8,128)(2,1)S(1)}, u32[]{:S(2)}, u32[]{:S(2)}) collective-permute-start(bf16[128,2048]{1,0:T(8,128)(2,1)} %get-tuple-element.30.refs_0_), channel_id=1, source_target_pairs={{192,0},{193,1},{194,2},{195,3},{196,4},{197,5},{198,6},{199,7},{2... | collective-permute-start | bytes 1572872 | tf_op jit(solution)/shard_map/ppermute | solution.py:30
  121.3 38.2 %collective-permute-start.19 = (bf16[128,2048]{1,0:T(8,128)(2,1)}, bf16[128,2048]{1,0:T(8,128)(2,1)S(1)}, u32[]{:S(2)}, u32[]{:S(2)}) collective-permute-start(bf16[128,2048]{1,0:T(8,128)(2,1)} %get-tuple-element.30.refs_0_), channel_id=1, source_target_pairs={{128,0},{129,1},{130,2},{131,3},{132,4},{133,5},{134,6},{135,7},{1... | collective-permute-start | bytes 1572872 | tf_op jit(solution)/shard_map/ppermute | solution.py:30
  123.9 35.6 %collective-permute-start.18 = (bf16[128,2048]{1,0:T(8,128)(2,1)}, bf16[128,2048]{1,0:T(8,128)(2,1)S(1)}, u32[]{:S(2)}, u32[]{:S(2)}) collective-permute-start(bf16[128,2048]{1,0:T(8,128)(2,1)} %get-tuple-element.30.refs_0_), channel_id=1, source_target_pairs={{64,0},{65,1},{66,2},{67,3},{68,4},{69,5},{70,6},{71,7},{72,8},{73... | collective-permute-start | bytes 1572872 | tf_op jit(solution)/shard_map/ppermute | solution.py:30
  165.8 35.5 %collective-permute-start.22 = (bf16[640,2048]{1,0:T(8,128)(2,1)}, bf16[640,2048]{1,0:T(8,128)(2,1)S(1)}, u32[]{:S(2)}, u32[]{:S(2)}) collective-permute-start(bf16[640,2048]{1,0:T(8,128)(2,1)} %shard_map.52.a_ref), channel_id=1, source_target_pairs={{16,0},{17,1},{18,2},{19,3},{20,4},{21,5},{22,6},{23,7},{24,8},{25... | collective-permute-start | bytes 7864328 | tf_op jit(solution)/shard_map/ppermute | solution.py:30
  167.2 11.9 %collective-permute-start.28 = (bf16[48,2048]{1,0:T(8,128)(2,1)S(1)}, bf16[48,2048]{1,0:T(8,128)(2,1)S(1)}, u32[]{:S(2)}, u32[]{:S(2)}) collective-permute-start(bf16[48,2048]{1,0:T(8,128)(2,1)S(1)} %slice.35), channel_id=1, source_target_pairs={{192,0},{193,1},{194,2},{195,3},{196,4},{197,5},{198,6},{199,7},{2... | collective-permute-start | bytes 589832 | tf_op jit(solution)/shard_map/ppermute | solution.py:30
  167.5 11.6 %collective-permute-start.27 = (bf16[48,2048]{1,0:T(8,128)(2,1)S(1)}, bf16[48,2048]{1,0:T(8,128)(2,1)S(1)}, u32[]{:S(2)}, u32[]{:S(2)}) collective-permute-start(bf16[48,2048]{1,0:T(8,128)(2,1)S(1)} %slice.35), channel_id=1, source_target_pairs={{128,0},{129,1},{130,2},{131,3},{132,4},{133,5},{134,6},{135,7},{1... | collective-permute-start | bytes 589832 | tf_op jit(solution)/shard_map/ppermute | solution.py:30
  170.3 16.6 %collective-permute-start.25 = (bf16[80,2048]{1,0:T(8,128)(2,1)S(1)}, bf16[80,2048]{1,0:T(8,128)(2,1)}, u32[]{:S(2)}, u32[]{:S(2)}) collective-permute-start(bf16[80,2048]{1,0:T(8,128)(2,1)S(1)} %slice.34), channel_id=1, source_target_pairs={{32,0},{33,1},{34,2},{35,3},{36,4},{37,5},{38,6},{39,7},{40,8},{41... | collective-permute-start | bytes 983048 | tf_op jit(solution)/shard_map/ppermute | solution.py:30
  171.7 15.1 %collective-permute-start.24 = (bf16[80,2048]{1,0:T(8,128)(2,1)S(1)}, bf16[80,2048]{1,0:T(8,128)(2,1)}, u32[]{:S(2)}, u32[]{:S(2)}) collective-permute-start(bf16[80,2048]{1,0:T(8,128)(2,1)S(1)} %slice.33), channel_id=1, source_target_pairs={{32,0},{33,1},{34,2},{35,3},{36,4},{37,5},{38,6},{39,7},{40,8},{41... | collective-permute-start | bytes 983048 | tf_op jit(solution)/shard_map/ppermute | solution.py:30
  179.1 14.0 %collective-permute-start.23 = (bf16[80,2048]{1,0:T(8,128)(2,1)}, bf16[80,2048]{1,0:T(8,128)(2,1)}, u32[]{:S(2)}, u32[]{:S(2)}) collective-permute-start(bf16[80,2048]{1,0:T(8,128)(2,1)} %slice.32), channel_id=1, source_target_pairs={{32,0},{33,1},{34,2},{35,3},{36,4},{37,5},{38,6},{39,7},{40,8},{41... | collective-permute-start | bytes 983048 | tf_op jit(solution)/shard_map/ppermute | solution.py:30
  179.1 5.9 %collective-permute-start.26 = (bf16[48,2048]{1,0:T(8,128)(2,1)S(1)}, bf16[48,2048]{1,0:T(8,128)(2,1)}, u32[]{:S(2)}, u32[]{:S(2)}) collective-permute-start(bf16[48,2048]{1,0:T(8,128)(2,1)S(1)} %slice.35), channel_id=1, source_target_pairs={{64,0},{65,1},{66,2},{67,3},{68,4},{69,5},{70,6},{71,7},{72,8},{73... | collective-permute-start | bytes 589832 | tf_op jit(solution)/shard_map/ppermute | solution.py:30
  185.0 13.1 %collective-permute-start.17 = (bf16[768,1024]{1,0:T(8,128)(2,1)}, bf16[768,1024]{1,0:T(8,128)(2,1)}, u32[]{:S(2)}, u32[]{:S(2)}) collective-permute-start(bf16[768,1024]{1,0:T(8,128)(2,1)} %get-tuple-element.29), channel_id=1, source_target_pairs={{16,0},{17,1},{18,2},{19,3},{20,4},{21,5},{22,6},{23,7},{24,8},{25... | collective-permute-start | bytes 4718600 | tf_op jit(solution)/shard_map/ppermute | solution.py:30
  196.5 4.8 %collective-permute-start.29 = (bf16[384,2048]{1,0:T(8,128)(2,1)}, bf16[384,2048]{1,0:T(8,128)(2,1)S(1)}, u32[]{:S(2)}, u32[]{:S(2)}) collective-permute-start(bf16[384,2048]{1,0:T(8,128)(2,1)} %shard_map.53.c_ref), channel_id=1, source_target_pairs={{16,0},{17,1},{18,2},{19,3},{20,4},{21,5},{22,6},{23,7},{24,8},{25... | collective-permute-start | bytes 4718600 | tf_op jit(solution)/shard_map/ppermute | solution.py:30
  (22 other events, 57.4 us)

commit v3 on v2

--- a/solution.py
+++ b/solution.py
@@ -38,10 +38,6 @@
     return fetch(value, lambda y, x, c, h, z: (y, x ^ 1, c, h, z))
 
 
-def from_z(value, dz):
-    return fetch(value, lambda y, x, c, h, z: (y, x, c, h, z + dz))
-
-
 def from_core(value):
     return fetch(value, lambda y, x, c, h, z: (y, x, c ^ 1, h, z))
 
@@ -68,13 +64,6 @@
     return codes * jnp.exp2(power[:, :1])
 
 
-def rows_of(pieces, flag, dy, dx):
-    if dy != 2:
-        return pieces[dy, dx][...]
-    far = jnp.concatenate([f[...] for f in pieces["far"]], axis=0)
-    return jnp.where(flag == dx, pieces["near"][...], far)
-
-
 def full(shape):
     return pl.BlockSpec(shape, lambda j: (0,) * len(shape))
 
@@ -84,30 +73,24 @@
 FAR = ((1, 1), (2, 1), (3, 1))
 
 
-def partial_call(flag, pieces, keys, weights, out_shape, out_specs, finish_step):
+def partial_call(pieces, keys, weights, out_shape, out_specs, finish_step):
     w0, w1 = weights
     depth, width = w0.shape
     block = width // STEPS
-    names = [k for k in pieces if k in keys or (k in ("near", "far") and any(q[0] == 2 for q in keys))]
-    flat = []
-    for k in names:
-        flat += pieces[k] if k == "far" else [pieces[k]]
-    rows = pieces[1, 1].shape[0]
-    total = len(keys) * rows
-
-    def body(flag_ref, *refs):
-        refs = list(refs)
-        by = {}
-        for k in names:
-            by[k] = [refs.pop(0), refs.pop(0)] if k == "far" else refs.pop(0)
-        w0_ref, w1_ref = refs[:2]
-        outs, left, acc = refs[2:-2], refs[-2], refs[-1]
+    flat = [pieces[k] for k in keys]
+    count = len(flat)
+    rows = flat[0].shape[0]
+    total = count * rows
+
+    def body(*refs):
+        w0_ref, w1_ref = refs[count : count + 2]
+        outs, left, acc = refs[count + 2 : -2], refs[-2], refs[-1]
         j = pl.program_id(0)
 
         @pl.when(j == 0)
         def _():
-            for n, (dy, dx) in enumerate(keys):
-                left[n * rows : (n + 1) * rows] = rows_of(by, flag_ref[0], dy, dx)
+            for n in range(count):
+                left[n * rows : (n + 1) * rows] = refs[n][...]
 
         value = jnp.dot(left[:, :depth], w0_ref[...], preferred_element_type=F32)
         value += jnp.dot(left[:, depth:], w1_ref[...], preferred_element_type=F32)
@@ -116,8 +99,7 @@
     return pl.pallas_call(
         body,
         grid=(STEPS,),
-        in_specs=[pl.BlockSpec(memory_space=pltpu.SMEM)]
-        + [full(v.shape) for v in flat]
+        in_specs=[full(v.shape) for v in flat]
         + [pl.BlockSpec((depth, block), lambda j: (0, j))] * 2,
         out_specs=out_specs,
         out_shape=out_shape,
@@ -125,10 +107,10 @@
             pltpu.VMEM((total, 2 * depth), BF16),
             pltpu.VMEM((STEPS, total, block), F32),
         ],
-    )(flag, *flat, w0, w1)
-
-
-def sends(flag, pieces, weights, rows, width):
+    )(*flat, w0, w1)
+
+
+def sends(pieces, weights, rows, width):
     a = ROWS_SUM
     shapes = [(3, a, width + LANES)] + [(rows - a, width + LANES)] * 3
 
@@ -145,23 +127,20 @@
                 put(outs[1 + k], (slice(None),), whole[a:])
 
     return partial_call(
-        flag, pieces, FAR, weights,
+        pieces, FAR, weights,
         [jax.ShapeDtypeStruct(s, jnp.int16) for s in shapes],
         [full(s) for s in shapes], step,
     )
 
 
-KEPT = ((1, 0), (2, 0), (3, 0), (0, 1), (0, 0))
-
-
-def keeps(flag, pieces, weights, rows, width):
-    total = len(KEPT) * rows
+def keeps(pieces, keys, weights, width):
+    total = len(keys) * pieces[keys[0]].shape[0]
 
     def step(j, value, outs, acc):
         outs[0][...] = value
 
     return partial_call(
-        flag, pieces, KEPT, weights,
+        pieces, keys, weights,
         jax.ShapeDtypeStruct((total, width), F32),
         pl.BlockSpec((total, width // STEPS), lambda j: (0, j)), step,
     )
@@ -207,7 +186,7 @@
     return pl.pallas_call(
         body,
         grid=(1,),
-        in_specs=[pl.BlockSpec((rows, width), lambda k: (3, 0))]
+        in_specs=[pl.BlockSpec((rows, width), lambda k: (0, 0))]
         + [full(received[0].shape)] * 3,
         out_specs=[full(shape), full((8, LANES))],
         out_shape=[
@@ -245,7 +224,7 @@
         grid=(1,),
         in_specs=[
             pl.BlockSpec(memory_space=pltpu.SMEM),
-            pl.BlockSpec((rows, width), lambda k: (4, 0)),
+            pl.BlockSpec((rows, width), lambda k: (1, 0)),
         ]
         + [full(received[0].shape)] * 4
         + [full(ids.shape)],
@@ -308,23 +287,15 @@
     )(place, *pieces, factors, ids)
 
 
-def turned(flag, pieces, rows, depth):
+def turned(token, pieces, rows, depth):
     g = ROWS_OUT
-    names = list(pieces)
-    flat = []
-    for k in names:
-        flat += pieces[k] if k == "far" else [pieces[k]]
-
-    def body(flag_ref, *refs):
-        refs = list(refs)
-        by = {}
-        for k in names:
-            by[k] = [refs.pop(0), refs.pop(0)] if k == "far" else refs.pop(0)
-        mine, theirs = refs
-        near = [rows_of(by, flag_ref[0], dy, dx) for dy, dx in NEAR]
-        far = [rows_of(by, flag_ref[0], dy, dx) for dy, dx in FAR]
+    flat = [pieces[k] for k in NEAR + FAR]
+
+    def body(token_ref, *refs):
+        ins, (mine, theirs) = refs[:8], refs[8:]
+        far = [r[...] for r in ins[5:]]
         far = jnp.concatenate([f[:g] for f in far] + [f[g:] for f in far], axis=0)
-        parts = near + [far[k * rows : (k + 1) * rows] for k in range(3)]
+        parts = [r[...] for r in ins[:5]] + [far[k * rows : (k + 1) * rows] for k in range(3)]
         for k, part in enumerate(parts):
             flipped = jnp.transpose(part)
             mine[:, k * rows : (k + 1) * rows] = flipped[:depth]
@@ -334,30 +305,29 @@
     return pl.pallas_call(
         body,
         grid=(1,),
-        in_specs=[pl.BlockSpec(memory_space=pltpu.SMEM)] + [full(v.shape) for v in flat],
+        in_specs=[full(token.shape)] + [full(v.shape) for v in flat],
         out_specs=[full(shape)] * 2,
         out_shape=[jax.ShapeDtypeStruct(shape, BF16)] * 2,
         name="turned",
-    )(flag, *flat)
+    )(token, *flat)
 
 
 def gradient(mine, theirs, near, near_other, far, far_other):
     depth = mine.shape[0]
     n, width = near.shape
-    block = width // STEPS
+    m = far.shape[0]
+    block = width // (2 * STEPS)
 
     def body(m_ref, t_ref, a_ref, b_ref, c_ref, d_ref, out):
-        value = jnp.dot(m_ref[:, :n], a_ref[...], preferred_element_type=F32)
-        value += jnp.dot(t_ref[:, :n], b_ref[...], preferred_element_type=F32)
-        value += jnp.dot(m_ref[:, n:], c_ref[...], preferred_element_type=F32)
-        value += jnp.dot(t_ref[:, n:], d_ref[...], preferred_element_type=F32)
-        out[...] = value
+        own = jnp.concatenate([a_ref[...], c_ref[...]], axis=0)
+        other = jnp.concatenate([b_ref[...], d_ref[...]], axis=0)
+        value = jnp.dot(m_ref[...], own, preferred_element_type=F32)
+        out[...] = value + jnp.dot(t_ref[...], other, preferred_element_type=F32)
 
     col = lambda r: pl.BlockSpec((r, block), lambda j: (0, j))
-    m = far.shape[0]
-    return pl.pallas_call(
-        body,
-        grid=(STEPS,),
+    return pl.pallas_call(
+        body,
+        grid=(2 * STEPS,),
         in_specs=[full(mine.shape)] * 2 + [col(n)] * 2 + [col(m)] * 2,
         out_specs=col(depth),
         out_shape=jax.ShapeDtypeStruct((depth, width), F32),
@@ -371,7 +341,6 @@
     c = here % C
     x = (here // C) % X
     y = here // (C * X)
-    odd = block_index % 2
     rows = hidden.shape[0]
     depth, width = head_weight.shape
 
@@ -381,43 +350,38 @@
         other = lax.dynamic_slice_in_dim(hidden, (chip * C + 1 - c) * depth, depth, 1)
         return jnp.concatenate([own, other], axis=1)
 
-    def two_hop(y, x, c, h, z):
-        return (y + 2, x ^ (z % 2), c, h, z)
-
     def outside(dy):
         return lambda y, x, c, h, z: (y + dy, x ^ 1, c, h ^ 1, z)
 
-    half = rows // 2
-    near2 = fetch(columns_for(2, odd), two_hop)
+    weights = (head_weight, from_core(head_weight))
     pieces = {
-        "near": near2,
-        "far": [from_z(near2[:half], -1), from_z(near2[half:], 1)],
+        (2, 1): fetch(columns_for(2, 1), lambda y, x, c, h, z: (y + 2, x ^ 1, c, h, z)),
         (1, 1): fetch(columns_for(1, 1), outside(1)),
         (3, 1): fetch(columns_for(3, 1), outside(3)),
+        (2, 0): from_y(columns_for(2, 0), 2),
         (1, 0): from_y(columns_for(1, 0), 1),
         (3, 0): from_y(columns_for(3, 0), 3),
         (0, 1): from_x(columns_for(0, 1)),
         (0, 0): columns_for(0, 0),
     }
-    flag = odd.reshape(1).astype(jnp.int32)
-    weights = (head_weight, from_core(head_weight))
-
-    to_x, *to_y = sends(flag, pieces, weights, rows, width)
+
+    to_x, *to_y = sends(pieces, weights, rows, width)
     got_x = from_x(to_x)
     got_y = [from_y(v, -dy) for v, dy in zip(to_y, (1, 2, 3))]
-    kept = keeps(flag, pieces, weights, rows, width)
-    send_y = combine_y(kept, got_x, rows, width)
-    send_x, token = combine_x(kept, got_y, rows, width)
+    kept_y = keeps(pieces, NEAR[1:4], weights, width)
+    kept_x = keeps(pieces, (NEAR[4], NEAR[0]), weights, width)
+    send_y = combine_y(kept_y, got_x, rows, width)
+    send_x, token = combine_x(kept_x, got_y, rows, width)
     received = [from_x(send_x)]
     received += [from_y(v, -dy) for v, dy in zip(send_y, (1, 2, 3))]
 
+    mine, sent = turned(token, pieces, rows, depth)
     token = token[0, 0]
-    mine, sent = turned(flag + token, pieces, rows, depth)
     theirs = from_core(sent)
     ids = (targets + token).astype(F32).reshape(16, rows)
     owners = [(((y + dy) % Y) * X + (x ^ dx)) * C + c for dy, dx in NEAR + FAR]
     place = jnp.stack([here, block_index * width, *owners]).astype(jnp.int32)
-    raised, stats = finish(kept, received, ids, place, rows, width)
+    raised, stats = finish(kept_x, received, ids, place, rows, width)
 
     g = ROWS_OUT
     side_x = from_x(raised)

time: 218 us -> 213 us (0.977)
  starting transfers between devices: 43.4 us -> 34.6 us
  Pallas kernels: 53.5 us -> 57.7 us
    ppermute x30 -> x29, starting transfers between devices: 43.4 us -> 34.6 us  [fetch(): return lax.ppermute(value, AXES, pairs)]
    pallas_call x4 -> x5, Pallas kernels: 33.5 us -> 37.6 us  [the longest x3 20.2 us: partial_call(): pl.pallas_call(body, grid=(STEPS,), in_specs=[full(v.shape) for v in flat...]
    concatenate x7 -> x8, other arithmetic: 4.5 us -> 5.25 us  [columns_for(): return jnp.concatenate([own, other], axis=1)]
    ppermute x30 -> x29, waiting for transfers between devices: 57.1 us -> 57.3 us  [fetch(): return lax.ppermute(value, AXES, pairs)]
    unnamed x48 -> x46, local copies, waits for them, and re-layouts: 12.1 us -> 12.2 us
  transfers between devices with their start and end apart: 30 -> 29, of which waited for: 10 -> 10; matrix products, arithmetic and copies ran while one was open for 7% -> 8% of each run, Pallas kernels for 15% -> 17%
where the time goes in v3:
time: 213 us; the launch traced here: 212 us
  Pallas kernels  57.7 us (27%)
  waiting for transfers between devices  57.3 us (27%)
  starting transfers between devices  34.6 us (16%)
  blocking collectives  33.1 us (16%)
  local copies, waits for them, and re-layouts  21.7 us (10%)
  other arithmetic  6.5 us (3%)
    ppermute x29, waiting for transfers between devices, fetch(): return lax.ppermute(value, AXES, pairs)  57.3 us
    ppermute x29, starting transfers between devices, fetch(): return lax.ppermute(value, AXES, pairs)  34.6 us
    all_to_all x1, blocking collectives, per_device(): every = lax.all_to_all(stats, 'vocab', 0, 0, tiled=True)  20.5 us
    pallas_call x3, Pallas kernels, partial_call(): pl.pallas_call(body, grid=(STEPS,), in_specs=[full(v.shape) for v in flat...  20.2 us
    pallas_call x1, Pallas kernels, gradient(): pl.pallas_call(body, grid=(2 * STEPS,), in_specs=[full(mine.shape)] * 2 +...  12.9 us
    all_to_all x1, blocking collectives, per_device(): factors = lax.all_to_all(factor, 'dp', 0, 0, tiled=True)  12.6 us
    unnamed x46, local copies, waits for them, and re-layouts  12.2 us
    pallas_call x2, Pallas kernels, slopes(): pl.pallas_call(body, grid=(1,), in_specs=[pl.BlockSpec(memory_space=pltpu...  7.79 us
  transfers between devices with their start and end apart: 29, of which 10 were waited for; matrix products, arithmetic and copies ran while one was open for 8% of the time, Pallas kernels for 17%

profile of v3, /device:TPU:1, one launch (start us, length us, event | category | flops | bytes accessed | tf_op | source)
XLA Modules:
  0.0 211.6 jit_solution(8108366968853452332)
XLA Ops:
  0.6 3.3 %collective-permute-start.1 = (bf16[768,2048]{1,0:T(8,128)(2,1)}, bf16[768,2048]{1,0:T(8,128)(2,1)S(1)}, u32[]{:S(2)}, u32[]{:S(2)}) collective-permute-start(bf16[768,2048]{1,0:T(8,128)(2,1)} %refs_3_.3), channel_id=1, source_target_pairs={{16,0},{17,1},{18,2},{19,3},{20,4},{21,5},{22,6},{23,7},{24,8},{25... | collective-permute-start | bytes 9437192 | tf_op jit(solution)/shard_map/ppermute | solution.py:30
  3.9 3.1 %constant_dynamic-slice_fusion.1 = (bf16[128,768]{1,0:T(8,128)(2,1)}, bf16[128,768]{1,0:T(8,128)(2,1)S(1)}, bf16[128,768]{1,0:T(8,128)(2,1)S(1)}, bf16[128,768]{...) fusion(bf16[128,12288]{1,0:T(8,128)(2,1)} %param.3, ...), kind=kLoop, calls=%fused_computation.10 | loop fusion | bytes 6291520 | tf_op jit(solution)/shard_map/dynamic_slice | solution.py:349
  7.8 3.8 %collective-permute-start.2 = (bf16[128,1536]{1,0:T(8,128)(2,1)S(1)}, bf16[128,1536]{1,0:T(8,128)(2,1)S(1)}, u32[]{:S(2)}, u32[]{:S(2)}) collective-permute-start(bf16[128,1536]{1,0:T(8,128)(2,1)S(1)} %pad_maximum_fusion.2), channel_id=1, source_target_pairs={{104,0},{105,1},{106,2},{107,3},{108,4},{109,5},{110,6},{111,7},{9... | collective-permute-start | bytes 1179656 | tf_op jit(solution)/shard_map/ppermute | solution.py:30
  13.9 7.8 %collective-permute-done.2.refs_0_.refs_5_ = bf16[128,1536]{1,0:T(8,128)(2,1)S(1)} collective-permute-done((bf16[128,1536]{1,0:T(8,128)(2,1)S(1)}, bf16[128,1536]{1,0:T(8,128)(2,1)S(1)}, u32[]{:S(2)}, u32[]{:S(2)}) %collective-permute-start.2) | collective-permute-done | bytes 393248 | tf_op jit(solution)/shard_map/ppermute | solution.py:30
  21.7 3.3 %collective-permute-start.9 = (bf16[128,1536]{1,0:T(8,128)(2,1)}, bf16[128,1536]{1,0:T(8,128)(2,1)}, u32[]{:S(2)}, u32[]{:S(2)}) collective-permute-start(bf16[128,1536]{1,0:T(8,128)(2,1)} %pad_maximum_fusion.5), channel_id=1, source_target_pairs={{64,0},{65,1},{66,2},{67,3},{68,4},{69,5},{70,6},{71,7},{72,8},{73... | collective-permute-start | bytes 1179656 | tf_op jit(solution)/shard_map/ppermute | solution.py:30
  25.7 10.1 %collective-permute-done.3.refs_1_.refs_6_ = bf16[128,1536]{1,0:T(8,128)(2,1)S(1)} collective-permute-done((bf16[128,1536]{1,0:T(8,128)(2,1)S(1)}, bf16[128,1536]{1,0:T(8,128)(2,1)S(1)}, u32[]{:S(2)}, u32[]{:S(2)}) %collective-permute-start.3) | collective-permute-done | bytes 393248 | tf_op jit(solution)/shard_map/ppermute | solution.py:30
  39.8 7.3 %shard_map.51 = (s16[3,48,2176]{2,1,0:T(8,128)(2,1)}, s16[80,2176]{1,0:T(8,128)(2,1)}, s16[80,2176]{1,0:T(8,128)(2,1)}, s16[80,2176]{1,0:T(8,128)(2,1)}) custom-call(bf16[128,1536]{1,0:T(8,128)(2,1)} %copy-done.3, bf16[128,1536]{1,0:T(8,128)(2,1)} %copy-done.4, bf16[128,1536]{1,0:T(8,128)(2,1)} %copy-done.5, bf16[768,2048]{1,0:T(8,128)(2,1)} %refs_3_.3, ...), custom_call_target="tpu_custom_call" | custom-call | tf_op jit(solution)/shard_map/pallas_call | solution.py:99
  49.4 2.8 %collective-permute-start.6 = (s16[80,2176]{1,0:T(8,128)(2,1)}, s16[80,2176]{1,0:T(8,128)(2,1)S(1)}, u32[]{:S(2)}, u32[]{:S(2)}) collective-permute-start(s16[80,2176]{1,0:T(8,128)(2,1)} %get-tuple-element.18), channel_id=1, source_target_pairs={{128,0},{129,1},{130,2},{131,3},{132,4},{133,5},{134,6},{135,7},{1... | collective-permute-start | bytes 1044488 | tf_op jit(solution)/shard_map/ppermute | solution.py:30
  52.2 1.8 pad_maximum_fusion.1.refs_1_.refs_0_
  54.0 6.0 %shard_map.50.kept_ref = f32[256,2048]{1,0:T(8,128)} custom-call(bf16[128,1536]{1,0:T(8,128)(2,1)} %copy-done.2, bf16[128,1536]{1,0:T(8,128)(2,1)} %pad_maximum_fusion.1.refs_1_.refs_0_, bf16[768,2048]{1,0:T(8,128)(2,1)} %refs_3_.3, bf16[768,2048]{1,0:T(8,128)(2,1)} %copy-done), custom_call_target="tpu_custom_call" | custom-call | tf_op jit(solution)/shard_map/pallas_call | solution.py:99
  60.8 6.9 %shard_map.52.kept_ref = f32[384,2048]{1,0:T(8,128)} custom-call(bf16[128,1536]{1,0:T(8,128)(2,1)} %collective-permute-done.9.refs_0_.refs_1_, bf16[128,1536]{1,0:T(8,128)(2,1)} %collective-permute-done.10.refs_1_.refs_2_, bf16[128,1536]{1,0:T(8,128)(2,1)} %copy-done.7, bf16[768,2048]{1,0:T(8,128)(2,1)} %refs_3_.3, bf16[768,2048]{1,0:T(8,128)(2,1)} %copy-done), custom_call_target="tpu_custom_call" | custom-call | tf_op jit(solution)/shard_map/pallas_call | solution.py:99
  67.7 3.9 %collective-permute-done.6.g2 = s16[80,2176]{1,0:T(8,128)(2,1)S(1)} collective-permute-done((s16[80,2176]{1,0:T(8,128)(2,1)}, s16[80,2176]{1,0:T(8,128)(2,1)S(1)}, u32[]{:S(2)}, u32[]{:S(2)}) %collective-permute-start.6) | collective-permute-done | bytes 348192 | tf_op jit(solution)/shard_map/ppermute | solution.py:30
  73.1 2.7 %combine_x.1 = (s16[128,2176]{1,0:T(8,128)(2,1)}, s32[8,128]{1,0:T(8,128)}) custom-call(f32[256,2048]{1,0:T(8,128)} %shard_map.50.kept_ref, s16[80,2176]{1,0:T(8,128)(2,1)} %copy-done.17, s16[80,2176]{1,0:T(8,128)(2,1)} %copy-done.18, s16[80,2176]{1,0:T(8,128)(2,1)} %copy-done.19), custom_call_target="tpu_custom_call" | custom-call | tf_op jit(solution)/shard_map/combine_x/pallas_call | solution.py:186
  75.8 2.0 collective-permute-start.8
  78.7 4.4 %combine_y.1 = (s16[128,2176]{1,0:T(8,128)(2,1)}, s16[128,2176]{1,0:T(8,128)(2,1)}, s16[128,2176]{1,0:T(8,128)(2,1)}) custom-call(f32[384,2048]{1,0:T(8,128)} %shard_map.52.kept_ref, s16[3,48,2176]{2,1,0:T(8,128)(2,1)} %copy-done.12), custom_call_target="tpu_custom_call" | custom-call | tf_op jit(solution)/shard_map/combine_y/pallas_call | solution.py:163
  84.3 2.1 collective-permute-start.15
  89.4 5.9 %collective-permute-done.13.g2 = s16[128,2176]{1,0:T(8,128)(2,1)S(1)} collective-permute-done((s16[128,2176]{1,0:T(8,128)(2,1)}, s16[128,2176]{1,0:T(8,128)(2,1)S(1)}, u32[]{:S(2)}, u32[]{:S(2)}) %collective-permute-start.13) | collective-permute-done | bytes 557088 | tf_op jit(solution)/shard_map/ppermute | solution.py:30
  95.3 10.3 %collective-permute-done.14.g3 = s16[128,2176]{1,0:T(8,128)(2,1)S(1)} collective-permute-done((s16[128,2176]{1,0:T(8,128)(2,1)}, s16[128,2176]{1,0:T(8,128)(2,1)S(1)}, u32[]{:S(2)}, u32[]{:S(2)}) %collective-permute-start.14) | collective-permute-done | bytes 557088 | tf_op jit(solution)/shard_map/ppermute | solution.py:30
  105.6 5.0 %collective-permute-done.15.g4 = s16[128,2176]{1,0:T(8,128)(2,1)S(1)} collective-permute-done((s16[128,2176]{1,0:T(8,128)(2,1)}, s16[128,2176]{1,0:T(8,128)(2,1)S(1)}, u32[]{:S(2)}, u32[]{:S(2)}) %collective-permute-start.15) | collective-permute-done | bytes 557088 | tf_op jit(solution)/shard_map/ppermute | solution.py:30
  111.5 3.6 %finish.1 = (bf16[128,2048]{1,0:T(8,128)(2,1)}, f32[16,8,128]{2,1,0:T(8,128)}) custom-call(s32[10]{0:T(128)} %stack.43.place_ref, f32[256,2048]{1,0:T(8,128)} %shard_map.50.kept_ref, s16[128,2176]{1,0:T(8,128)(2,1)} %copy-done.13, s16[128,2176]{1,0:T(8,128)(2,1)} %copy-done.14, s16[128,2176]{1,0:T(8,128)(2,1)} %copy-done.15, s16[128,2176]{1,0:T(8,128)(2,1)} %copy-done.16, ...), custom_call_target="tpu_custom_call" | custom-call | tf_op jit(solution)/shard_map/finish/pallas_call | solution.py:222
  115.1 1.8 collective-permute-start.19
  116.9 2.7 %collective-permute-start.18 = (bf16[128,2048]{1,0:T(8,128)(2,1)}, bf16[128,2048]{1,0:T(8,128)(2,1)S(1)}, u32[]{:S(2)}, u32[]{:S(2)}) collective-permute-start(bf16[128,2048]{1,0:T(8,128)(2,1)} %get-tuple-element.30.refs_0_), channel_id=1, source_target_pairs={{128,0},{129,1},{130,2},{131,3},{132,4},{133,5},{134,6},{135,7},{1... | collective-permute-start | bytes 1572872 | tf_op jit(solution)/shard_map/ppermute | solution.py:30
  119.6 20.5 %all_to_all.10.every_ref = f32[16,8,128]{2,1,0:T(8,128)} all-to-all(f32[16,8,128]{2,1,0:T(8,128)} %get-tuple-element.26.own_ref), channel_id=1, replica_groups=mesh['dp'=16,'vocab'=16] {'vocab'}, dimensions={0} | all-to-all | bytes 131072 | tf_op jit(solution)/shard_map/all_to_all | solution.py:392
  141.7 12.6 %all_to_all.11.refs_5_.refs_6_ = f32[16,8,128]{2,1,0:T(8,128)} all-to-all(f32[16,8,128]{2,1,0:T(8,128)} %get-tuple-element.31), channel_id=1, replica_groups=mesh['dp'=16,'vocab'=16] {'dp'}, dimensions={0} | all-to-all | bytes 131072 | tf_op jit(solution)/shard_map/all_to_all | solution.py:394
  156.3 4.4 %shard_map.53.a_ref = bf16[640,2048]{1,0:T(8,128)(2,1)} custom-call(s32[10]{0:T(128)} %stack.43.place_ref, bf16[128,2048]{1,0:T(8,128)(2,1)} %get-tuple-element.30.refs_0_, bf16[128,2048]{1,0:T(8,128)(2,1)} %copy-done.8, bf16[128,2048]{1,0:T(8,128)(2,1)} %copy-done.9, bf16[128,2048]{1,0:T(8,128)(2,1)} %copy-done.10, bf16[128,2048]{1,0:T(8,128)(2,1)} %copy-done.11, ...), custom_call_target="tpu_custom_call" | custom-call | tf_op jit(solution)/shard_map/pallas_call | solution.py:279
  169.5 4.4 %collective-permute-done.27.refs_5_ = bf16[48,2048]{1,0:T(8,128)(2,1)S(1)} collective-permute-done((bf16[48,2048]{1,0:T(8,128)(2,1)S(1)}, bf16[48,2048]{1,0:T(8,128)(2,1)S(1)}, u32[]{:S(2)}, u32[]{:S(2)}) %collective-permute-start.27) | collective-permute-done | bytes 196640 | tf_op jit(solution)/shard_map/ppermute | solution.py:30
  175.3 4.4 %turned.1 = (bf16[768,1024]{1,0:T(8,128)(2,1)}, bf16[768,1024]{1,0:T(8,128)(2,1)}) custom-call(s32[8,128]{1,0:T(8,128)} %get-tuple-element.25.token_ref, bf16[128,1536]{1,0:T(8,128)(2,1)} %pad_maximum_fusion.1.refs_1_.refs_0_, bf16[128,1536]{1,0:T(8,128)(2,1)} %collective-permute-done.9.refs_0_.refs_1_, ...), custom_call_target="tpu_custom_call" | custom-call | tf_op jit(solution)/shard_map/turned/pallas_call | solution.py:305
  180.9 1.8 collective-permute-start.16
  182.7 5.2 %collective-permute-done.22.refs_0_ = bf16[80,2048]{1,0:T(8,128)(2,1)} collective-permute-done((bf16[80,2048]{1,0:T(8,128)(2,1)}, bf16[80,2048]{1,0:T(8,128)(2,1)}, u32[]{:S(2)}, u32[]{:S(2)}) %collective-permute-start.22) | collective-permute-done | bytes 327712 | tf_op jit(solution)/shard_map/ppermute | solution.py:30
  187.9 3.4 %shard_map.54.c_ref = bf16[384,2048]{1,0:T(8,128)(2,1)} custom-call(s32[10]{0:T(128)} %stack.43.place_ref, bf16[80,2048]{1,0:T(8,128)(2,1)} %collective-permute-done.22.refs_0_, bf16[80,2048]{1,0:T(8,128)(2,1)} %collective-permute-done.23.refs_1_, bf16[80,2048]{1,0:T(8,128)(2,1)} %collective-permute-done.24.refs_2_, ...), custom_call_target="tpu_custom_call" | custom-call | tf_op jit(solution)/shard_map/pallas_call | solution.py:279
  192.9 3.2 %collective-permute-done.28.d_ref = bf16[384,2048]{1,0:T(8,128)(2,1)S(1)} collective-permute-done((bf16[384,2048]{1,0:T(8,128)(2,1)}, bf16[384,2048]{1,0:T(8,128)(2,1)S(1)}, u32[]{:S(2)}, u32[]{:S(2)}) %collective-permute-start.28) | collective-permute-done | bytes 1572896 | tf_op jit(solution)/shard_map/ppermute | solution.py:30
  198.7 12.9 %gradient.1 = f32[768,2048]{1,0:T(8,128)} custom-call(bf16[768,1024]{1,0:T(8,128)(2,1)} %get-tuple-element.28.m_ref, bf16[768,1024]{1,0:T(8,128)(2,1)} %collective-permute-done.16.t_ref, bf16[640,2048]{1,0:T(8,128)(2,1)} %shard_map.53.a_ref, bf16[640,2048]{1,0:T(8,128)(2,1)} %copy-done.1, bf16[384,2048]{1,0:T(8,128)(2,1)} %shard_map.54.c_ref, ...), custom_call_target="tpu_custom_call" | custom-call | tf_op jit(solution)/shard_map/gradient/pallas_call | solution.py:328
  (101 shorter events, 37.2 us)
Async XLA Ops:
  0.6 37.6 %collective-permute-start.1 = (bf16[768,2048]{1,0:T(8,128)(2,1)}, bf16[768,2048]{1,0:T(8,128)(2,1)S(1)}, u32[]{:S(2)}, u32[]{:S(2)}) collective-permute-start(bf16[768,2048]{1,0:T(8,128)(2,1)} %refs_3_.3), channel_id=1, source_target_pairs={{16,0},{17,1},{18,2},{19,3},{20,4},{21,5},{22,6},{23,7},{24,8},{25... | collective-permute-start | bytes 9437192 | tf_op jit(solution)/shard_map/ppermute | solution.py:30
  7.7 40.6 %collective-permute-start = (bf16[128,1536]{1,0:T(8,128)(2,1)}, bf16[128,1536]{1,0:T(8,128)(2,1)S(1)}, u32[]{:S(2)}, u32[]{:S(2)}) collective-permute-start(bf16[128,1536]{1,0:T(8,128)(2,1)} %pad_maximum_fusion), channel_id=1, source_target_pairs={{32,0},{33,1},{34,2},{35,3},{36,4},{37,5},{38,6},{39,7},{40,8},{41... | collective-permute-start | bytes 1179656 | tf_op jit(solution)/shard_map/ppermute | solution.py:30
  7.8 13.9 %collective-permute-start.2 = (bf16[128,1536]{1,0:T(8,128)(2,1)S(1)}, bf16[128,1536]{1,0:T(8,128)(2,1)S(1)}, u32[]{:S(2)}, u32[]{:S(2)}) collective-permute-start(bf16[128,1536]{1,0:T(8,128)(2,1)S(1)} %pad_maximum_fusion.2), channel_id=1, source_target_pairs={{104,0},{105,1},{106,2},{107,3},{108,4},{109,5},{110,6},{111,7},{9... | collective-permute-start | bytes 1179656 | tf_op jit(solution)/shard_map/ppermute | solution.py:30
  11.7 24.2 %collective-permute-start.3 = (bf16[128,1536]{1,0:T(8,128)(2,1)S(1)}, bf16[128,1536]{1,0:T(8,128)(2,1)S(1)}, u32[]{:S(2)}, u32[]{:S(2)}) collective-permute-start(bf16[128,1536]{1,0:T(8,128)(2,1)S(1)} %pad_maximum_fusion.3), channel_id=1, source_target_pairs={{160,0},{161,1},{162,2},{163,3},{164,4},{165,5},{166,6},{167,7},{1... | collective-permute-start | bytes 1179656 | tf_op jit(solution)/shard_map/ppermute | solution.py:30
  12.2 25.3 %collective-permute-start.4 = (bf16[128,1536]{1,0:T(8,128)(2,1)S(1)}, bf16[128,1536]{1,0:T(8,128)(2,1)S(1)}, u32[]{:S(2)}, u32[]{:S(2)}) collective-permute-start(bf16[128,1536]{1,0:T(8,128)(2,1)S(1)} %pad_maximum_fusion.4), channel_id=1, source_target_pairs={{232,0},{233,1},{234,2},{235,3},{236,4},{237,5},{238,6},{239,7},{2... | collective-permute-start | bytes 1179656 | tf_op jit(solution)/shard_map/ppermute | solution.py:30
  21.7 15.7 %copy-start.3 = (bf16[128,1536]{1,0:T(8,128)(2,1)}, bf16[128,1536]{1,0:T(8,128)(2,1)S(1)}, u32[]{:S(2)}) copy-start(bf16[128,1536]{1,0:T(8,128)(2,1)S(1)} %collective-permute-done.2.refs_0_.refs_5_) | copy-start | bytes 1179652
  21.7 27.8 %collective-permute-start.9 = (bf16[128,1536]{1,0:T(8,128)(2,1)}, bf16[128,1536]{1,0:T(8,128)(2,1)}, u32[]{:S(2)}, u32[]{:S(2)}) collective-permute-start(bf16[128,1536]{1,0:T(8,128)(2,1)} %pad_maximum_fusion.5), channel_id=1, source_target_pairs={{64,0},{65,1},{66,2},{67,3},{68,4},{69,5},{70,6},{71,7},{72,8},{73... | collective-permute-start | bytes 1179656 | tf_op jit(solution)/shard_map/ppermute | solution.py:30
  35.8 16.3 %collective-permute-start.10 = (bf16[128,1536]{1,0:T(8,128)(2,1)}, bf16[128,1536]{1,0:T(8,128)(2,1)}, u32[]{:S(2)}, u32[]{:S(2)}) collective-permute-start(bf16[128,1536]{1,0:T(8,128)(2,1)} %pad_maximum_fusion.6), channel_id=1, source_target_pairs={{128,0},{129,1},{130,2},{131,3},{132,4},{133,5},{134,6},{135,7},{1... | collective-permute-start | bytes 1179656 | tf_op jit(solution)/shard_map/ppermute | solution.py:30
  47.2 30.7 %collective-permute-start.12 = (s16[3,48,2176]{2,1,0:T(8,128)(2,1)}, s16[3,48,2176]{2,1,0:T(8,128)(2,1)S(1)}, u32[]{:S(2)}, u32[]{:S(2)}) collective-permute-start(s16[3,48,2176]{2,1,0:T(8,128)(2,1)} %get-tuple-element.21), channel_id=1, source_target_pairs={{32,0},{33,1},{34,2},{35,3},{36,4},{37,5},{38,6},{39,7},{40,8},{41... | collective-permute-start | bytes 1880072 | tf_op jit(solution)/shard_map/ppermute | solution.py:30
  48.2 11.8 %collective-permute-start.11 = (bf16[128,1536]{1,0:T(8,128)(2,1)S(1)}, bf16[128,1536]{1,0:T(8,128)(2,1)S(1)}, u32[]{:S(2)}, u32[]{:S(2)}) collective-permute-start(bf16[128,1536]{1,0:T(8,128)(2,1)S(1)} %pad_maximum_fusion.7), channel_id=1, source_target_pairs={{192,0},{193,1},{194,2},{195,3},{196,4},{197,5},{198,6},{199,7},{2... | collective-permute-start | bytes 1179656 | tf_op jit(solution)/shard_map/ppermute | solution.py:30
  48.4 19.3 %collective-permute-start.5 = (s16[80,2176]{1,0:T(8,128)(2,1)}, s16[80,2176]{1,0:T(8,128)(2,1)S(1)}, u32[]{:S(2)}, u32[]{:S(2)}) collective-permute-start(s16[80,2176]{1,0:T(8,128)(2,1)} %get-tuple-element.17), channel_id=1, source_target_pairs={{192,0},{193,1},{194,2},{195,3},{196,4},{197,5},{198,6},{199,7},{2... | collective-permute-start | bytes 1044488 | tf_op jit(solution)/shard_map/ppermute | solution.py:30
  49.4 22.2 %collective-permute-start.6 = (s16[80,2176]{1,0:T(8,128)(2,1)}, s16[80,2176]{1,0:T(8,128)(2,1)S(1)}, u32[]{:S(2)}, u32[]{:S(2)}) collective-permute-start(s16[80,2176]{1,0:T(8,128)(2,1)} %get-tuple-element.18), channel_id=1, source_target_pairs={{128,0},{129,1},{130,2},{131,3},{132,4},{133,5},{134,6},{135,7},{1... | collective-permute-start | bytes 1044488 | tf_op jit(solution)/shard_map/ppermute | solution.py:30
  52.2 19.4 %collective-permute-start.7 = (s16[80,2176]{1,0:T(8,128)(2,1)}, s16[80,2176]{1,0:T(8,128)(2,1)S(1)}, u32[]{:S(2)}, u32[]{:S(2)}) collective-permute-start(s16[80,2176]{1,0:T(8,128)(2,1)} %get-tuple-element.19), channel_id=1, source_target_pairs={{64,0},{65,1},{66,2},{67,3},{68,4},{69,5},{70,6},{71,7},{72,8},{73... | collective-permute-start | bytes 1044488 | tf_op jit(solution)/shard_map/ppermute | solution.py:30
  75.8 13.6 %collective-permute-start.8 = (s16[128,2176]{1,0:T(8,128)(2,1)}, s16[128,2176]{1,0:T(8,128)(2,1)S(1)}, u32[]{:S(2)}, u32[]{:S(2)}) collective-permute-start(s16[128,2176]{1,0:T(8,128)(2,1)} %get-tuple-element.20), channel_id=1, source_target_pairs={{32,0},{33,1},{34,2},{35,3},{36,4},{37,5},{38,6},{39,7},{40,8},{41... | collective-permute-start | bytes 1671176 | tf_op jit(solution)/shard_map/ppermute | solution.py:30
  83.1 12.2 %collective-permute-start.13 = (s16[128,2176]{1,0:T(8,128)(2,1)}, s16[128,2176]{1,0:T(8,128)(2,1)S(1)}, u32[]{:S(2)}, u32[]{:S(2)}) collective-permute-start(s16[128,2176]{1,0:T(8,128)(2,1)} %get-tuple-element.22), channel_id=1, source_target_pairs={{192,0},{193,1},{194,2},{195,3},{196,4},{197,5},{198,6},{199,7},{2... | collective-permute-start | bytes 1671176 | tf_op jit(solution)/shard_map/ppermute | solution.py:30
  83.1 22.5 %collective-permute-start.14 = (s16[128,2176]{1,0:T(8,128)(2,1)}, s16[128,2176]{1,0:T(8,128)(2,1)S(1)}, u32[]{:S(2)}, u32[]{:S(2)}) collective-permute-start(s16[128,2176]{1,0:T(8,128)(2,1)} %get-tuple-element.23), channel_id=1, source_target_pairs={{128,0},{129,1},{130,2},{131,3},{132,4},{133,5},{134,6},{135,7},{1... | collective-permute-start | bytes 1671176 | tf_op jit(solution)/shard_map/ppermute | solution.py:30
  84.3 26.4 %collective-permute-start.15 = (s16[128,2176]{1,0:T(8,128)(2,1)}, s16[128,2176]{1,0:T(8,128)(2,1)S(1)}, u32[]{:S(2)}, u32[]{:S(2)}) collective-permute-start(s16[128,2176]{1,0:T(8,128)(2,1)} %get-tuple-element.24), channel_id=1, source_target_pairs={{64,0},{65,1},{66,2},{67,3},{68,4},{69,5},{70,6},{71,7},{72,8},{73... | collective-permute-start | bytes 1671176 | tf_op jit(solution)/shard_map/ppermute | solution.py:30
  89.4 21.3 %copy-start.13 = (s16[128,2176]{1,0:T(8,128)(2,1)}, s16[128,2176]{1,0:T(8,128)(2,1)S(1)}, u32[]{:S(2)}) copy-start(s16[128,2176]{1,0:T(8,128)(2,1)S(1)} %collective-permute-done.8.g1) | copy-start | bytes 1671172
  95.3 15.3 %copy-start.14 = (s16[128,2176]{1,0:T(8,128)(2,1)}, s16[128,2176]{1,0:T(8,128)(2,1)S(1)}, u32[]{:S(2)}) copy-start(s16[128,2176]{1,0:T(8,128)(2,1)S(1)} %collective-permute-done.13.g2) | copy-start | bytes 1671172
  115.1 39.2 %collective-permute-start.20 = (bf16[128,2048]{1,0:T(8,128)(2,1)}, bf16[128,2048]{1,0:T(8,128)(2,1)S(1)}, u32[]{:S(2)}, u32[]{:S(2)}) collective-permute-start(bf16[128,2048]{1,0:T(8,128)(2,1)} %get-tuple-element.30.refs_0_), channel_id=1, source_target_pairs={{32,0},{33,1},{34,2},{35,3},{36,4},{37,5},{38,6},{39,7},{40,8},{41... | collective-permute-start | bytes 1572872 | tf_op jit(solution)/shard_map/ppermute | solution.py:30
  115.1 39.2 %collective-permute-start.19 = (bf16[128,2048]{1,0:T(8,128)(2,1)}, bf16[128,2048]{1,0:T(8,128)(2,1)S(1)}, u32[]{:S(2)}, u32[]{:S(2)}) collective-permute-start(bf16[128,2048]{1,0:T(8,128)(2,1)} %get-tuple-element.30.refs_0_), channel_id=1, source_target_pairs={{192,0},{193,1},{194,2},{195,3},{196,4},{197,5},{198,6},{199,7},{2... | collective-permute-start | bytes 1572872 | tf_op jit(solution)/shard_map/ppermute | solution.py:30
  116.9 37.4 %collective-permute-start.18 = (bf16[128,2048]{1,0:T(8,128)(2,1)}, bf16[128,2048]{1,0:T(8,128)(2,1)S(1)}, u32[]{:S(2)}, u32[]{:S(2)}) collective-permute-start(bf16[128,2048]{1,0:T(8,128)(2,1)} %get-tuple-element.30.refs_0_), channel_id=1, source_target_pairs={{128,0},{129,1},{130,2},{131,3},{132,4},{133,5},{134,6},{135,7},{1... | collective-permute-start | bytes 1572872 | tf_op jit(solution)/shard_map/ppermute | solution.py:30
  119.6 34.7 %collective-permute-start.17 = (bf16[128,2048]{1,0:T(8,128)(2,1)}, bf16[128,2048]{1,0:T(8,128)(2,1)S(1)}, u32[]{:S(2)}, u32[]{:S(2)}) collective-permute-start(bf16[128,2048]{1,0:T(8,128)(2,1)} %get-tuple-element.30.refs_0_), channel_id=1, source_target_pairs={{64,0},{65,1},{66,2},{67,3},{68,4},{69,5},{70,6},{71,7},{72,8},{73... | collective-permute-start | bytes 1572872 | tf_op jit(solution)/shard_map/ppermute | solution.py:30
  160.6 35.5 %collective-permute-start.21 = (bf16[640,2048]{1,0:T(8,128)(2,1)}, bf16[640,2048]{1,0:T(8,128)(2,1)S(1)}, u32[]{:S(2)}, u32[]{:S(2)}) collective-permute-start(bf16[640,2048]{1,0:T(8,128)(2,1)} %shard_map.53.a_ref), channel_id=1, source_target_pairs={{16,0},{17,1},{18,2},{19,3},{20,4},{21,5},{22,6},{23,7},{24,8},{25... | collective-permute-start | bytes 7864328 | tf_op jit(solution)/shard_map/ppermute | solution.py:30
  162.0 11.9 %collective-permute-start.27 = (bf16[48,2048]{1,0:T(8,128)(2,1)S(1)}, bf16[48,2048]{1,0:T(8,128)(2,1)S(1)}, u32[]{:S(2)}, u32[]{:S(2)}) collective-permute-start(bf16[48,2048]{1,0:T(8,128)(2,1)S(1)} %slice.25), channel_id=1, source_target_pairs={{192,0},{193,1},{194,2},{195,3},{196,4},{197,5},{198,6},{199,7},{2... | collective-permute-start | bytes 589832 | tf_op jit(solution)/shard_map/ppermute | solution.py:30
  162.4 11.6 %collective-permute-start.26 = (bf16[48,2048]{1,0:T(8,128)(2,1)S(1)}, bf16[48,2048]{1,0:T(8,128)(2,1)S(1)}, u32[]{:S(2)}, u32[]{:S(2)}) collective-permute-start(bf16[48,2048]{1,0:T(8,128)(2,1)S(1)} %slice.25), channel_id=1, source_target_pairs={{128,0},{129,1},{130,2},{131,3},{132,4},{133,5},{134,6},{135,7},{1... | collective-permute-start | bytes 589832 | tf_op jit(solution)/shard_map/ppermute | solution.py:30
  165.1 17.6 %collective-permute-start.24 = (bf16[80,2048]{1,0:T(8,128)(2,1)S(1)}, bf16[80,2048]{1,0:T(8,128)(2,1)}, u32[]{:S(2)}, u32[]{:S(2)}) collective-permute-start(bf16[80,2048]{1,0:T(8,128)(2,1)S(1)} %slice.24), channel_id=1, source_target_pairs={{32,0},{33,1},{34,2},{35,3},{36,4},{37,5},{38,6},{39,7},{40,8},{41... | collective-permute-start | bytes 983048 | tf_op jit(solution)/shard_map/ppermute | solution.py:30
  166.6 16.1 %collective-permute-start.23 = (bf16[80,2048]{1,0:T(8,128)(2,1)S(1)}, bf16[80,2048]{1,0:T(8,128)(2,1)}, u32[]{:S(2)}, u32[]{:S(2)}) collective-permute-start(bf16[80,2048]{1,0:T(8,128)(2,1)S(1)} %slice.23), channel_id=1, source_target_pairs={{32,0},{33,1},{34,2},{35,3},{36,4},{37,5},{38,6},{39,7},{40,8},{41... | collective-permute-start | bytes 983048 | tf_op jit(solution)/shard_map/ppermute | solution.py:30
  173.9 14.0 %collective-permute-start.22 = (bf16[80,2048]{1,0:T(8,128)(2,1)}, bf16[80,2048]{1,0:T(8,128)(2,1)}, u32[]{:S(2)}, u32[]{:S(2)}) collective-permute-start(bf16[80,2048]{1,0:T(8,128)(2,1)} %slice.22), channel_id=1, source_target_pairs={{32,0},{33,1},{34,2},{35,3},{36,4},{37,5},{38,6},{39,7},{40,8},{41... | collective-permute-start | bytes 983048 | tf_op jit(solution)/shard_map/ppermute | solution.py:30
  175.3 5.6 %collective-permute-start.25 = (bf16[48,2048]{1,0:T(8,128)(2,1)S(1)}, bf16[48,2048]{1,0:T(8,128)(2,1)}, u32[]{:S(2)}, u32[]{:S(2)}) collective-permute-start(bf16[48,2048]{1,0:T(8,128)(2,1)S(1)} %slice.25), channel_id=1, source_target_pairs={{64,0},{65,1},{66,2},{67,3},{68,4},{69,5},{70,6},{71,7},{72,8},{73... | collective-permute-start | bytes 589832 | tf_op jit(solution)/shard_map/ppermute | solution.py:30
  180.9 12.0 %collective-permute-start.16 = (bf16[768,1024]{1,0:T(8,128)(2,1)}, bf16[768,1024]{1,0:T(8,128)(2,1)}, u32[]{:S(2)}, u32[]{:S(2)}) collective-permute-start(bf16[768,1024]{1,0:T(8,128)(2,1)} %get-tuple-element.29), channel_id=1, source_target_pairs={{16,0},{17,1},{18,2},{19,3},{20,4},{21,5},{22,6},{23,7},{24,8},{25... | collective-permute-start | bytes 4718600 | tf_op jit(solution)/shard_map/ppermute | solution.py:30
  191.3 4.8 %collective-permute-start.28 = (bf16[384,2048]{1,0:T(8,128)(2,1)}, bf16[384,2048]{1,0:T(8,128)(2,1)S(1)}, u32[]{:S(2)}, u32[]{:S(2)}) collective-permute-start(bf16[384,2048]{1,0:T(8,128)(2,1)} %shard_map.54.c_ref), channel_id=1, source_target_pairs={{16,0},{17,1},{18,2},{19,3},{20,4},{21,5},{22,6},{23,7},{24,8},{25... | collective-permute-start | bytes 4718600 | tf_op jit(solution)/shard_map/ppermute | solution.py:30
  (20 other events, 42.6 us)

commit v4 on v3

--- a/solution.py
+++ b/solution.py
@@ -92,8 +92,8 @@
             for n in range(count):
                 left[n * rows : (n + 1) * rows] = refs[n][...]
 
-        value = jnp.dot(left[:, :depth], w0_ref[...], preferred_element_type=F32)
-        value += jnp.dot(left[:, depth:], w1_ref[...], preferred_element_type=F32)
+        right = jnp.concatenate([w0_ref[...], w1_ref[...]], axis=0)
+        value = jnp.dot(left[...], right, preferred_element_type=F32)
         finish_step(j, value, outs, acc)
 
     return pl.pallas_call(
@@ -245,14 +245,14 @@
         picked = jnp.sum(picks, axis=0, keepdims=True)
         loss_ref[...] = top + jnp.log(total) - picked
         factor = jnp.exp(own_ref[0, :1] - top) / total
-        factor_ref[...] = jnp.broadcast_to(factor[None], factor_ref.shape)
+        factor_ref[...] = jnp.broadcast_to(factor, factor_ref.shape)
 
     rows = every.shape[-1]
     return pl.pallas_call(
         body,
         out_shape=[
             jax.ShapeDtypeStruct((1, rows), F32),
-            jax.ShapeDtypeStruct(every.shape, F32),
+            jax.ShapeDtypeStruct((8, rows), F32),
         ],
         name="settle",
     )(every, stats)
@@ -263,13 +263,14 @@
     total = sum(sizes)
 
     def body(place_ref, *refs):
-        ins, factor_ref, ids_ref, out = refs[:-3], refs[-3], refs[-2], refs[-1]
+        ins, factor_refs, ids_ref, out = refs[:-6], refs[-6:-2], refs[-2], refs[-1]
         columns = lax.broadcasted_iota(jnp.int32, (max(sizes), width), 1) + place_ref[1]
         columns = columns.astype(F32)
         at = 0
         for ref, n, (k, a, b) in zip(ins, sizes, spans):
             owner = place_ref[2 + k]
-            scale = upright(factor_ref[owner, :1])[a:b, :1]
+            dy, dx = (NEAR + FAR)[k]
+            scale = upright(factor_refs[dy][dx, :1])[a:b, :1]
             label = upright(ids_ref[pl.ds(owner, 1), :])[a:b, :1]
             value = ref[...].astype(F32) * scale
             value = value - jnp.where(columns[:n] == label, 1.0, 0.0)
@@ -281,10 +282,11 @@
         grid=(1,),
         in_specs=[pl.BlockSpec(memory_space=pltpu.SMEM)]
         + [full(p.shape) for p in pieces]
-        + [full(factors.shape), full(ids.shape)],
+        + [full(f.shape) for f in factors]
+        + [full(ids.shape)],
         out_specs=full((total, width)),
         out_shape=jax.ShapeDtypeStruct((total, width), BF16),
-    )(place, *pieces, factors, ids)
+    )(place, *pieces, *factors, ids)
 
 
 def turned(token, pieces, rows, depth):
@@ -316,18 +318,17 @@
     depth = mine.shape[0]
     n, width = near.shape
     m = far.shape[0]
-    block = width // (2 * STEPS)
+    block = width // STEPS
 
     def body(m_ref, t_ref, a_ref, b_ref, c_ref, d_ref, out):
-        own = jnp.concatenate([a_ref[...], c_ref[...]], axis=0)
-        other = jnp.concatenate([b_ref[...], d_ref[...]], axis=0)
-        value = jnp.dot(m_ref[...], own, preferred_element_type=F32)
-        out[...] = value + jnp.dot(t_ref[...], other, preferred_element_type=F32)
+        left = jnp.concatenate([m_ref[...], t_ref[...]], axis=1)
+        right = jnp.concatenate([a_ref[...], c_ref[...], b_ref[...], d_ref[...]], axis=0)
+        out[...] = jnp.dot(left, right, preferred_element_type=F32)
 
     col = lambda r: pl.BlockSpec((r, block), lambda j: (0, j))
     return pl.pallas_call(
         body,
-        grid=(2 * STEPS,),
+        grid=(STEPS,),
         in_specs=[full(mine.shape)] * 2 + [col(n)] * 2 + [col(m)] * 2,
         out_specs=col(depth),
         out_shape=jax.ShapeDtypeStruct((depth, width), F32),
@@ -391,7 +392,8 @@
 
     every = lax.all_to_all(stats, "vocab", 0, 0, tiled=True)
     loss, factor = settle(every, stats)
-    factors = lax.all_to_all(factor, "dp", 0, 0, tiled=True)
+    pair = jnp.stack([factor, from_x(factor)])
+    factors = [pair] + [from_y(pair, dy) for dy in (1, 2, 3)]
 
     near_spans = [(k, 0, rows) for k in range(5)]
     far_spans = [(5 + k, 0, g) for k in range(3)] + [(5 + k, g, rows) for k in range(3)]

time: 213 us -> 219 us (1.028)
  blocking collectives: 33.1 us -> 20.5 us
  waiting for transfers between devices: 57.3 us -> 67.8 us
  starting transfers between devices: 34.6 us -> 44.7 us
    all_to_all x1 -> x0, blocking collectives: 12.6 us -> none  [per_device(): factors = lax.all_to_all(factor, 'dp', 0, 0, tiled=True)]
    ppermute x29 -> x33, waiting for transfers between devices: 57.3 us -> 67.8 us  [fetch(): return lax.ppermute(value, AXES, pairs)]
    ppermute x29 -> x33, starting transfers between devices: 34.6 us -> 44.7 us  [fetch(): return lax.ppermute(value, AXES, pairs)]
    unnamed x46 -> x54, local copies, waits for them, and re-layouts: 12.2 us -> 11.5 us
  transfers between devices with their start and end apart: 29 -> 33, of which waited for: 10 -> 15; matrix products, arithmetic and copies ran while one was open for 8% -> 8% of each run, Pallas kernels for 17% -> 17%
where the time goes in v4:
time: 219 us; the launch traced here: 218 us
  waiting for transfers between devices  67.8 us (31%)
  Pallas kernels  56.2 us (26%)
  starting transfers between devices  44.7 us (20%)
  local copies, waits for them, and re-layouts  21 us (10%)
  blocking collectives  20.5 us (9%)
  other arithmetic  7.17 us (3%)
    ppermute x33, waiting for transfers between devices, fetch(): return lax.ppermute(value, AXES, pairs)  67.8 us
    ppermute x33, starting transfers between devices, fetch(): return lax.ppermute(value, AXES, pairs)  44.7 us
    all_to_all x1, blocking collectives, per_device(): every = lax.all_to_all(stats, 'vocab', 0, 0, tiled=True)  20.5 us
    pallas_call x3, Pallas kernels, partial_call(): pl.pallas_call(body, grid=(STEPS,), in_specs=[full(v.shape) for v in flat...  20.3 us
    unnamed x54, local copies, waits for them, and re-layouts  11.5 us
    pallas_call x1, Pallas kernels, gradient(): pl.pallas_call(body, grid=(STEPS,), in_specs=[full(mine.shape)] * 2 + [co...  11.5 us
    pallas_call x2, Pallas kernels, slopes(): pl.pallas_call(body, grid=(1,), in_specs=[pl.BlockSpec(memory_space=pltpu...  7.85 us
    concatenate x8, other arithmetic, columns_for(): return jnp.concatenate([own, other], axis=1)  5.25 us
  transfers between devices with their start and end apart: 33, of which 15 were waited for; matrix products, arithmetic and copies ran while one was open for 8% of the time, Pallas kernels for 17%

profile of v4, /device:TPU:1, one launch (start us, length us, event | category | flops | bytes accessed | tf_op | source)
XLA Modules:
  0.0 218.2 jit_solution(12115923295125155960)
XLA Ops:
  0.6 3.3 %collective-permute-start.1 = (bf16[768,2048]{1,0:T(8,128)(2,1)}, bf16[768,2048]{1,0:T(8,128)(2,1)S(1)}, u32[]{:S(2)}, u32[]{:S(2)}) collective-permute-start(bf16[768,2048]{1,0:T(8,128)(2,1)} %refs_3_.3), channel_id=1, source_target_pairs={{16,0},{17,1},{18,2},{19,3},{20,4},{21,5},{22,6},{23,7},{24,8},{25... | collective-permute-start | bytes 9437192 | tf_op jit(solution)/shard_map/ppermute | solution.py:30
  3.9 3.1 %constant_dynamic-slice_fusion.1 = (bf16[128,768]{1,0:T(8,128)(2,1)}, bf16[128,768]{1,0:T(8,128)(2,1)S(1)}, bf16[128,768]{1,0:T(8,128)(2,1)S(1)}, bf16[128,768]{...) fusion(bf16[128,12288]{1,0:T(8,128)(2,1)} %param.3, ...), kind=kLoop, calls=%fused_computation.11 | loop fusion | bytes 6291520 | tf_op jit(solution)/shard_map/dynamic_slice | solution.py:350
  7.8 3.8 %collective-permute-start.2 = (bf16[128,1536]{1,0:T(8,128)(2,1)S(1)}, bf16[128,1536]{1,0:T(8,128)(2,1)S(1)}, u32[]{:S(2)}, u32[]{:S(2)}) collective-permute-start(bf16[128,1536]{1,0:T(8,128)(2,1)S(1)} %pad_maximum_fusion.2), channel_id=1, source_target_pairs={{104,0},{105,1},{106,2},{107,3},{108,4},{109,5},{110,6},{111,7},{9... | collective-permute-start | bytes 1179656 | tf_op jit(solution)/shard_map/ppermute | solution.py:30
  13.9 7.8 %collective-permute-done.2.refs_0_.refs_5_ = bf16[128,1536]{1,0:T(8,128)(2,1)S(1)} collective-permute-done((bf16[128,1536]{1,0:T(8,128)(2,1)S(1)}, bf16[128,1536]{1,0:T(8,128)(2,1)S(1)}, u32[]{:S(2)}, u32[]{:S(2)}) %collective-permute-start.2) | collective-permute-done | bytes 393248 | tf_op jit(solution)/shard_map/ppermute | solution.py:30
  21.7 3.3 %collective-permute-start.9 = (bf16[128,1536]{1,0:T(8,128)(2,1)}, bf16[128,1536]{1,0:T(8,128)(2,1)}, u32[]{:S(2)}, u32[]{:S(2)}) collective-permute-start(bf16[128,1536]{1,0:T(8,128)(2,1)} %pad_maximum_fusion.5), channel_id=1, source_target_pairs={{64,0},{65,1},{66,2},{67,3},{68,4},{69,5},{70,6},{71,7},{72,8},{73... | collective-permute-start | bytes 1179656 | tf_op jit(solution)/shard_map/ppermute | solution.py:30
  25.7 10.1 %collective-permute-done.3.refs_1_.refs_6_ = bf16[128,1536]{1,0:T(8,128)(2,1)S(1)} collective-permute-done((bf16[128,1536]{1,0:T(8,128)(2,1)S(1)}, bf16[128,1536]{1,0:T(8,128)(2,1)S(1)}, u32[]{:S(2)}, u32[]{:S(2)}) %collective-permute-start.3) | collective-permute-done | bytes 393248 | tf_op jit(solution)/shard_map/ppermute | solution.py:30
  39.9 7.4 %shard_map.51 = (s16[3,48,2176]{2,1,0:T(8,128)(2,1)}, s16[80,2176]{1,0:T(8,128)(2,1)}, s16[80,2176]{1,0:T(8,128)(2,1)}, s16[80,2176]{1,0:T(8,128)(2,1)}) custom-call(bf16[128,1536]{1,0:T(8,128)(2,1)} %copy-done.3, bf16[128,1536]{1,0:T(8,128)(2,1)} %copy-done.4, bf16[128,1536]{1,0:T(8,128)(2,1)} %copy-done.5, bf16[768,2048]{1,0:T(8,128)(2,1)} %refs_3_.3, ...), custom_call_target="tpu_custom_call" | custom-call | tf_op jit(solution)/shard_map/pallas_call | solution.py:99
  49.5 2.8 %collective-permute-start.6 = (s16[80,2176]{1,0:T(8,128)(2,1)}, s16[80,2176]{1,0:T(8,128)(2,1)S(1)}, u32[]{:S(2)}, u32[]{:S(2)}) collective-permute-start(s16[80,2176]{1,0:T(8,128)(2,1)} %get-tuple-element.18), channel_id=1, source_target_pairs={{128,0},{129,1},{130,2},{131,3},{132,4},{133,5},{134,6},{135,7},{1... | collective-permute-start | bytes 1044488 | tf_op jit(solution)/shard_map/ppermute | solution.py:30
  54.0 6.0 %shard_map.50.kept_ref = f32[256,2048]{1,0:T(8,128)} custom-call(bf16[128,1536]{1,0:T(8,128)(2,1)} %copy-done.2, bf16[128,1536]{1,0:T(8,128)(2,1)} %pad_maximum_fusion.1.refs_1_.refs_0_, bf16[768,2048]{1,0:T(8,128)(2,1)} %refs_3_.3, bf16[768,2048]{1,0:T(8,128)(2,1)} %copy-done), custom_call_target="tpu_custom_call" | custom-call | tf_op jit(solution)/shard_map/pallas_call | solution.py:99
  60.8 6.9 %shard_map.52.kept_ref = f32[384,2048]{1,0:T(8,128)} custom-call(bf16[128,1536]{1,0:T(8,128)(2,1)} %collective-permute-done.9.refs_0_.refs_1_, bf16[128,1536]{1,0:T(8,128)(2,1)} %collective-permute-done.10.refs_1_.refs_2_, bf16[128,1536]{1,0:T(8,128)(2,1)} %copy-done.7, bf16[768,2048]{1,0:T(8,128)(2,1)} %refs_3_.3, bf16[768,2048]{1,0:T(8,128)(2,1)} %copy-done), custom_call_target="tpu_custom_call" | custom-call | tf_op jit(solution)/shard_map/pallas_call | solution.py:99
  67.7 4.0 %collective-permute-done.6.g2 = s16[80,2176]{1,0:T(8,128)(2,1)S(1)} collective-permute-done((s16[80,2176]{1,0:T(8,128)(2,1)}, s16[80,2176]{1,0:T(8,128)(2,1)S(1)}, u32[]{:S(2)}, u32[]{:S(2)}) %collective-permute-start.6) | collective-permute-done | bytes 348192 | tf_op jit(solution)/shard_map/ppermute | solution.py:30
  73.1 2.7 %combine_x.1 = (s16[128,2176]{1,0:T(8,128)(2,1)}, s32[8,128]{1,0:T(8,128)}) custom-call(f32[256,2048]{1,0:T(8,128)} %shard_map.50.kept_ref, s16[80,2176]{1,0:T(8,128)(2,1)} %copy-done.17, s16[80,2176]{1,0:T(8,128)(2,1)} %copy-done.18, s16[80,2176]{1,0:T(8,128)(2,1)} %copy-done.19), custom_call_target="tpu_custom_call" | custom-call | tf_op jit(solution)/shard_map/combine_x/pallas_call | solution.py:186
  78.7 4.4 %combine_y.1 = (s16[128,2176]{1,0:T(8,128)(2,1)}, s16[128,2176]{1,0:T(8,128)(2,1)}, s16[128,2176]{1,0:T(8,128)(2,1)}) custom-call(f32[384,2048]{1,0:T(8,128)} %shard_map.52.kept_ref, s16[3,48,2176]{2,1,0:T(8,128)(2,1)} %copy-done.12), custom_call_target="tpu_custom_call" | custom-call | tf_op jit(solution)/shard_map/combine_y/pallas_call | solution.py:163
  89.4 5.9 %collective-permute-done.13.g2 = s16[128,2176]{1,0:T(8,128)(2,1)S(1)} collective-permute-done((s16[128,2176]{1,0:T(8,128)(2,1)}, s16[128,2176]{1,0:T(8,128)(2,1)S(1)}, u32[]{:S(2)}, u32[]{:S(2)}) %collective-permute-start.13) | collective-permute-done | bytes 557088 | tf_op jit(solution)/shard_map/ppermute | solution.py:30
  95.3 10.3 %collective-permute-done.14.g3 = s16[128,2176]{1,0:T(8,128)(2,1)S(1)} collective-permute-done((s16[128,2176]{1,0:T(8,128)(2,1)}, s16[128,2176]{1,0:T(8,128)(2,1)S(1)}, u32[]{:S(2)}, u32[]{:S(2)}) %collective-permute-start.14) | collective-permute-done | bytes 557088 | tf_op jit(solution)/shard_map/ppermute | solution.py:30
  105.6 5.0 %collective-permute-done.15.g4 = s16[128,2176]{1,0:T(8,128)(2,1)S(1)} collective-permute-done((s16[128,2176]{1,0:T(8,128)(2,1)}, s16[128,2176]{1,0:T(8,128)(2,1)S(1)}, u32[]{:S(2)}, u32[]{:S(2)}) %collective-permute-start.15) | collective-permute-done | bytes 557088 | tf_op jit(solution)/shard_map/ppermute | solution.py:30
  111.5 3.6 %finish.1 = (bf16[128,2048]{1,0:T(8,128)(2,1)}, f32[16,8,128]{2,1,0:T(8,128)}) custom-call(s32[10]{0:T(128)} %stack.52.place_ref, f32[256,2048]{1,0:T(8,128)} %shard_map.50.kept_ref, s16[128,2176]{1,0:T(8,128)(2,1)} %copy-done.13, s16[128,2176]{1,0:T(8,128)(2,1)} %copy-done.14, s16[128,2176]{1,0:T(8,128)(2,1)} %copy-done.15, s16[128,2176]{1,0:T(8,128)(2,1)} %copy-done.16, ...), custom_call_target="tpu_custom_call" | custom-call | tf_op jit(solution)/shard_map/finish/pallas_call | solution.py:222
  116.9 2.7 %collective-permute-start.18 = (bf16[128,2048]{1,0:T(8,128)(2,1)}, bf16[128,2048]{1,0:T(8,128)(2,1)S(1)}, u32[]{:S(2)}, u32[]{:S(2)}) collective-permute-start(bf16[128,2048]{1,0:T(8,128)(2,1)} %get-tuple-element.30.refs_0_), channel_id=1, source_target_pairs={{128,0},{129,1},{130,2},{131,3},{132,4},{133,5},{134,6},{135,7},{1... | collective-permute-start | bytes 1572872 | tf_op jit(solution)/shard_map/ppermute | solution.py:30
  119.6 20.5 %all_to_all.5.every_ref = f32[16,8,128]{2,1,0:T(8,128)} all-to-all(f32[16,8,128]{2,1,0:T(8,128)} %get-tuple-element.26.own_ref), channel_id=1, replica_groups=mesh['dp'=16,'vocab'=16] {'vocab'}, dimensions={0} | all-to-all | bytes 131072 | tf_op jit(solution)/shard_map/all_to_all | solution.py:393
  141.6 2.7 %collective-permute-done.21 = f32[8,128]{1,0:T(8,128)S(1)} collective-permute-done((f32[8,128]{1,0:T(8,128)}, f32[8,128]{1,0:T(8,128)S(1)}, u32[]{:S(2)}, u32[]{:S(2)}) %collective-permute-start.21) | collective-permute-done | bytes 4128 | tf_op jit(solution)/shard_map/ppermute | solution.py:30
  146.5 2.2 %collective-permute-done.24.refs_8_.refs_9_ = f32[2,8,128]{2,1,0:T(8,128)S(1)} collective-permute-done((f32[2,8,128]{2,1,0:T(8,128)S(1)}, f32[2,8,128]{2,1,0:T(8,128)S(1)}, u32[]{:S(2)}, u32[]{:S(2)}) %collective-permute-start.24) | collective-permute-done | bytes 8224 | tf_op jit(solution)/shard_map/ppermute | solution.py:30
  149.3 3.4 %collective-permute-done.23.refs_7_.refs_8_ = f32[2,8,128]{2,1,0:T(8,128)S(1)} collective-permute-done((f32[2,8,128]{2,1,0:T(8,128)S(1)}, f32[2,8,128]{2,1,0:T(8,128)S(1)}, u32[]{:S(2)}, u32[]{:S(2)}) %collective-permute-start.23) | collective-permute-done | bytes 8224 | tf_op jit(solution)/shard_map/ppermute | solution.py:30
  152.7 2.5 %collective-permute-done.22.refs_6_.refs_7_ = f32[2,8,128]{2,1,0:T(8,128)S(1)} collective-permute-done((f32[2,8,128]{2,1,0:T(8,128)S(1)}, f32[2,8,128]{2,1,0:T(8,128)S(1)}, u32[]{:S(2)}, u32[]{:S(2)}) %collective-permute-start.22) | collective-permute-done | bytes 8224 | tf_op jit(solution)/shard_map/ppermute | solution.py:30
  157.2 4.4 %shard_map.53.a_ref = bf16[640,2048]{1,0:T(8,128)(2,1)} custom-call(s32[10]{0:T(128)} %stack.52.place_ref, bf16[128,2048]{1,0:T(8,128)(2,1)} %get-tuple-element.30.refs_0_, bf16[128,2048]{1,0:T(8,128)(2,1)} %copy-done.8, bf16[128,2048]{1,0:T(8,128)(2,1)} %copy-done.9, bf16[128,2048]{1,0:T(8,128)(2,1)} %copy-done.10, bf16[128,2048]{1,0:T(8,128)(2,1)} %copy-done.11, ...), custom_call_target="tpu_custom_call" | custom-call | tf_op jit(solution)/shard_map/pallas_call | solution.py:280
  161.6 7.4 %collective-permute-start.25 = (bf16[640,2048]{1,0:T(8,128)(2,1)}, bf16[640,2048]{1,0:T(8,128)(2,1)S(1)}, u32[]{:S(2)}, u32[]{:S(2)}) collective-permute-start(bf16[640,2048]{1,0:T(8,128)(2,1)} %shard_map.53.a_ref), channel_id=1, source_target_pairs={{16,0},{17,1},{18,2},{19,3},{20,4},{21,5},{22,6},{23,7},{24,8},{25... | collective-permute-start | bytes 7864328 | tf_op jit(solution)/shard_map/ppermute | solution.py:30
  178.1 3.2 %collective-permute-done.30.refs_4_ = bf16[48,2048]{1,0:T(8,128)(2,1)S(1)} collective-permute-done((bf16[48,2048]{1,0:T(8,128)(2,1)S(1)}, bf16[48,2048]{1,0:T(8,128)(2,1)S(1)}, u32[]{:S(2)}, u32[]{:S(2)}) %collective-permute-start.30) | collective-permute-done | bytes 196640 | tf_op jit(solution)/shard_map/ppermute | solution.py:30
  182.0 4.4 %turned.1 = (bf16[768,1024]{1,0:T(8,128)(2,1)}, bf16[768,1024]{1,0:T(8,128)(2,1)}) custom-call(s32[8,128]{1,0:T(8,128)} %get-tuple-element.25.token_ref, bf16[128,1536]{1,0:T(8,128)(2,1)} %pad_maximum_fusion.1.refs_1_.refs_0_, bf16[128,1536]{1,0:T(8,128)(2,1)} %collective-permute-done.9.refs_0_.refs_1_, ...), custom_call_target="tpu_custom_call" | custom-call | tf_op jit(solution)/shard_map/turned/pallas_call | solution.py:307
  186.9 2.9 %collective-permute-start.16 = (bf16[768,1024]{1,0:T(8,128)(2,1)}, bf16[768,1024]{1,0:T(8,128)(2,1)}, u32[]{:S(2)}, u32[]{:S(2)}) collective-permute-start(bf16[768,1024]{1,0:T(8,128)(2,1)} %get-tuple-element.29), channel_id=1, source_target_pairs={{16,0},{17,1},{18,2},{19,3},{20,4},{21,5},{22,6},{23,7},{24,8},{25... | collective-permute-start | bytes 4718600 | tf_op jit(solution)/shard_map/ppermute | solution.py:30
  189.8 6.2 %collective-permute-done.26.refs_0_ = bf16[80,2048]{1,0:T(8,128)(2,1)} collective-permute-done((bf16[80,2048]{1,0:T(8,128)(2,1)}, bf16[80,2048]{1,0:T(8,128)(2,1)}, u32[]{:S(2)}, u32[]{:S(2)}) %collective-permute-start.26) | collective-permute-done | bytes 327712 | tf_op jit(solution)/shard_map/ppermute | solution.py:30
  196.0 3.5 %shard_map.54.c_ref = bf16[384,2048]{1,0:T(8,128)(2,1)} custom-call(s32[10]{0:T(128)} %stack.52.place_ref, bf16[80,2048]{1,0:T(8,128)(2,1)} %collective-permute-done.26.refs_0_, bf16[80,2048]{1,0:T(8,128)(2,1)} %collective-permute-done.27.refs_1_, bf16[80,2048]{1,0:T(8,128)(2,1)} %collective-permute-done.28.refs_2_, ...), custom_call_target="tpu_custom_call" | custom-call | tf_op jit(solution)/shard_map/pallas_call | solution.py:280
  200.9 3.2 %collective-permute-done.32.d_ref = bf16[384,2048]{1,0:T(8,128)(2,1)S(1)} collective-permute-done((bf16[384,2048]{1,0:T(8,128)(2,1)}, bf16[384,2048]{1,0:T(8,128)(2,1)S(1)}, u32[]{:S(2)}, u32[]{:S(2)}) %collective-permute-start.32) | collective-permute-done | bytes 1572896 | tf_op jit(solution)/shard_map/ppermute | solution.py:30
  206.8 11.5 %gradient.1 = f32[768,2048]{1,0:T(8,128)} custom-call(bf16[768,1024]{1,0:T(8,128)(2,1)} %get-tuple-element.28.m_ref, bf16[768,1024]{1,0:T(8,128)(2,1)} %collective-permute-done.16.t_ref, bf16[640,2048]{1,0:T(8,128)(2,1)} %shard_map.53.a_ref, bf16[640,2048]{1,0:T(8,128)(2,1)} %copy-done.1, bf16[384,2048]{1,0:T(8,128)(2,1)} %shard_map.54.c_ref, ...), custom_call_target="tpu_custom_call" | custom-call | tf_op jit(solution)/shard_map/gradient/pallas_call | solution.py:329
  (117 shorter events, 46.3 us)
Async XLA Ops:
  0.6 37.6 %collective-permute-start.1 = (bf16[768,2048]{1,0:T(8,128)(2,1)}, bf16[768,2048]{1,0:T(8,128)(2,1)S(1)}, u32[]{:S(2)}, u32[]{:S(2)}) collective-permute-start(bf16[768,2048]{1,0:T(8,128)(2,1)} %refs_3_.3), channel_id=1, source_target_pairs={{16,0},{17,1},{18,2},{19,3},{20,4},{21,5},{22,6},{23,7},{24,8},{25... | collective-permute-start | bytes 9437192 | tf_op jit(solution)/shard_map/ppermute | solution.py:30
  7.8 40.6 %collective-permute-start = (bf16[128,1536]{1,0:T(8,128)(2,1)}, bf16[128,1536]{1,0:T(8,128)(2,1)S(1)}, u32[]{:S(2)}, u32[]{:S(2)}) collective-permute-start(bf16[128,1536]{1,0:T(8,128)(2,1)} %pad_maximum_fusion), channel_id=1, source_target_pairs={{32,0},{33,1},{34,2},{35,3},{36,4},{37,5},{38,6},{39,7},{40,8},{41... | collective-permute-start | bytes 1179656 | tf_op jit(solution)/shard_map/ppermute | solution.py:30
  7.8 13.9 %collective-permute-start.2 = (bf16[128,1536]{1,0:T(8,128)(2,1)S(1)}, bf16[128,1536]{1,0:T(8,128)(2,1)S(1)}, u32[]{:S(2)}, u32[]{:S(2)}) collective-permute-start(bf16[128,1536]{1,0:T(8,128)(2,1)S(1)} %pad_maximum_fusion.2), channel_id=1, source_target_pairs={{104,0},{105,1},{106,2},{107,3},{108,4},{109,5},{110,6},{111,7},{9... | collective-permute-start | bytes 1179656 | tf_op jit(solution)/shard_map/ppermute | solution.py:30
  11.7 24.2 %collective-permute-start.3 = (bf16[128,1536]{1,0:T(8,128)(2,1)S(1)}, bf16[128,1536]{1,0:T(8,128)(2,1)S(1)}, u32[]{:S(2)}, u32[]{:S(2)}) collective-permute-start(bf16[128,1536]{1,0:T(8,128)(2,1)S(1)} %pad_maximum_fusion.3), channel_id=1, source_target_pairs={{160,0},{161,1},{162,2},{163,3},{164,4},{165,5},{166,6},{167,7},{1... | collective-permute-start | bytes 1179656 | tf_op jit(solution)/shard_map/ppermute | solution.py:30
  12.2 25.3 %collective-permute-start.4 = (bf16[128,1536]{1,0:T(8,128)(2,1)S(1)}, bf16[128,1536]{1,0:T(8,128)(2,1)S(1)}, u32[]{:S(2)}, u32[]{:S(2)}) collective-permute-start(bf16[128,1536]{1,0:T(8,128)(2,1)S(1)} %pad_maximum_fusion.4), channel_id=1, source_target_pairs={{232,0},{233,1},{234,2},{235,3},{236,4},{237,5},{238,6},{239,7},{2... | collective-permute-start | bytes 1179656 | tf_op jit(solution)/shard_map/ppermute | solution.py:30
  21.7 27.8 %collective-permute-start.9 = (bf16[128,1536]{1,0:T(8,128)(2,1)}, bf16[128,1536]{1,0:T(8,128)(2,1)}, u32[]{:S(2)}, u32[]{:S(2)}) collective-permute-start(bf16[128,1536]{1,0:T(8,128)(2,1)} %pad_maximum_fusion.5), channel_id=1, source_target_pairs={{64,0},{65,1},{66,2},{67,3},{68,4},{69,5},{70,6},{71,7},{72,8},{73... | collective-permute-start | bytes 1179656 | tf_op jit(solution)/shard_map/ppermute | solution.py:30
  35.9 16.4 %collective-permute-start.10 = (bf16[128,1536]{1,0:T(8,128)(2,1)}, bf16[128,1536]{1,0:T(8,128)(2,1)}, u32[]{:S(2)}, u32[]{:S(2)}) collective-permute-start(bf16[128,1536]{1,0:T(8,128)(2,1)} %pad_maximum_fusion.6), channel_id=1, source_target_pairs={{128,0},{129,1},{130,2},{131,3},{132,4},{133,5},{134,6},{135,7},{1... | collective-permute-start | bytes 1179656 | tf_op jit(solution)/shard_map/ppermute | solution.py:30
  47.2 30.6 %collective-permute-start.12 = (s16[3,48,2176]{2,1,0:T(8,128)(2,1)}, s16[3,48,2176]{2,1,0:T(8,128)(2,1)S(1)}, u32[]{:S(2)}, u32[]{:S(2)}) collective-permute-start(s16[3,48,2176]{2,1,0:T(8,128)(2,1)} %get-tuple-element.21), channel_id=1, source_target_pairs={{32,0},{33,1},{34,2},{35,3},{36,4},{37,5},{38,6},{39,7},{40,8},{41... | collective-permute-start | bytes 1880072 | tf_op jit(solution)/shard_map/ppermute | solution.py:30
  48.3 11.8 %collective-permute-start.11 = (bf16[128,1536]{1,0:T(8,128)(2,1)S(1)}, bf16[128,1536]{1,0:T(8,128)(2,1)S(1)}, u32[]{:S(2)}, u32[]{:S(2)}) collective-permute-start(bf16[128,1536]{1,0:T(8,128)(2,1)S(1)} %pad_maximum_fusion.7), channel_id=1, source_target_pairs={{192,0},{193,1},{194,2},{195,3},{196,4},{197,5},{198,6},{199,7},{2... | collective-permute-start | bytes 1179656 | tf_op jit(solution)/shard_map/ppermute | solution.py:30
  48.4 19.3 %collective-permute-start.5 = (s16[80,2176]{1,0:T(8,128)(2,1)}, s16[80,2176]{1,0:T(8,128)(2,1)S(1)}, u32[]{:S(2)}, u32[]{:S(2)}) collective-permute-start(s16[80,2176]{1,0:T(8,128)(2,1)} %get-tuple-element.17), channel_id=1, source_target_pairs={{192,0},{193,1},{194,2},{195,3},{196,4},{197,5},{198,6},{199,7},{2... | collective-permute-start | bytes 1044488 | tf_op jit(solution)/shard_map/ppermute | solution.py:30
  49.5 22.2 %collective-permute-start.6 = (s16[80,2176]{1,0:T(8,128)(2,1)}, s16[80,2176]{1,0:T(8,128)(2,1)S(1)}, u32[]{:S(2)}, u32[]{:S(2)}) collective-permute-start(s16[80,2176]{1,0:T(8,128)(2,1)} %get-tuple-element.18), channel_id=1, source_target_pairs={{128,0},{129,1},{130,2},{131,3},{132,4},{133,5},{134,6},{135,7},{1... | collective-permute-start | bytes 1044488 | tf_op jit(solution)/shard_map/ppermute | solution.py:30
  52.2 19.4 %collective-permute-start.7 = (s16[80,2176]{1,0:T(8,128)(2,1)}, s16[80,2176]{1,0:T(8,128)(2,1)S(1)}, u32[]{:S(2)}, u32[]{:S(2)}) collective-permute-start(s16[80,2176]{1,0:T(8,128)(2,1)} %get-tuple-element.19), channel_id=1, source_target_pairs={{64,0},{65,1},{66,2},{67,3},{68,4},{69,5},{70,6},{71,7},{72,8},{73... | collective-permute-start | bytes 1044488 | tf_op jit(solution)/shard_map/ppermute | solution.py:30
  75.8 13.6 %collective-permute-start.8 = (s16[128,2176]{1,0:T(8,128)(2,1)}, s16[128,2176]{1,0:T(8,128)(2,1)S(1)}, u32[]{:S(2)}, u32[]{:S(2)}) collective-permute-start(s16[128,2176]{1,0:T(8,128)(2,1)} %get-tuple-element.20), channel_id=1, source_target_pairs={{32,0},{33,1},{34,2},{35,3},{36,4},{37,5},{38,6},{39,7},{40,8},{41... | collective-permute-start | bytes 1671176 | tf_op jit(solution)/shard_map/ppermute | solution.py:30
  83.1 12.2 %collective-permute-start.13 = (s16[128,2176]{1,0:T(8,128)(2,1)}, s16[128,2176]{1,0:T(8,128)(2,1)S(1)}, u32[]{:S(2)}, u32[]{:S(2)}) collective-permute-start(s16[128,2176]{1,0:T(8,128)(2,1)} %get-tuple-element.22), channel_id=1, source_target_pairs={{192,0},{193,1},{194,2},{195,3},{196,4},{197,5},{198,6},{199,7},{2... | collective-permute-start | bytes 1671176 | tf_op jit(solution)/shard_map/ppermute | solution.py:30
  83.1 22.5 %collective-permute-start.14 = (s16[128,2176]{1,0:T(8,128)(2,1)}, s16[128,2176]{1,0:T(8,128)(2,1)S(1)}, u32[]{:S(2)}, u32[]{:S(2)}) collective-permute-start(s16[128,2176]{1,0:T(8,128)(2,1)} %get-tuple-element.23), channel_id=1, source_target_pairs={{128,0},{129,1},{130,2},{131,3},{132,4},{133,5},{134,6},{135,7},{1... | collective-permute-start | bytes 1671176 | tf_op jit(solution)/shard_map/ppermute | solution.py:30
  84.3 26.4 %collective-permute-start.15 = (s16[128,2176]{1,0:T(8,128)(2,1)}, s16[128,2176]{1,0:T(8,128)(2,1)S(1)}, u32[]{:S(2)}, u32[]{:S(2)}) collective-permute-start(s16[128,2176]{1,0:T(8,128)(2,1)} %get-tuple-element.24), channel_id=1, source_target_pairs={{64,0},{65,1},{66,2},{67,3},{68,4},{69,5},{70,6},{71,7},{72,8},{73... | collective-permute-start | bytes 1671176 | tf_op jit(solution)/shard_map/ppermute | solution.py:30
  115.1 40.1 %collective-permute-start.20 = (bf16[128,2048]{1,0:T(8,128)(2,1)}, bf16[128,2048]{1,0:T(8,128)(2,1)S(1)}, u32[]{:S(2)}, u32[]{:S(2)}) collective-permute-start(bf16[128,2048]{1,0:T(8,128)(2,1)} %get-tuple-element.30.refs_0_), channel_id=1, source_target_pairs={{32,0},{33,1},{34,2},{35,3},{36,4},{37,5},{38,6},{39,7},{40,8},{41... | collective-permute-start | bytes 1572872 | tf_op jit(solution)/shard_map/ppermute | solution.py:30
  115.1 40.1 %collective-permute-start.19 = (bf16[128,2048]{1,0:T(8,128)(2,1)}, bf16[128,2048]{1,0:T(8,128)(2,1)S(1)}, u32[]{:S(2)}, u32[]{:S(2)}) collective-permute-start(bf16[128,2048]{1,0:T(8,128)(2,1)} %get-tuple-element.30.refs_0_), channel_id=1, source_target_pairs={{192,0},{193,1},{194,2},{195,3},{196,4},{197,5},{198,6},{199,7},{2... | collective-permute-start | bytes 1572872 | tf_op jit(solution)/shard_map/ppermute | solution.py:30
  116.9 38.3 %collective-permute-start.18 = (bf16[128,2048]{1,0:T(8,128)(2,1)}, bf16[128,2048]{1,0:T(8,128)(2,1)S(1)}, u32[]{:S(2)}, u32[]{:S(2)}) collective-permute-start(bf16[128,2048]{1,0:T(8,128)(2,1)} %get-tuple-element.30.refs_0_), channel_id=1, source_target_pairs={{128,0},{129,1},{130,2},{131,3},{132,4},{133,5},{134,6},{135,7},{1... | collective-permute-start | bytes 1572872 | tf_op jit(solution)/shard_map/ppermute | solution.py:30
  119.6 35.7 %collective-permute-start.17 = (bf16[128,2048]{1,0:T(8,128)(2,1)}, bf16[128,2048]{1,0:T(8,128)(2,1)S(1)}, u32[]{:S(2)}, u32[]{:S(2)}) collective-permute-start(bf16[128,2048]{1,0:T(8,128)(2,1)} %get-tuple-element.30.refs_0_), channel_id=1, source_target_pairs={{64,0},{65,1},{66,2},{67,3},{68,4},{69,5},{70,6},{71,7},{72,8},{73... | collective-permute-start | bytes 1572872 | tf_op jit(solution)/shard_map/ppermute | solution.py:30
  141.6 2.7 %collective-permute-start.21 = (f32[8,128]{1,0:T(8,128)}, f32[8,128]{1,0:T(8,128)S(1)}, u32[]{:S(2)}, u32[]{:S(2)}) collective-permute-start(f32[8,128]{1,0:T(8,128)} %get-tuple-element.31), channel_id=1, source_target_pairs={{32,0},{33,1},{34,2},{35,3},{36,4},{37,5},{38,6},{39,7},{40,8},{41... | collective-permute-start | bytes 12296 | tf_op jit(solution)/shard_map/ppermute | solution.py:30
  145.0 3.7 %collective-permute-start.24 = (f32[2,8,128]{2,1,0:T(8,128)S(1)}, f32[2,8,128]{2,1,0:T(8,128)S(1)}, u32[]{:S(2)}, u32[]{:S(2)}) collective-permute-start(f32[2,8,128]{2,1,0:T(8,128)S(1)} %pad_maximum_fusion.8.refs_5_.refs_6_), channel_id=1, source_target_pairs={{192,0},{193,1},{194,2},{195,3},{196,4},{197,5},{198,6},{199,7},{2... | collective-permute-start | bytes 24584 | tf_op jit(solution)/shard_map/ppermute | solution.py:30
  148.7 4.0 %collective-permute-start.23 = (f32[2,8,128]{2,1,0:T(8,128)S(1)}, f32[2,8,128]{2,1,0:T(8,128)S(1)}, u32[]{:S(2)}, u32[]{:S(2)}) collective-permute-start(f32[2,8,128]{2,1,0:T(8,128)S(1)} %pad_maximum_fusion.8.refs_5_.refs_6_), channel_id=1, source_target_pairs={{128,0},{129,1},{130,2},{131,3},{132,4},{133,5},{134,6},{135,7},{1... | collective-permute-start | bytes 24584 | tf_op jit(solution)/shard_map/ppermute | solution.py:30
  161.6 42.6 %collective-permute-start.25 = (bf16[640,2048]{1,0:T(8,128)(2,1)}, bf16[640,2048]{1,0:T(8,128)(2,1)S(1)}, u32[]{:S(2)}, u32[]{:S(2)}) collective-permute-start(bf16[640,2048]{1,0:T(8,128)(2,1)} %shard_map.53.a_ref), channel_id=1, source_target_pairs={{16,0},{17,1},{18,2},{19,3},{20,4},{21,5},{22,6},{23,7},{24,8},{25... | collective-permute-start | bytes 7864328 | tf_op jit(solution)/shard_map/ppermute | solution.py:30
  169.9 8.2 %collective-permute-start.31 = (bf16[48,2048]{1,0:T(8,128)(2,1)S(1)}, bf16[48,2048]{1,0:T(8,128)(2,1)S(1)}, u32[]{:S(2)}, u32[]{:S(2)}) collective-permute-start(bf16[48,2048]{1,0:T(8,128)(2,1)S(1)} %slice.25), channel_id=1, source_target_pairs={{192,0},{193,1},{194,2},{195,3},{196,4},{197,5},{198,6},{199,7},{2... | collective-permute-start | bytes 589832 | tf_op jit(solution)/shard_map/ppermute | solution.py:30
  170.5 10.8 %collective-permute-start.30 = (bf16[48,2048]{1,0:T(8,128)(2,1)S(1)}, bf16[48,2048]{1,0:T(8,128)(2,1)S(1)}, u32[]{:S(2)}, u32[]{:S(2)}) collective-permute-start(bf16[48,2048]{1,0:T(8,128)(2,1)S(1)} %slice.25), channel_id=1, source_target_pairs={{128,0},{129,1},{130,2},{131,3},{132,4},{133,5},{134,6},{135,7},{1... | collective-permute-start | bytes 589832 | tf_op jit(solution)/shard_map/ppermute | solution.py:30
  173.1 16.8 %collective-permute-start.28 = (bf16[80,2048]{1,0:T(8,128)(2,1)S(1)}, bf16[80,2048]{1,0:T(8,128)(2,1)}, u32[]{:S(2)}, u32[]{:S(2)}) collective-permute-start(bf16[80,2048]{1,0:T(8,128)(2,1)S(1)} %slice.24), channel_id=1, source_target_pairs={{32,0},{33,1},{34,2},{35,3},{36,4},{37,5},{38,6},{39,7},{40,8},{41... | collective-permute-start | bytes 983048 | tf_op jit(solution)/shard_map/ppermute | solution.py:30
  174.2 15.7 %collective-permute-start.27 = (bf16[80,2048]{1,0:T(8,128)(2,1)S(1)}, bf16[80,2048]{1,0:T(8,128)(2,1)}, u32[]{:S(2)}, u32[]{:S(2)}) collective-permute-start(bf16[80,2048]{1,0:T(8,128)(2,1)S(1)} %slice.23), channel_id=1, source_target_pairs={{32,0},{33,1},{34,2},{35,3},{36,4},{37,5},{38,6},{39,7},{40,8},{41... | collective-permute-start | bytes 983048 | tf_op jit(solution)/shard_map/ppermute | solution.py:30
  178.1 17.9 %collective-permute-start.26 = (bf16[80,2048]{1,0:T(8,128)(2,1)}, bf16[80,2048]{1,0:T(8,128)(2,1)}, u32[]{:S(2)}, u32[]{:S(2)}) collective-permute-start(bf16[80,2048]{1,0:T(8,128)(2,1)} %slice.22), channel_id=1, source_target_pairs={{32,0},{33,1},{34,2},{35,3},{36,4},{37,5},{38,6},{39,7},{40,8},{41... | collective-permute-start | bytes 983048 | tf_op jit(solution)/shard_map/ppermute | solution.py:30
  182.0 4.9 %collective-permute-start.29 = (bf16[48,2048]{1,0:T(8,128)(2,1)S(1)}, bf16[48,2048]{1,0:T(8,128)(2,1)}, u32[]{:S(2)}, u32[]{:S(2)}) collective-permute-start(bf16[48,2048]{1,0:T(8,128)(2,1)S(1)} %slice.25), channel_id=1, source_target_pairs={{64,0},{65,1},{66,2},{67,3},{68,4},{69,5},{70,6},{71,7},{72,8},{73... | collective-permute-start | bytes 589832 | tf_op jit(solution)/shard_map/ppermute | solution.py:30
  186.9 14.0 %collective-permute-start.16 = (bf16[768,1024]{1,0:T(8,128)(2,1)}, bf16[768,1024]{1,0:T(8,128)(2,1)}, u32[]{:S(2)}, u32[]{:S(2)}) collective-permute-start(bf16[768,1024]{1,0:T(8,128)(2,1)} %get-tuple-element.29), channel_id=1, source_target_pairs={{16,0},{17,1},{18,2},{19,3},{20,4},{21,5},{22,6},{23,7},{24,8},{25... | collective-permute-start | bytes 4718600 | tf_op jit(solution)/shard_map/ppermute | solution.py:30
  199.5 4.7 %collective-permute-start.32 = (bf16[384,2048]{1,0:T(8,128)(2,1)}, bf16[384,2048]{1,0:T(8,128)(2,1)S(1)}, u32[]{:S(2)}, u32[]{:S(2)}) collective-permute-start(bf16[384,2048]{1,0:T(8,128)(2,1)} %shard_map.54.c_ref), channel_id=1, source_target_pairs={{16,0},{17,1},{18,2},{19,3},{20,4},{21,5},{22,6},{23,7},{24,8},{25... | collective-permute-start | bytes 4718600 | tf_op jit(solution)/shard_map/ppermute | solution.py:30
  (28 other events, 120.1 us)
